TPU v7x, 32 devices: a whole 2x2x4 slice. The times are simulated.
32 devices in a mesh: seq: 4 (over y, x), shard: 8 (over z, core).
Axes of the slice: x: 2, y: 2, z: 4, core: 2. Of those that a mesh axis runs over, the one named last changes fastest.
Arguments:
- layer_input: bfloat16 [8, 2048, 1024], P('shard', 'seq'), may hold values from -6 to 6
- cotangent: float32 [8, 2048, 1024], P('shard', 'seq'), may hold values from -6 to 6
- weight_qkv: float32 [1024, 3072], P(('seq', 'shard')), may hold values from -0.3125 to 0.3125
- weight_merge: float32 [1024, 1024], P(('seq', 'shard')), may hold values from -0.3125 to 0.3125
- weight_expand: float32 [1024, 4096], P(('seq', 'shard')), may hold values from -0.1875 to 0.1875
- weight_shrink: float32 [4096, 1024], P(('seq', 'shard')), may hold values from -0.09375 to 0.09375
- norm_gains: float32 [2, 1024], P(None, ('seq', 'shard')), may hold values from 0.5 to 1.5
- all_biases: float32 [6, 1024], P(None, ('seq', 'shard')), may hold values from -2 to 2
- bias_hidden: float32 [4096], P(('seq', 'shard')), may hold values from -2 to 2
- moment_qkv: float32 [1024, 3072], P(('seq', 'shard')), may hold values from -96 to 96
- moment_merge: float32 [1024, 1024], P(('seq', 'shard')), may hold values from -96 to 96
- moment_expand: float32 [1024, 4096], P(('seq', 'shard')), may hold values from -96 to 96
- moment_shrink: float32 [4096, 1024], P(('seq', 'shard')), may hold values from -96 to 96
- moment_gains: float32 [2, 1024], P(None, ('seq', 'shard')), may hold values from -96 to 96
- moment_biases: float32 [6, 1024], P(None, ('seq', 'shard')), may hold values from -96 to 96
- moment_hidden: float32 [4096], P(('seq', 'shard')), may hold values from -96 to 96
- squares_qkv: float32 [1024, 3072], P(('seq', 'shard')), may hold values from 4.096 to 40.96
- squares_merge: float32 [1024, 1024], P(('seq', 'shard')), may hold values from 4.096 to 40.96
- squares_expand: float32 [1024, 4096], P(('seq', 'shard')), may hold values from 4.096 to 40.96
- squares_shrink: float32 [4096, 1024], P(('seq', 'shard')), may hold values from 4.096 to 40.96
- squares_gains: float32 [2, 1024], P(None, ('seq', 'shard')), may hold values from 4.096 to 40.96
- squares_biases: float32 [6, 1024], P(None, ('seq', 'shard')), may hold values from 4.096 to 40.96
- squares_hidden: float32 [4096], P(('seq', 'shard')), may hold values from 4.096 to 40.96
Outputs:
- layer_output: bfloat16 [8, 2048, 1024], P('shard', 'seq')
- grad_input: float32 [8, 2048, 1024], P('shard', 'seq')
- grad_qkv: float32 [1024, 3072], P(('seq', 'shard'))
- grad_merge: float32 [1024, 1024], P(('seq', 'shard'))
- grad_expand: float32 [1024, 4096], P(('seq', 'shard'))
- grad_shrink: float32 [4096, 1024], P(('seq', 'shard'))
- grad_gains: float32 [2, 1024], P(None, ('seq', 'shard'))
- grad_biases: float32 [6, 1024], P(None, ('seq', 'shard'))
- grad_hidden: float32 [4096], P(('seq', 'shard'))
- master_qkv: float32 [1024, 3072], P(('seq', 'shard'))
- master_merge: float32 [1024, 1024], P(('seq', 'shard'))
- master_expand: float32 [1024, 4096], P(('seq', 'shard'))
- master_shrink: float32 [4096, 1024], P(('seq', 'shard'))
- change_gains: float32 [2, 1024], P(None, ('seq', 'shard'))
- change_biases: float32 [6, 1024], P(None, ('seq', 'shard'))
- change_hidden: float32 [4096], P(('seq', 'shard'))
- momentum_qkv: float32 [1024, 3072], P(('seq', 'shard'))
- momentum_merge: float32 [1024, 1024], P(('seq', 'shard'))
- momentum_expand: float32 [1024, 4096], P(('seq', 'shard'))
- momentum_shrink: float32 [4096, 1024], P(('seq', 'shard'))
- momentum_gains: float32 [2, 1024], P(None, ('seq', 'shard'))
- momentum_biases: float32 [6, 1024], P(None, ('seq', 'shard'))
- momentum_hidden: float32 [4096], P(('seq', 'shard'))
- squared_qkv: float32 [1024, 3072], P(('seq', 'shard'))
- squared_merge: float32 [1024, 1024], P(('seq', 'shard'))
- squared_expand: float32 [1024, 4096], P(('seq', 'shard'))
- squared_shrink: float32 [4096, 1024], P(('seq', 'shard'))
- squared_gains: float32 [2, 1024], P(None, ('seq', 'shard'))
- squared_biases: float32 [6, 1024], P(None, ('seq', 'shard'))
- squared_hidden: float32 [4096], P(('seq', 'shard'))
All inputs are finite; a program needn't handle non-finite values.
Results may differ from a plain program's by a relative error of at most 0.014.
The roundings to bfloat16 on the way count: a program that leaves them out, or rounds other values in their place, can miss the bound.
Values may be sent and summed in bfloat16 or wider, within the bound.
No kernel may reach another device: no remote copies, remote signals or barrier semaphores. Data moves between devices by JAX's collectives and lax.ppermute only.
A program may use at most 192 MiB of HBM per device.

v0:
```python
import jax
import jax.numpy as jnp
from jax import lax
from jax.sharding import PartitionSpec as P

HD = 64
STEP = 10


def norm_forward(value, gain, shift):
    centre = value - jnp.mean(value, axis=-1, keepdims=True)
    inverse = lax.rsqrt(jnp.mean(centre * centre, axis=-1, keepdims=True) + 1e-06)
    normed = centre * inverse
    return (normed * gain + shift, normed, inverse)


def norm_backward(grad, normed, inverse, gain):
    scaled = grad * gain
    inner = jnp.mean(scaled * normed, axis=-1, keepdims=True)
    return inverse * (scaled - jnp.mean(scaled, axis=-1, keepdims=True) - normed * inner)


def gelu_slope(hidden):
    return (
        0.5 * (1.0 + lax.erf(hidden * 0.7071067811865476))
        + hidden * jnp.exp(-0.5 * hidden * hidden) * 0.3989422804014327
    )


def attend_forward(query, keys, values, block):
    length = query.shape[0]

    def one_block(piece):
        scores = jnp.einsum("qhd,khd->hqk", piece, keys, preferred_element_type=jnp.float32) * 0.125
        highest = jnp.max(scores, axis=-1, keepdims=True)
        totals = highest + jnp.log(jnp.sum(jnp.exp(scores - highest), axis=-1, keepdims=True))
        probs = jnp.exp(scores - totals).astype(jnp.bfloat16)
        context = jnp.einsum("hqk,khd->qhd", probs, values, preferred_element_type=jnp.float32)
        return (context.astype(jnp.bfloat16), totals[..., 0])

    pieces = query.reshape(length // block, block, query.shape[1], query.shape[2])
    context, totals = lax.map(one_block, pieces)
    return (context.reshape(query.shape), totals)


def attend_backward(query, keys, values, totals, grad_context, block):
    length = query.shape[0]
    pieces = query.reshape(length // block, block, query.shape[1], query.shape[2])
    grad_pieces = grad_context.reshape(length // block, block, query.shape[1], query.shape[2])

    def one_block(carry, inputs):
        key_grad, value_grad = carry
        piece, grad_piece, total = inputs
        scores = jnp.einsum("qhd,khd->hqk", piece, keys, preferred_element_type=jnp.float32) * 0.125
        probs = jnp.exp(scores - total[..., None])
        rounded = probs.astype(jnp.bfloat16)
        value_grad = value_grad + jnp.einsum(
            "hqk,qhd->khd", rounded, grad_piece, preferred_element_type=jnp.float32
        )
        prob_grad = jnp.einsum(
            "qhd,khd->hqk", grad_piece, values, preferred_element_type=jnp.float32
        )
        inner = jnp.sum(probs * prob_grad, axis=-1, keepdims=True)
        score_grad = (probs * (prob_grad - inner)).astype(jnp.bfloat16)
        query_grad = (
            jnp.einsum("hqk,khd->qhd", score_grad, keys, preferred_element_type=jnp.float32) * 0.125
        )
        key_grad = (
            key_grad
            + jnp.einsum("hqk,qhd->khd", score_grad, piece, preferred_element_type=jnp.float32)
            * 0.125
        )
        return ((key_grad, value_grad), query_grad)

    zeros = jnp.zeros(keys.shape, jnp.float32)
    (key_grad, value_grad), query_grad = lax.scan(
        one_block, (zeros, zeros), (pieces, grad_pieces, totals)
    )
    return (query_grad.reshape(query.shape), key_grad, value_grad)


def adam_update(param, grad, moment, squares, decay):
    momentum = 0.9 * moment + 0.1 * grad
    squared = 0.999 * squares + 0.001 * grad * grad
    update = momentum / (1.0 - 0.9**STEP) / (jnp.sqrt(squared / (1.0 - 0.999**STEP)) + 1e-08)
    if decay:
        update = update + 0.01 * param
    change = -0.02 * update
    return (param - 0.02 * update, change, momentum, squared)


def body(
    layer_input,
    cotangent,
    weight_qkv,
    weight_merge,
    weight_expand,
    weight_shrink,
    norm_gains,
    all_biases,
    bias_hidden,
    moment_qkv,
    moment_merge,
    moment_expand,
    moment_shrink,
    moment_gains,
    moment_biases,
    moment_hidden,
    squares_qkv,
    squares_merge,
    squares_expand,
    squares_shrink,
    squares_gains,
    squares_biases,
    squares_hidden,
):
    params = (
        weight_qkv,
        weight_merge,
        weight_expand,
        weight_shrink,
        norm_gains,
        all_biases,
        bias_hidden,
    )
    moments = (
        moment_qkv,
        moment_merge,
        moment_expand,
        moment_shrink,
        moment_gains,
        moment_biases,
        moment_hidden,
    )
    squares = (
        squares_qkv,
        squares_merge,
        squares_expand,
        squares_shrink,
        squares_gains,
        squares_biases,
        squares_hidden,
    )
    lowered = tuple((param.astype(jnp.bfloat16) for param in params))
    gathered = (
        lax.all_gather(lowered[0], ("seq", "shard"), axis=0, tiled=True),
        lax.all_gather(lowered[1], ("seq", "shard"), axis=0, tiled=True),
        lax.all_gather(lowered[2], ("seq", "shard"), axis=0, tiled=True),
        lax.all_gather(lowered[3], ("seq", "shard"), axis=0, tiled=True),
        lax.all_gather(lowered[4], ("seq", "shard"), axis=1, tiled=True),
        lax.all_gather(lowered[5], ("seq", "shard"), axis=1, tiled=True),
        lax.all_gather(lowered[6], ("seq", "shard"), axis=0, tiled=True),
    )
    full_qkv, full_merge, full_expand, full_shrink, full_gains, full_biases, full_hidden = gathered
    gains = full_gains.astype(jnp.float32)
    biases = full_biases.astype(jnp.float32)
    hidden_bias = full_hidden.astype(jnp.float32)
    tokens = layer_input[0]
    width = tokens.shape[1]
    zero_row = jnp.zeros((width,), jnp.float32)
    qkv = jnp.dot(tokens, full_qkv, preferred_element_type=jnp.float32) + jnp.concatenate(
        [biases[1], zero_row, biases[2]]
    )
    qkv = qkv.astype(jnp.bfloat16)
    query = qkv[:, :width]
    keys = qkv[:, width : 2 * width]
    values = qkv[:, 2 * width :]
    query, keys, values = (
        lax.all_to_all(query, "seq", split_axis=1, concat_axis=0, tiled=True),
        lax.all_to_all(keys, "seq", split_axis=1, concat_axis=0, tiled=True),
        lax.all_to_all(values, "seq", split_axis=1, concat_axis=0, tiled=True),
    )
    length = query.shape[0]
    local_width = query.shape[1]
    shape = (length, local_width // HD, HD)
    block = min(512, length)
    head_query = query.reshape(shape)
    head_keys = keys.reshape(shape)
    head_values = values.reshape(shape)
    context, totals = attend_forward(head_query, head_keys, head_values, block)
    context = lax.all_to_all(
        context.reshape(length, local_width), "seq", split_axis=0, concat_axis=1, tiled=True
    )
    attended = jnp.dot(context, full_merge, preferred_element_type=jnp.float32) + biases[3]
    first, normed_one, inverse_one = norm_forward(
        tokens.astype(jnp.float32) + attended, gains[0], biases[0]
    )
    first_low = first.astype(jnp.bfloat16)
    hidden = jnp.dot(first_low, full_expand, preferred_element_type=jnp.float32) + hidden_bias
    active = jax.nn.gelu(hidden, approximate=False).astype(jnp.bfloat16)
    branch = jnp.dot(active, full_shrink, preferred_element_type=jnp.float32) + biases[5]
    result, normed_two, inverse_two = norm_forward(first + branch, gains[1], biases[4])
    grad_out = cotangent[0]
    grad_gain_two = jnp.sum(grad_out * normed_two, axis=0)
    grad_shift_two = jnp.sum(grad_out, axis=0)
    grad_mid = norm_backward(grad_out, normed_two, inverse_two, gains[1])
    grad_branch = grad_mid.astype(jnp.bfloat16)
    grad_shrink_bias = jnp.sum(grad_branch, axis=0, dtype=jnp.float32)
    grad_shrink = jnp.einsum("tf,td->fd", active, grad_branch, preferred_element_type=jnp.float32)
    grad_active = jnp.einsum(
        "td,fd->tf", grad_branch, full_shrink, preferred_element_type=jnp.float32
    )
    grad_hidden = (grad_active * gelu_slope(hidden)).astype(jnp.bfloat16)
    grad_hidden_bias = jnp.sum(grad_hidden, axis=0, dtype=jnp.float32)
    grad_expand = jnp.einsum(
        "td,tf->df", first_low, grad_hidden, preferred_element_type=jnp.float32
    )
    grad_first = grad_mid + jnp.einsum(
        "tf,df->td", grad_hidden, full_expand, preferred_element_type=jnp.float32
    )
    grad_gain_one = jnp.sum(grad_first * normed_one, axis=0)
    grad_shift_one = jnp.sum(grad_first, axis=0)
    grad_residual = norm_backward(grad_first, normed_one, inverse_one, gains[0])
    grad_attended = grad_residual.astype(jnp.bfloat16)
    grad_merge_bias = jnp.sum(grad_attended, axis=0, dtype=jnp.float32)
    grad_merge = jnp.einsum("td,te->de", context, grad_attended, preferred_element_type=jnp.float32)
    grad_heads = jnp.einsum(
        "te,de->td", grad_attended, full_merge, preferred_element_type=jnp.float32
    ).astype(jnp.bfloat16)
    grad_heads = lax.all_to_all(grad_heads, "seq", split_axis=1, concat_axis=0, tiled=True)
    query_grad, key_grad, value_grad = attend_backward(
        head_query, head_keys, head_values, totals, grad_heads.reshape(shape), block
    )
    query_grad = query_grad.reshape(length, local_width).astype(jnp.bfloat16)
    key_grad = key_grad.reshape(length, local_width).astype(jnp.bfloat16)
    value_grad = value_grad.reshape(length, local_width).astype(jnp.bfloat16)
    query_grad, key_grad, value_grad = (
        lax.all_to_all(query_grad, "seq", split_axis=0, concat_axis=1, tiled=True),
        lax.all_to_all(key_grad, "seq", split_axis=0, concat_axis=1, tiled=True),
        lax.all_to_all(value_grad, "seq", split_axis=0, concat_axis=1, tiled=True),
    )
    grad_rows = jnp.concatenate([query_grad, key_grad, value_grad], axis=1)
    grad_weight_qkv = jnp.einsum("td,te->de", tokens, grad_rows, preferred_element_type=jnp.float32)
    grad_input = grad_residual + jnp.einsum(
        "te,de->td", grad_rows, full_qkv, preferred_element_type=jnp.float32
    )
    grad_query_bias = jnp.sum(query_grad, axis=0, dtype=jnp.float32)
    grad_value_bias = jnp.sum(value_grad, axis=0, dtype=jnp.float32)
    grad_gain_rows = jnp.stack([grad_gain_one, grad_gain_two])
    grad_bias_rows = jnp.stack(
        [
            grad_shift_one,
            grad_query_bias,
            grad_value_bias,
            grad_merge_bias,
            grad_shift_two,
            grad_shrink_bias,
        ]
    )
    summed = (
        lax.psum_scatter(grad_weight_qkv, ("seq", "shard"), scatter_dimension=0, tiled=True),
        lax.psum_scatter(grad_merge, ("seq", "shard"), scatter_dimension=0, tiled=True),
        lax.psum_scatter(grad_expand, ("seq", "shard"), scatter_dimension=0, tiled=True),
        lax.psum_scatter(grad_shrink, ("seq", "shard"), scatter_dimension=0, tiled=True),
        lax.psum_scatter(grad_gain_rows, ("seq", "shard"), scatter_dimension=1, tiled=True),
        lax.psum_scatter(grad_bias_rows, ("seq", "shard"), scatter_dimension=1, tiled=True),
        lax.psum_scatter(grad_hidden_bias, ("seq", "shard"), scatter_dimension=0, tiled=True),
    )
    summed = tuple(summed)
    finals = []
    momenta = []
    squared_all = []
    for index in range(7):
        master, change, momentum, squared = adam_update(
            params[index], summed[index], moments[index], squares[index], index < 4
        )
        finals.append(master if index < 4 else change)
        momenta.append(momentum)
        squared_all.append(squared)
    layer_output = result.astype(jnp.bfloat16)[None]
    return (
        (layer_output, grad_input[None])
        + summed
        + tuple(finals)
        + tuple(momenta)
        + tuple(squared_all)
    )


def solution(mesh):
    in_specs = (
        P("shard", "seq", None),
        P("shard", "seq", None),
        P(("seq", "shard"), None),
        P(("seq", "shard"), None),
        P(("seq", "shard"), None),
        P(("seq", "shard"), None),
        P(None, ("seq", "shard")),
        P(None, ("seq", "shard")),
        P(("seq", "shard")),
        P(("seq", "shard"), None),
        P(("seq", "shard"), None),
        P(("seq", "shard"), None),
        P(("seq", "shard"), None),
        P(None, ("seq", "shard")),
        P(None, ("seq", "shard")),
        P(("seq", "shard")),
        P(("seq", "shard"), None),
        P(("seq", "shard"), None),
        P(("seq", "shard"), None),
        P(("seq", "shard"), None),
        P(None, ("seq", "shard")),
        P(None, ("seq", "shard")),
        P(("seq", "shard")),
    )
    out_specs = (
        P("shard", "seq", None),
        P("shard", "seq", None),
        P(("seq", "shard"), None),
        P(("seq", "shard"), None),
        P(("seq", "shard"), None),
        P(("seq", "shard"), None),
        P(None, ("seq", "shard")),
        P(None, ("seq", "shard")),
        P(("seq", "shard")),
        P(("seq", "shard"), None),
        P(("seq", "shard"), None),
        P(("seq", "shard"), None),
        P(("seq", "shard"), None),
        P(None, ("seq", "shard")),
        P(None, ("seq", "shard")),
        P(("seq", "shard")),
        P(("seq", "shard"), None),
        P(("seq", "shard"), None),
        P(("seq", "shard"), None),
        P(("seq", "shard"), None),
        P(None, ("seq", "shard")),
        P(None, ("seq", "shard")),
        P(("seq", "shard")),
        P(("seq", "shard"), None),
        P(("seq", "shard"), None),
        P(("seq", "shard"), None),
        P(("seq", "shard"), None),
        P(None, ("seq", "shard")),
        P(None, ("seq", "shard")),
        P(("seq", "shard")),
    )
    return jax.shard_map(body, mesh=mesh, in_specs=in_specs, out_specs=out_specs, check_vma=False)
```

profile of v0, /device:TPU:0, one launch (start us, length us, event | category | flops | bytes accessed | tf_op | source)
XLA Modules:
  0.0 1530.7 jit_solution(16189287071771679174)
XLA Ops:
  13.1 43.8 %all-gather = bf16[32,32,6]{1,2,0:T(8,128)(2,1)S(1)} all-gather(bf16[1,32,6]{1,2,0:T(8,128)(2,1)S(1)} %convert_bitcast_fusion), channel_id=1, replica_groups=mesh['seq'=4,'shard'=8] {'seq','shard'}, dimensions={0}, use_global_device_ids=true | all-gather | bytes 12672 | tf_op jit(solution)/shard_map/all_gather | solution.py:151
  57.7 26.3 %all-gather.8.cloned.1.call-done = bf16[1024,3072]{1,0:T(8,128)(2,1)} async-done(((bf16[32,3072]{1,0:T(8,128)(2,1)}), bf16[1024,3072]{1,0:T(8,128)(2,1)}) %all-gather.8.cloned.1.call-update) | async-done | bytes 6291472 | tf_op jit(solution)/shard_map/all_gather | solution.py:146
  96.5 13.3 all-to-all-done.1
  114.3 14.3 all-to-all-done.2
  138.5 10.9 all-to-all-done
  150.9 66.6 %while.27 = (s32[]{:T(128)}, bf16[4,512,4,64]{1,3,2,0:T(8,128)(2,1)}, f32[4,4,512]{2,1,0:T(4,128)S(1)}, bf16[4,512,4,64]{1,3,2,0:T(8,128)(2,1)S(1)}, bf16[2048,4...) while((s32[]{:T(128)}, bf16[4,512,4,64]{1,3,2,0:T(8,128)(2,1)}, ...), condition=%wide.region_3.4_spmd, body=%wide.region_0.3_spmd.sunk | while | flops 1107425280 | bytes 120127616 | solution.py:42
  221.8 41.2 %all-gather.2 = bf16[32,1,128]{2,1,0:T(2,128)(2,1)S(1)} all-gather(bf16[1,1,128]{2,1,0:T(2,128)(2,1)S(1)} %convert_bitcast_fusion.1), channel_id=1, replica_groups=mesh['seq'=4,'shard'=8] {'seq','shard'}, dimensions={0}, use_global_device_ids=true | all-gather | bytes 8448 | tf_op jit(solution)/shard_map/all_gather | solution.py:152
  263.0 37.1 %all-gather.1 = bf16[32,32,2]{1,2,0:T(2,128)(2,1)S(1)} all-gather(bf16[1,32,2]{1,2,0:T(2,128)(2,1)S(1)} %convert_bitcast_fusion.2), channel_id=1, replica_groups=mesh['seq'=4,'shard'=8] {'seq','shard'}, dimensions={0}, use_global_device_ids=true | all-gather | bytes 4224 | tf_op jit(solution)/shard_map/all_gather | solution.py:150
  305.5 27.4 %fusion.41 = (bf16[512,4096]{1,0:T(8,128)(2,1)}, f32[512,4096]{1,0:T(8,128)}) fusion(f32[4096]{0:T(1024)S(1)} %bitcast.249, bf16[1024,4096]{1,0:T(8,128)(2,1)} %all-gather.12.cloned.1.call-done, f32[512,1024]{1,0:T(8,128)} %copy-done.5, f32[1024]{0:T(1024)S(1)} %bitcast.255, f32[1024]{0:T(1024)S(1)} %bitcast.240, f32[512]{0:T(512)S(1)} %add_rsqrt_fusion.1, ...), kind=kOutput, calls=%fused_computation.49 | convolution fusion | flops 4436000768 | bytes 23097344 | tf_op jit(solution)/shard_map/dot_general | solution.py:189
  333.0 10.0 fusion.93
  347.3 14.0 convert_reduce_fusion
  378.6 14.5 all-to-all-done.4
  395.4 156.6 %while.28 = (s32[]{:T(128)}, f32[2048,4,64]{0,2,1:T(8,128)}, f32[2048,4,64]{0,2,1:T(8,128)}, bf16[4,512,4,64]{1,3,2,0:T(8,128)(2,1)}, bf16[4,512,4,64]{1,3,2,0:T...) while((s32[]{:T(128)}, f32[2048,4,64]{0,2,1:T(8,128)}, ...), condition=%wide.region_14.15_spmd.clone, body=%wide.region_12.14_spmd.clone.sunk | while | flops 2737436672 | bytes 172548272 | solution.py:76
  412.4 10.5 multiply_convert_fusion.2
  450.6 10.5 multiply_convert_fusion.2
  481.2 9.1 multiply_reduce_fusion.11
  490.3 10.5 multiply_convert_fusion.2
  521.0 9.1 multiply_reduce_fusion.11
  530.0 10.5 multiply_convert_fusion.2
  576.7 10.3 all-to-all-done.7
  595.1 16.2 %all_to_all.131 = bf16[4,512,256]{1,2,0:T(8,128)(2,1)S(1)} all-to-all(bf16[4,512,256]{1,2,0:T(8,128)(2,1)S(1)} %copy.151), channel_id=1, replica_groups=mesh['seq'=4,'shard'=8] {'seq'}, dimensions={0} | all-to-all | bytes 2097152 | tf_op jit(solution)/shard_map/all_to_all | solution.py:229
  612.3 9.5 convolution_bitcast_fusion
  621.8 12.6 copy.159
  636.0 10.5 fusion.78
  648.1 10.7 fusion.75
  659.4 39.2 %all-reduce = f32[4096]{0:T(1024)S(1)} all-reduce(f32[4096]{0:T(1024)S(1)} %copy-done.28), channel_id=8, replica_groups=mesh['seq'=4,'shard'=8] {'seq','shard'}, use_global_device_ids=true, to_apply=%region_30.31.clone | all-reduce | flops 4096 | bytes 32768
  699.2 11.8 reduce-scatter.21.cloned.1.call-done
  720.7 123.6 %reduce-scatter.23.cloned.1.call-done = f32[32,6]{1,0:T(8,128)} async-done(((f32[1024,6]{1,0:T(8,128)}), f32[32,6]{1,0:T(8,128)}) %reduce-scatter.23.cloned.1.call-update) | async-done | bytes 784
  845.8 140.4 %reduce-scatter.13.cloned.1.call-done = f32[32,1024]{1,0:T(8,128)} async-done(((f32[1024,1024]{1,0:T(8,128)}), f32[32,1024]{1,0:T(8,128)}) %reduce-scatter.13.cloned.1.call-update) | async-done | bytes 131088 | tf_op jit(solution)/shard_map/reduce_scatter | solution.py:252
  988.1 157.0 %reduce-scatter.19.cloned.1.call-done = f32[32,3072]{1,0:T(8,128)} async-done(((f32[1024,3072]{1,0:T(8,128)}), f32[32,3072]{1,0:T(8,128)}) %reduce-scatter.19.cloned.1.call-update) | async-done | bytes 393232
  1147.5 186.3 %reduce-scatter.15.cloned.1.call-done = f32[32,4096]{1,0:T(8,128)} async-done(((f32[1024,4096]{1,0:T(8,128)}), f32[32,4096]{1,0:T(8,128)}) %reduce-scatter.15.cloned.1.call-update) | async-done | bytes 524304 | tf_op jit(solution)/shard_map/reduce_scatter | solution.py:253
  1336.7 184.3 %reduce-scatter.17.cloned.1.call-done = f32[128,1024]{1,0:T(8,128)} async-done(((f32[4096,1024]{1,0:T(8,128)}), f32[128,1024]{1,0:T(8,128)}) %reduce-scatter.17.cloned.1.call-update) | async-done | bytes 524304 | tf_op jit(solution)/shard_map/reduce_scatter | solution.py:254
  (255 shorter events, 290.0 us)
Async XLA Ops:
  7.2 76.8 %all-gather.8.cloned.1.call-start = ((), (), s32[]{:S(2)}) async-start(), calls=%async_computation.14 | async-start | bytes 6488064 | tf_op jit(solution)/shard_map/all_gather | solution.py:146
  9.0 291.3 %all-gather.10.cloned.1.call-start = ((), (), s32[]{:S(2)}) async-start(), calls=%async_computation.15 | async-start | bytes 2162688 | tf_op jit(solution)/shard_map/all_gather | solution.py:147
  10.6 294.9 %all-gather.12.cloned.1.call-start = ((), (), s32[]{:S(2)}) async-start(), calls=%async_computation.16 | async-start | bytes 8650752 | tf_op jit(solution)/shard_map/all_gather | solution.py:148
  57.7 275.2 %copy-start.34 = (f32[1,1024]{1,0:T(1,128)}, f32[1,1024]{1,0:T(1,128)S(1)}, u32[]{:S(2)}) copy-start(f32[1,1024]{1,0:T(1,128)S(1)} %get-tuple-element.417) | copy-start | bytes 12292
  91.9 17.8 %all-to-all-start.1 = ((bf16[512,4,256]{2,0,1:T(8,128)(2,1)}), bf16[512,4,256]{2,0,1:T(8,128)(2,1)S(1)}, u32[]{:S(2)}, u32[]{:S(2)}) async-start(bf16[512,4,256]{2,0,1:T(8,128)(2,1)} %bitcast.174), calls=%async_computation.1 | async-start | bytes 2097152 | tf_op jit(solution)/shard_map/all_to_all | solution.py:170
  109.8 18.9 %all-to-all-start.2 = ((bf16[512,4,256]{2,0,1:T(8,128)(2,1)}), bf16[512,4,256]{2,0,1:T(8,128)(2,1)S(1)}, u32[]{:S(2)}, u32[]{:S(2)}) async-start(bf16[512,4,256]{2,0,1:T(8,128)(2,1)} %bitcast.173), calls=%async_computation.2 | async-start | bytes 2097152 | tf_op jit(solution)/shard_map/all_to_all | solution.py:171
  128.6 20.8 %all-to-all-start = ((bf16[512,4,256]{2,0,1:T(8,128)(2,1)}), bf16[512,4,256]{2,0,1:T(8,128)(2,1)}, u32[]{:S(2)}, u32[]{:S(2)}) async-start(bf16[512,4,256]{2,0,1:T(8,128)(2,1)} %bitcast.175), calls=%async_computation | async-start | bytes 2097152 | tf_op jit(solution)/shard_map/all_to_all | solution.py:169
  132.9 200.0 %all-gather.14.cloned.1.call-start = ((), (), s32[]{:S(2)}) async-start(), calls=%async_computation.17 | async-start | bytes 8650752 | tf_op jit(solution)/shard_map/all_gather | solution.py:149
  150.9 70.9 %copy-start.46 = (f32[128]{0:T(128)S(1)}, f32[128]{0:T(128)}, u32[]{:S(2)}) copy-start(f32[128]{0:T(128)} %param.35) | copy-start | bytes 1540
  150.9 112.1 %copy-start.45 = (f32[2,32]{1,0:T(2,128)S(1)}, f32[2,32]{1,0:T(2,128)}, u32[]{:S(2)}) copy-start(f32[2,32]{1,0:T(2,128)} %param.33) | copy-start | bytes 772
  217.5 82.8 %all-to-all-start.3 = ((bf16[4,512,256]{1,2,0:T(8,128)(2,1)}), bf16[4,512,256]{1,2,0:T(8,128)(2,1)}, u32[]{:S(2)}, u32[]{:S(2)}) async-start(bf16[4,512,256]{1,2,0:T(8,128)(2,1)} %bitcast.226), calls=%async_computation.3 | async-start | bytes 2097152 | tf_op jit(solution)/shard_map/all_to_all | solution.py:181
  300.2 68.9 %copy-start.26 = (f32[1,1024]{1,0:T(1,128)}, f32[1,1024]{1,0:T(1,128)S(1)}, u32[]{:S(2)}) copy-start(f32[1,1024]{1,0:T(1,128)S(1)} %get-tuple-element.422) | copy-start | bytes 12292
  303.8 65.3 %copy-start.21 = (f32[512]{0:T(512)}, f32[512]{0:T(512)S(1)}, u32[]{:S(2)}) copy-start(f32[512]{0:T(512)S(1)} %broadcast_multiply_fusion.5) | copy-start | bytes 6148
  305.5 63.6 %copy-start.31 = (f32[512]{0:T(512)}, f32[512]{0:T(512)S(1)}, u32[]{:S(2)}) copy-start(f32[512]{0:T(512)S(1)} %add_rsqrt_fusion.1) | copy-start | bytes 6148
  374.1 19.0 %all-to-all-start.4 = ((bf16[512,4,256]{2,0,1:T(8,128)(2,1)}), bf16[512,4,256]{2,0,1:T(8,128)(2,1)}, u32[]{:S(2)}, u32[]{:S(2)}) async-start(bf16[512,4,256]{2,0,1:T(8,128)(2,1)} %bitcast.218), calls=%async_computation.4 | async-start | bytes 2097152 | tf_op jit(solution)/shard_map/all_to_all | solution.py:220
  552.0 18.4 %all-to-all-start.5 = ((bf16[4,512,256]{1,2,0:T(8,128)(2,1)}), bf16[4,512,256]{1,2,0:T(8,128)(2,1)}, u32[]{:S(2)}, u32[]{:S(2)}) async-start(bf16[4,512,256]{1,2,0:T(8,128)(2,1)} %bitcast.227), calls=%async_computation.5 | async-start | bytes 2097152 | tf_op jit(solution)/shard_map/all_to_all | solution.py:228
  570.4 16.6 %all-to-all-start.7 = ((bf16[4,512,256]{1,2,0:T(8,128)(2,1)}), bf16[4,512,256]{1,2,0:T(8,128)(2,1)S(1)}, u32[]{:S(2)}, u32[]{:S(2)}) async-start(bf16[4,512,256]{1,2,0:T(8,128)(2,1)} %copy.152), calls=%async_computation.7 | async-start | bytes 2097152 | tf_op jit(solution)/shard_map/all_to_all | solution.py:230
  573.9 137.1 %reduce-scatter.21.cloned.1.call-start = ((), (), s32[]{:S(2)}) async-start(), calls=%async_computation.22 | async-start | bytes 540672
  575.2 269.1 %reduce-scatter.23.cloned.1.call-start = ((), (), s32[]{:S(2)}) async-start(), calls=%async_computation.23 | async-start | bytes 540672
  588.4 397.8 %reduce-scatter.13.cloned.1.call-start = ((), (), s32[]{:S(2)}) async-start(), calls=%async_computation.18 | async-start | bytes 4325376 | tf_op jit(solution)/shard_map/reduce_scatter | solution.py:252
  593.9 551.2 %reduce-scatter.19.cloned.1.call-start = ((), (), s32[]{:S(2)}) async-start(), calls=%async_computation.21 | async-start | bytes 12976128
  634.4 699.4 %reduce-scatter.15.cloned.1.call-start = ((), (), s32[]{:S(2)}) async-start(), calls=%async_computation.19 | async-start | bytes 17301504 | tf_op jit(solution)/shard_map/reduce_scatter | solution.py:253
  646.5 874.5 %reduce-scatter.17.cloned.1.call-start = ((), (), s32[]{:S(2)}) async-start(), calls=%async_computation.20 | async-start | bytes 17301504 | tf_op jit(solution)/shard_map/reduce_scatter | solution.py:254
  658.8 53.7 %copy-start.9 = (f32[512,1024]{1,0:T(8,128)S(1)}, f32[512,1024]{1,0:T(8,128)}, u32[]{:S(2)}) copy-start(f32[512,1024]{1,0:T(8,128)} %copy-done.8) | copy-start | bytes 6291460
  658.8 53.7 %copy-start.12 = (bf16[4,512,256]{1,2,0:T(8,128)(2,1)S(1)}, bf16[4,512,256]{1,2,0:T(8,128)(2,1)}, u32[]{:S(2)}) copy-start(bf16[4,512,256]{1,2,0:T(8,128)(2,1)} %copy-done.10) | copy-start | bytes 3145732
  712.4 132.7 %copy-start.38 = (f32[6,32]{1,0:T(8,128)S(1)}, f32[6,32]{1,0:T(8,128)}, u32[]{:S(2)}) copy-start(f32[6,32]{1,0:T(8,128)} %param.41) | copy-start | bytes 2308
  712.4 132.7 %copy-start.39 = (f32[6,32]{1,0:T(8,128)S(1)}, f32[6,32]{1,0:T(8,128)}, u32[]{:S(2)}) copy-start(f32[6,32]{1,0:T(8,128)} %param.48) | copy-start | bytes 2308
  712.5 432.6 %copy-start.17 = (f32[32,3072]{1,0:T(8,128)S(1)}, f32[32,3072]{1,0:T(8,128)}, u32[]{:S(2)}) copy-start(f32[32,3072]{1,0:T(8,128)} %param.29) | copy-start | bytes 1179652
  720.7 800.3 %copy-start.15 = (f32[128,1024]{1,0:T(8,128)S(1)}, f32[128,1024]{1,0:T(8,128)}, u32[]{:S(2)}) copy-start(f32[128,1024]{1,0:T(8,128)} %param.32) | copy-start | bytes 1572868
  720.7 800.3 %copy-start.19 = (f32[128,1024]{1,0:T(8,128)S(1)}, f32[128,1024]{1,0:T(8,128)}, u32[]{:S(2)}) copy-start(f32[128,1024]{1,0:T(8,128)} %param.39) | copy-start | bytes 1572868
  720.7 800.3 %copy-start.20 = (f32[128,1024]{1,0:T(8,128)S(1)}, f32[128,1024]{1,0:T(8,128)}, u32[]{:S(2)}) copy-start(f32[128,1024]{1,0:T(8,128)} %param.46) | copy-start | bytes 1572868
  845.1 678.3 %copy-start.29 = (f32[6,32]{1,0:T(8,128)}, f32[6,32]{1,0:T(8,128)S(1)}, u32[]{:S(2)}) copy-start(f32[6,32]{1,0:T(8,128)S(1)} %copy.164) | copy-start | bytes 2308
  (40 other events, 535.4 us)
Sparse Core Ops, SparseCore 0:
  11.6 72.3 all-gather.7
  87.6 68.2 all-gather.9
  159.5 75.2 all-gather.11
  238.1 76.1 all-gather.13
  577.3 133.7 reduce-scatter.20
  713.8 130.4 reduce-scatter.22
  847.2 138.9 reduce-scatter.12
  992.8 152.2 reduce-scatter.18
  1148.0 185.7 reduce-scatter.14
  1336.6 184.3 reduce-scatter.16
where the time goes:
time: 1540 us; the launch traced here: 1530 us
  waiting for transfers between devices  901 us (59%)
  matrix products  272 us (18%)
  blocking collectives  177 us (11%)
  other arithmetic  83.8 us (5%)
  local copies, waits for them, and re-layouts  52.4 us (3%)
  starting transfers between devices  28.5 us (2%)
    unnamed x13, waiting for transfers between devices  293 us
    reduce_scatter x1, waiting for transfers between devices, body(): lax.psum_scatter(grad_expand, ('seq', 'shard'), scatter_dimension=0, tile...  186 us
    reduce_scatter x1, waiting for transfers between devices, body(): lax.psum_scatter(grad_shrink, ('seq', 'shard'), scatter_dimension=0, tile...  184 us
    reduce_scatter x1, waiting for transfers between devices, body(): lax.psum_scatter(grad_merge, ('seq', 'shard'), scatter_dimension=0, tiled...  140 us
    all_gather x1, blocking collectives, body(): lax.all_gather(lowered[5], ('seq', 'shard'), axis=1, tiled=True)  43.8 us
    convert_element_type x4, other arithmetic, one_block(): score_grad = (probs * (prob_grad - inner)).astype(jnp.bfloat16)  42 us
    all_gather x1, blocking collectives, body(): lax.all_gather(lowered[6], ('seq', 'shard'), axis=0, tiled=True)  41.2 us
    unnamed x1, blocking collectives  39.2 us
  transfers between devices with their start and end apart: 17, of which 13 were waited for; matrix products, arithmetic and copies ran while one was open for 12% of the time, Pallas kernels for 0%

commit v1 on v0

v1 whole, which is shorter than its diff:
```python
import functools

import jax
import jax.numpy as jnp
from jax import lax
from jax.experimental import pallas as pl
from jax.experimental.pallas import tpu as pltpu
from jax.sharding import PartitionSpec as P

HD = 64
STEP = 10
F32 = jnp.float32
BF16 = jnp.bfloat16
NT = (((1,), (1,)), ((), ()))
NN = (((1,), (0,)), ((), ()))
TN = (((0,), (0,)), ((), ()))


def norm_forward(value, gain, shift):
    centre = value - jnp.mean(value, axis=-1, keepdims=True)
    inverse = lax.rsqrt(jnp.mean(centre * centre, axis=-1, keepdims=True) + 1e-06)
    normed = centre * inverse
    return (normed * gain + shift, normed, inverse)


def norm_backward(grad, normed, inverse, gain):
    scaled = grad * gain
    inner = jnp.mean(scaled * normed, axis=-1, keepdims=True)
    return inverse * (scaled - jnp.mean(scaled, axis=-1, keepdims=True) - normed * inner)


def gelu_slope(hidden):
    return (
        0.5 * (1.0 + lax.erf(hidden * 0.7071067811865476))
        + hidden * jnp.exp(-0.5 * hidden * hidden) * 0.3989422804014327
    )


def adam_update(param, grad, moment, squares, decay):
    momentum = 0.9 * moment + 0.1 * grad
    squared = 0.999 * squares + 0.001 * grad * grad
    update = momentum / (1.0 - 0.9**STEP) / (jnp.sqrt(squared / (1.0 - 0.999**STEP)) + 1e-08)
    if decay:
        update = update + 0.01 * param
    change = -0.02 * update
    return (param - 0.02 * update, change, momentum, squared)


def forward_kernel(q_ref, k_ref, v_ref, c_ref, total_ref, flipped_ref):
    @pl.when(pl.program_id(0) == 0)
    def _():
        flipped_ref[...] = jnp.transpose(v_ref[...])

    query = q_ref[...] * jnp.asarray(0.125, BF16)
    lane = lax.broadcasted_iota(jnp.int32, query.shape, 1)
    pieces, rows = [], []
    for head in range(2):
        own = (lane >= HD * head) & (lane < HD * head + HD)
        scores = lax.dot_general(
            k_ref[...], jnp.where(own, query, jnp.zeros_like(query)), NT, preferred_element_type=F32
        )
        highest = jnp.max(scores, axis=0, keepdims=True)
        weights = jnp.exp(scores - highest)
        total = jnp.sum(weights, axis=0, keepdims=True)
        context = lax.dot_general(
            flipped_ref[HD * head : HD * head + HD, :],
            weights.astype(BF16),
            NN,
            preferred_element_type=F32,
        )
        pieces.append(context * (1.0 / total))
        rows.append(highest + jnp.log(total))
    c_ref[...] = jnp.transpose(jnp.concatenate(pieces, axis=0)).astype(BF16)
    total_ref[...] = jnp.concatenate(rows, axis=0)[None]


def attend_forward(query, keys, values, pair, block):
    length = query.shape[0]
    whole = pl.BlockSpec((length, 128), lambda i: (0, pair))
    return pl.pallas_call(
        forward_kernel,
        grid=(length // block,),
        in_specs=[pl.BlockSpec((block, 128), lambda i: (i, pair)), whole, whole],
        out_specs=[
            pl.BlockSpec((block, 128), lambda i: (i, 0)),
            pl.BlockSpec((1, 2, block), lambda i: (0, 0, i)),
        ],
        out_shape=[
            jax.ShapeDtypeStruct((length, 128), BF16),
            jax.ShapeDtypeStruct((1, 2, length), F32),
        ],
        scratch_shapes=[pltpu.VMEM((128, length), BF16)],
        compiler_params=pltpu.CompilerParams(vmem_limit_bytes=44 << 20),
        cost_estimate=pl.CostEstimate(
            flops=32 * length * length * HD,
            transcendentals=2 * length * length,
            bytes_accessed=8 * length * 128,
        ),
        name="attend_forward",
    )(query, keys, values)


def backward_kernel(
    q_ref, k_ref, v_ref, c_ref, g_ref, total_ref, dq_ref, dk_ref, dv_ref, sum_ref, inner_ref
):
    step = pl.program_id(0)

    @pl.when(step == 0)
    def _():
        product = g_ref[...].astype(F32) * c_ref[...].astype(F32)
        upper = product.astype(BF16)
        lower = (product - upper.astype(F32)).astype(BF16)
        row = lax.broadcasted_iota(jnp.int32, (8, 128), 0)
        column = lax.broadcasted_iota(jnp.int32, (8, 128), 1)
        pick = jnp.where(
            (column >= HD * row) & (column < HD * row + HD), 1.0, 0.0
        ).astype(BF16)
        inner_ref[...] = lax.dot_general(
            pick, upper, NT, preferred_element_type=F32
        ) + lax.dot_general(pick, lower, NT, preferred_element_type=F32)

    keys = k_ref[...] * jnp.asarray(0.125, BF16)
    values = v_ref[...]
    flipped = jnp.transpose(keys)
    lane = lax.broadcasted_iota(jnp.int32, keys.shape, 1)
    nothing = jnp.zeros_like(keys)
    value_grads, key_grads, query_grads = [], [], []
    for head in range(2):
        own = (lane >= HD * head) & (lane < HD * head + HD)
        scores = lax.dot_general(
            jnp.where(own, keys, nothing), q_ref[...], NT, preferred_element_type=F32
        )
        probs = jnp.exp(scores - total_ref[0, head : head + 1, :])
        value_grads.append(
            lax.dot_general(probs.astype(BF16), g_ref[...], NN, preferred_element_type=F32)
        )
        prob_grad = lax.dot_general(
            jnp.where(own, values, nothing), g_ref[...], NT, preferred_element_type=F32
        )
        score_grad = (probs * (prob_grad - inner_ref[head : head + 1, :])).astype(BF16)
        key_grads.append(
            lax.dot_general(score_grad, q_ref[...], NN, preferred_element_type=F32)
        )
        query_grads.append(
            lax.dot_general(
                flipped[HD * head : HD * head + HD, :],
                score_grad,
                NN,
                preferred_element_type=F32,
            )
        )
    first = lane < HD
    dk_ref[...] = (jnp.where(first, key_grads[0], key_grads[1]) * 0.125).astype(BF16)
    dv_ref[...] = jnp.where(first, value_grads[0], value_grads[1]).astype(BF16)
    query_grad = jnp.concatenate(query_grads, axis=0)

    @pl.when(step == 0)
    def _():
        sum_ref[...] = query_grad

    @pl.when(step > 0)
    def _():
        sum_ref[...] += query_grad

    @pl.when(step == pl.num_programs(0) - 1)
    def _():
        dq_ref[...] = jnp.transpose(sum_ref[...]).astype(BF16)


def attend_backward(query, keys, values, context, grad, totals, pair, block):
    length = query.shape[0]
    whole = pl.BlockSpec((length, 128), lambda j: (0, pair))
    part = pl.BlockSpec((block, 128), lambda j: (j, pair))
    single = pl.BlockSpec((length, 128), lambda j: (0, 0))
    out_part = pl.BlockSpec((block, 128), lambda j: (j, 0))
    return pl.pallas_call(
        backward_kernel,
        grid=(length // block,),
        in_specs=[
            whole,
            part,
            part,
            single,
            whole,
            pl.BlockSpec((1, 2, length), lambda j: (0, 0, 0)),
        ],
        out_specs=[single, out_part, out_part],
        out_shape=[jax.ShapeDtypeStruct((length, 128), BF16)] * 3,
        scratch_shapes=[pltpu.VMEM((128, length), F32), pltpu.VMEM((8, length), F32)],
        compiler_params=pltpu.CompilerParams(vmem_limit_bytes=48 << 20),
        cost_estimate=pl.CostEstimate(
            flops=80 * length * length * HD,
            transcendentals=2 * length * length,
            bytes_accessed=20 * length * 128,
        ),
        name="attend_backward",
    )(query, keys, values, context, grad, totals)


def swap(value, axis, mask, size):
    return lax.ppermute(value, axis, [(i, i ^ mask) for i in range(size)])


def bits_of(axis, size):
    mine = lax.axis_index(axis)
    count = size.bit_length() - 1
    return [(axis, 1 << b, size, (mine >> b) & 1) for b in reversed(range(count))]


def gather_bits(value, bits, order):
    held = []
    for place in order:
        axis, mask, size, bit = bits[place]
        other = swap(value, axis, mask, size)
        at = sum(1 for h in held if h < place)
        low = jnp.where(bit == 1, other, value)
        high = jnp.where(bit == 1, value, other)
        value = jnp.stack([low, high], axis=at)
        held.append(place)
    return value


def scatter_bits(value, bits, order, last=F32, wire=BF16):
    left = list(range(len(bits)))
    for place in order:
        axis, mask, size, bit = bits[place]
        at = left.index(place)
        away = lax.dynamic_index_in_dim(value, 1 - bit, at, keepdims=False).astype(wire)
        keep = lax.dynamic_index_in_dim(value, bit, at, keepdims=False)
        left.remove(place)
        value = keep.astype(F32) + swap(away, axis, mask, size).astype(F32)
        value = value.astype(wire if left else last)
    return value


def in_number_order(pieces, mine):
    pieces = list(pieces)
    step = 1
    while step < len(pieces):
        flip = (mine & step) != 0
        for i in range(len(pieces)):
            if not i & step:
                a, b = pieces[i], pieces[i | step]
                pieces[i] = jnp.where(flip, b, a)
                pieces[i | step] = jnp.where(flip, a, b)
        step *= 2
    return pieces


def gather_blocks(value, axis, size, masks):
    held = {0: value}
    for mask in masks:
        held.update({r ^ mask: swap(piece, axis, mask, size) for r, piece in list(held.items())})
    return held


def body(
    seqs,
    shards,
    layer_input,
    cotangent,
    weight_qkv,
    weight_merge,
    weight_expand,
    weight_shrink,
    norm_gains,
    all_biases,
    bias_hidden,
    moment_qkv,
    moment_merge,
    moment_expand,
    moment_shrink,
    moment_gains,
    moment_biases,
    moment_hidden,
    squares_qkv,
    squares_merge,
    squares_expand,
    squares_shrink,
    squares_gains,
    squares_biases,
    squares_hidden,
):
    params = (
        weight_qkv,
        weight_merge,
        weight_expand,
        weight_shrink,
        norm_gains,
        all_biases,
        bias_hidden,
    )
    moments = (
        moment_qkv,
        moment_merge,
        moment_expand,
        moment_shrink,
        moment_gains,
        moment_biases,
        moment_hidden,
    )
    squares = (
        squares_qkv,
        squares_merge,
        squares_expand,
        squares_shrink,
        squares_gains,
        squares_biases,
        squares_hidden,
    )
    devices = seqs * shards
    mine = lax.axis_index("seq")
    seq_bits = bits_of("seq", seqs)
    shard_bits = bits_of("shard", shards)
    bits = seq_bits + shard_bits
    ks, kh = len(seq_bits), len(shard_bits)
    core = ks + kh - 1
    far = [place for place in reversed(range(ks, core))]
    one_way = [core] + list(reversed(range(ks))) + far
    other_way = [core] + list(range(ks)) + far
    tokens = layer_input[0]
    count, width = tokens.shape
    local = width // seqs
    pairs = local // 128
    hidden_width = bias_hidden.shape[0] * devices
    part = norm_gains.shape[1]

    small = jnp.concatenate(
        [
            norm_gains.astype(BF16).reshape(-1),
            all_biases.astype(BF16).reshape(-1),
            bias_hidden.astype(BF16),
        ]
    )
    small = gather_bits(small[None], bits, list(range(len(bits))))
    small = small.reshape(devices, 8 * part + bias_hidden.shape[0]).astype(F32)
    rows = small[:, : 8 * part].reshape(devices, 8, part).transpose(1, 0, 2).reshape(8, width)
    gains, biases = rows[:2], rows[2:]
    hidden_bias = small[:, 8 * part :].reshape(hidden_width)

    by_heads = weight_qkv.astype(BF16).reshape(-1, 3, seqs, local)
    columns = [
        swap(lax.dynamic_index_in_dim(by_heads, mine ^ r, 2, keepdims=False), "seq", r, seqs)
        if r
        else lax.dynamic_index_in_dim(by_heads, mine, 2, keepdims=False)
        for r in range(seqs)
    ]
    columns = jnp.stack(in_number_order(columns, mine))
    columns = columns.reshape(seqs, -1, 3 * local)
    for place in range(kh):
        axis, mask, size, bit = shard_bits[place]
        other = swap(columns, axis, mask, size)
        columns = jnp.stack(
            [jnp.where(bit == 1, other, columns), jnp.where(bit == 1, columns, other)],
            axis=1 + place,
        )
    own_qkv = columns.reshape(width, 3 * local)

    half = count // 2
    masks = [1 << b for b in range(ks)]
    upper = gather_blocks(tokens[:half], "seq", seqs, masks)
    lower = gather_blocks(tokens[half:], "seq", seqs, masks[::-1])
    every = jnp.concatenate(
        [piece for r in range(seqs) for piece in (upper[r], lower[r])], axis=0
    )

    full_merge = gather_bits(
        weight_merge.astype(BF16), bits, list(range(ks, core)) + list(range(ks)) + [core]
    ).reshape(width, width)
    full_expand = lax.all_gather(weight_expand.astype(BF16), ("seq", "shard"), axis=0, tiled=True)
    full_shrink = lax.all_gather(weight_shrink.astype(BF16), ("seq", "shard"), axis=0, tiled=True)

    own_bias = lax.dynamic_slice_in_dim(biases[1:3], mine * local, local, 1)
    bias_row = jnp.concatenate([own_bias[0], jnp.zeros((local,), F32), own_bias[1]])
    qkv = (jnp.dot(every, own_qkv, preferred_element_type=F32) + bias_row).astype(BF16)
    query, keys, values = qkv[:, :local], qkv[:, local : 2 * local], qkv[:, 2 * local :]
    length = qkv.shape[0]
    block = min(512, length)
    contexts, totals, arrived = [], [], []
    for pair in range(pairs):
        context_pair, total = attend_forward(query, keys, values, pair, block)
        contexts.append(context_pair)
        totals.append(total)
        arrived.append(
            in_number_order(
                [
                    swap(context_pair[r * count : (r + 1) * count], "seq", r, seqs)
                    if r
                    else context_pair[:count]
                    for r in range(seqs)
                ],
                mine,
            )
        )
    context = jnp.concatenate(
        [arrived[pair][s] for s in range(seqs) for pair in range(pairs)], axis=1
    )

    attended = jnp.dot(context, full_merge, preferred_element_type=F32) + biases[3]
    first, normed_one, inverse_one = norm_forward(
        tokens.astype(F32) + attended, gains[0], biases[0]
    )
    first_low = first.astype(BF16)
    hidden = jnp.dot(first_low, full_expand, preferred_element_type=F32) + hidden_bias
    active = jax.nn.gelu(hidden, approximate=False).astype(BF16)
    branch = jnp.dot(active, full_shrink, preferred_element_type=F32) + biases[5]
    result, normed_two, inverse_two = norm_forward(first + branch, gains[1], biases[4])
    grad_out = cotangent[0]
    grad_gain_two = jnp.sum(grad_out * normed_two, axis=0)
    grad_shift_two = jnp.sum(grad_out, axis=0)
    grad_mid = norm_backward(grad_out, normed_two, inverse_two, gains[1])
    grad_branch = grad_mid.astype(BF16)
    grad_shrink_bias = jnp.sum(grad_branch, axis=0, dtype=F32)

    def summed_weight(left, right):
        middle = right.shape[1] // 2
        parts = []
        for piece, order in ((right[:, :middle], one_way), (right[:, middle:], other_way)):
            grad = lax.dot_general(left, piece, TN, preferred_element_type=F32).astype(BF16)
            grad = grad.reshape((2,) * len(bits) + (-1, middle))
            parts.append(scatter_bits(grad, bits, order))
        return jnp.concatenate(parts, axis=1)

    summed_shrink = summed_weight(active, grad_branch)
    grad_active = lax.dot_general(grad_branch, full_shrink, NT, preferred_element_type=F32)
    grad_hidden = (grad_active * gelu_slope(hidden)).astype(BF16)
    grad_hidden_bias = jnp.sum(grad_hidden, axis=0, dtype=F32)
    summed_expand = summed_weight(first_low, grad_hidden)
    grad_first = grad_mid + lax.dot_general(
        grad_hidden, full_expand, NT, preferred_element_type=F32
    )
    grad_gain_one = jnp.sum(grad_first * normed_one, axis=0)
    grad_shift_one = jnp.sum(grad_first, axis=0)
    grad_residual = norm_backward(grad_first, normed_one, inverse_one, gains[0])
    grad_attended = grad_residual.astype(BF16)
    grad_merge_bias = jnp.sum(grad_attended, axis=0, dtype=F32)
    grad_heads = lax.dot_general(
        grad_attended, full_merge, NT, preferred_element_type=F32
    ).astype(BF16)
    grad_context = jnp.concatenate(
        [
            swap(lax.dynamic_slice_in_dim(grad_heads, (mine ^ r) * local, local, 1), "seq", r, seqs)
            if r
            else lax.dynamic_slice_in_dim(grad_heads, mine * local, local, 1)
            for r in range(seqs)
        ],
        axis=0,
    )
    summed_merge = summed_weight(context, grad_attended)

    small_grads = jnp.concatenate(
        [
            jnp.stack(
                [
                    grad_gain_one,
                    grad_gain_two,
                    grad_shift_one,
                    grad_merge_bias,
                    grad_shift_two,
                    grad_shrink_bias,
                ]
            )
            .reshape(6, devices, part)
            .transpose(1, 0, 2)
            .reshape(devices, 6 * part),
            grad_hidden_bias.reshape(devices, -1),
        ],
        axis=1,
    )
    small_grads = scatter_bits(
        small_grads.reshape((2,) * len(bits) + (1, -1)), bits, list(range(len(bits))), F32, F32
    )[0]

    grads = [
        attend_backward(
            query, keys, values, contexts[pair], grad_context, totals[pair], pair, block
        )
        for pair in range(pairs)
    ]
    grad_rows = jnp.concatenate(
        [grads[pair][which] for which in range(3) for pair in range(pairs)], axis=1
    )
    grad_weight = lax.dot_general(every, grad_rows, TN, preferred_element_type=F32).astype(BF16)
    grad_weight = grad_weight.reshape((seqs,) + (2,) * kh + (-1, 3 * local))
    for turn, place in enumerate(reversed(range(kh))):
        axis, mask, size, bit = shard_bits[place]
        away = lax.dynamic_index_in_dim(grad_weight, 1 - bit, 1 + place, keepdims=False)
        keep = lax.dynamic_index_in_dim(grad_weight, bit, 1 + place, keepdims=False)
        grad_weight = (
            keep.astype(F32) + swap(away, axis, mask, size).astype(F32)
        ).astype(BF16)
    summed_qkv = in_number_order(
        [
            swap(lax.dynamic_index_in_dim(grad_weight, mine ^ r, 0, keepdims=False), "seq", r, seqs)
            if r
            else lax.dynamic_index_in_dim(grad_weight, mine, 0, keepdims=False)
            for r in range(seqs)
        ],
        mine,
    )
    summed_qkv = (
        jnp.stack([piece.reshape(-1, 3, local) for piece in summed_qkv], axis=2)
        .reshape(-1, 3 * width)
        .astype(F32)
    )
    head_sums = jnp.stack(
        [
            jnp.sum(grad_rows[:, :local], axis=0, dtype=F32).reshape(shards, part),
            jnp.sum(grad_rows[:, 2 * local :], axis=0, dtype=F32).reshape(shards, part),
        ],
        axis=1,
    )
    head_sums = scatter_bits(
        head_sums.reshape((2,) * kh + (2, part)), shard_bits, list(range(kh)), F32, F32
    )
    spread = lax.dot_general(grad_rows, own_qkv, NT, preferred_element_type=F32)
    grad_input = grad_residual + spread[:count]
    for r in range(1, seqs):
        away = spread[r * count : (r + 1) * count].astype(BF16)
        grad_input = grad_input + swap(away, "seq", r, seqs).astype(F32)

    small_rows = small_grads[: 6 * part].reshape(6, part)
    summed = (
        summed_qkv,
        summed_merge,
        summed_expand,
        summed_shrink,
        small_rows[:2],
        jnp.concatenate([small_rows[2:3], head_sums, small_rows[3:]], axis=0),
        small_grads[6 * part :],
    )
    finals = []
    momenta = []
    squared_all = []
    for index in range(7):
        master, change, momentum, squared = adam_update(
            params[index], summed[index], moments[index], squares[index], index < 4
        )
        finals.append(master if index < 4 else change)
        momenta.append(momentum)
        squared_all.append(squared)
    layer_output = result.astype(BF16)[None]
    return (
        (layer_output, grad_input[None])
        + summed
        + tuple(finals)
        + tuple(momenta)
        + tuple(squared_all)
    )


def solution(mesh):
    both = ("seq", "shard")
    rows, columns, flat = P(both, None), P(None, both), P(both)
    group = (rows, rows, rows, rows, columns, columns, flat)
    states = P("shard", "seq", None)
    return jax.shard_map(
        functools.partial(body, mesh.shape["seq"], mesh.shape["shard"]),
        mesh=mesh,
        in_specs=(states, states) + group * 3,
        out_specs=(states, states) + group * 4,
        check_vma=False,
    )
```

time: 1540 us -> 586 us (0.38)
  waiting for transfers between devices: 901 us -> 217 us
  matrix products: 272 us -> 93.8 us
  blocking collectives: 177 us -> 0 us
  Pallas kernels: 0 us -> 76.7 us
  starting transfers between devices: 28.5 us -> 78.9 us
  other arithmetic: 83.8 us -> 45.4 us
    reduce_scatter x3 -> x0, waiting for transfers between devices: 511 us -> none  [the longest x1 186 us: body(): lax.psum_scatter(grad_expand, ('seq', 'shard'), scatter_dimension=0, tile...]
    unnamed x13 -> x2, waiting for transfers between devices: 293 us -> 0.03 us
    ppermute x0 -> x78, waiting for transfers between devices: none -> 216 us  [swap(): return lax.ppermute(value, axis, [(i, i ^ mask) for i in range(size)])]
    dot_general x40 -> x15, matrix products: 272 us -> 93.8 us  [the longest x1 27.9 us: body(): jnp.dot(first_low, full_expand, preferred_element_type=F32) + hidden_bias]
    all_gather x3 -> x0, blocking collectives: 122 us -> none  [the longest x1 43.8 us: body(): lax.all_gather(lowered[5], ('seq', 'shard'), axis=1, tiled=True)]
    ppermute x0 -> x78, starting transfers between devices: none -> 78.8 us  [swap(): return lax.ppermute(value, axis, [(i, i ^ mask) for i in range(size)])]
    pallas_call x0 -> x4, Pallas kernels: none -> 76.7 us  [the longest x2 47.5 us: attend_backward(): pl.pallas_call(backward_kernel, grid=(length // block,), in_specs=[whole,...]
    all_to_all x7 -> x0, waiting for transfers between devices: 71.3 us -> none  [the longest x1 14.5 us: body(): lax.all_to_all(grad_heads, 'seq', split_axis=1, concat_axis=0, tiled=True)]
  transfers between devices with their start and end apart: 17 -> 80, of which waited for: 13 -> 40; matrix products, arithmetic and copies ran while one was open for 12% -> 21% of each run, Pallas kernels for 0% -> 13%
where the time goes in v1:
time: 586 us; the launch traced here: 580 us
  waiting for transfers between devices  217 us (37%)
  matrix products  93.8 us (16%)
  starting transfers between devices  78.9 us (13%)
  Pallas kernels  76.7 us (13%)
  local copies, waits for them, and re-layouts  52.2 us (9%)
  other arithmetic  45.4 us (8%)
  between operations  16.1 us (3%)
    ppermute x78, waiting for transfers between devices, swap(): return lax.ppermute(value, axis, [(i, i ^ mask) for i in range(size)])  216 us
    ppermute x78, starting transfers between devices, swap(): return lax.ppermute(value, axis, [(i, i ^ mask) for i in range(size)])  78.8 us
    pallas_call x2, Pallas kernels, attend_backward(): pl.pallas_call(backward_kernel, grid=(length // block,), in_specs=[whole,...  47.5 us
    pallas_call x2, Pallas kernels, attend_forward(): pl.pallas_call(forward_kernel, grid=(length // block,), in_specs=[pl.Bloc...  29.2 us
    dot_general x1, matrix products, body(): jnp.dot(first_low, full_expand, preferred_element_type=F32) + hidden_bias  27.9 us
    dot_general x6, matrix products, summed_weight(): lax.dot_general(left, piece, TN, preferred_element_type=F32).astype(BF16)  22.6 us
    unnamed x143, local copies, waits for them, and re-layouts  19.2 us
    convert_element_type x24, other arithmetic, scatter_bits(): value = value.astype(wire if left else last)  14.5 us
  transfers between devices with their start and end apart: 80, of which 40 were waited for; matrix products, arithmetic and copies ran while one was open for 21% of the time, Pallas kernels for 13%

profile of v1, /device:TPU:0, one launch (start us, length us, event | category | flops | bytes accessed | tf_op | source)
XLA Modules:
  0.0 580.4 jit_solution(5689312094979635787)
XLA Ops:
  48.4 5.9 %collective-permute-done.23 = bf16[32,1024]{1,0:T(8,128)(2,1)S(1)} collective-permute-done((bf16[32,1024]{1,0:T(8,128)(2,1)}, bf16[32,1024]{1,0:T(8,128)(2,1)S(1)}, u32[]{:S(2)}, u32[]{:S(2)}) %collective-permute-start.23) | collective-permute-done | bytes 65568 | tf_op jit(solution)/shard_map/ppermute | solution.py:201
  54.6 5.7 collective-permute-done.24
  60.5 12.8 %collective-permute-done.9 = bf16[4,32,768]{2,1,0:T(8,128)(2,1)S(1)} collective-permute-done((bf16[4,32,768]{2,1,0:T(8,128)(2,1)S(1)}, bf16[4,32,768]{2,1,0:T(8,128)(2,1)S(1)}, u32[]{:S(2)}, u32[]{:S(2)}) %collective-permute-start.9) | collective-permute-done | bytes 196640 | tf_op jit(solution)/shard_map/ppermute | solution.py:201
  74.9 11.2 %collective-permute-done.25 = bf16[2,2,32,1024]{3,2,1,0:T(8,128)(2,1)S(1)} collective-permute-done((bf16[2,2,32,1024]{3,2,1,0:T(8,128)(2,1)S(1)}, bf16[2,2,32,1024]{3,2,1,0:T(8,128)(2,1)S(1)}, u32[]{:S(2)}, u32[]{:S(2)}) %collective-permute-start.25) | collective-permute-done | bytes 262176 | tf_op jit(solution)/shard_map/ppermute | solution.py:201
  92.3 15.3 %collective-permute-done.10 = bf16[4,2,32,768]{3,2,0,1:T(8,128)(2,1)S(1)} collective-permute-done((bf16[4,2,32,768]{3,2,0,1:T(8,128)(2,1)S(1)}, bf16[4,2,32,768]{3,2,0,1:T(8,128)(2,1)S(1)}, u32[]{:S(2)}, u32[]{:S(2)}) %collective-permute-start.10) | collective-permute-done | bytes 393248 | tf_op jit(solution)/shard_map/ppermute | solution.py:201
  109.7 5.5 collective-permute-done.5
  117.7 3.8 add_convert_fusion
  121.8 14.6 %attend_forward.2 = (bf16[2048,128]{1,0:T(8,128)(2,1)S(1)}, f32[1,2,2048]{2,1,0:T(2,128)S(1)}) custom-call(bf16[2048,256]{1,0:T(8,128)(2,1)S(1)} %get-tuple-element.106.q_ref, bf16[2048,256]{1,0:T(8,128)(2,1)S(1)} %get-tuple-element.105.k_ref, bf16[2048,256]{1,0:T(8,128)(2,1)S(1)} %get-tuple-element.104.v_ref), custom_call_target="tpu_custom_call" | custom-call | flops 8589934592 | bytes 2097152 | tf_op jit(solution)/shard_map/attend_forward/pallas_call | solution.py:80
  140.0 14.6 %attend_forward.3 = (bf16[2048,128]{1,0:T(8,128)(2,1)S(1)}, f32[1,2,2048]{2,1,0:T(2,128)S(1)}) custom-call(bf16[2048,256]{1,0:T(8,128)(2,1)S(1)} %get-tuple-element.106.q_ref, bf16[2048,256]{1,0:T(8,128)(2,1)S(1)} %get-tuple-element.105.k_ref, bf16[2048,256]{1,0:T(8,128)(2,1)S(1)} %get-tuple-element.104.v_ref), custom_call_target="tpu_custom_call" | custom-call | flops 8589934592 | bytes 2097152 | tf_op jit(solution)/shard_map/attend_forward/pallas_call | solution.py:80
  167.5 27.9 %fusion.2 = (bf16[512,4096]{1,0:T(8,128)(2,1)}, f32[512,4096]{1,0:T(8,128)}) fusion(f32[4096]{0:T(1024)S(1)} %slice_bitcast_fusion.2, bf16[1024,4096]{1,0:T(8,128)(2,1)} %all-gather.3.cloned.1.call-done, f32[512,1024]{1,0:T(8,128)} %copy-done.14, f32[1024]{0:T(1024)S(1)} %add.499, f32[1024]{0:T(1024)S(1)} %mul.402, f32[512]{0:T(512)S(1)} %add_rsqrt_fusion.1, ...), kind=kOutput, calls=%fused_computation.4 | convolution fusion | flops 4436000768 | bytes 23097344 | tf_op jit(solution)/shard_map/dot_general | solution.py:404
  196.2 9.9 %fusion.117 = (f32[512]{0:T(512)S(1)}, f32[512,1024]{1,0:T(8,128)S(1)}) fusion(f32[1024]{0:T(1024)S(1)} %add.505, bf16[512,4096]{1,0:T(8,128)(2,1)} %get-tuple-element.175, bf16[4096,1024]{1,0:T(8,128)(2,1)} %all-gather.5.cloned.1.call-done, f32[1024]{0:T(1024)S(1)} %add.499, f32[1024]{0:T(1024)S(1)} %mul.402, f32[512]{0:T(512)S(1)} %add_rsqrt_fusion.1, ...), kind=kOutput, calls=%fused_computation.404 | convolution fusion | flops 4298636800 | bytes 16795648 | tf_op jit(solution)/shard_map/dot_general | solution.py:406
  211.1 4.6 convolution_convert_fusion.1
  215.6 4.5 convolution_convert_fusion
  220.2 10.6 %convert_reduce_fusion = (f32[4096]{0:T(1024)S(1)}, bf16[512,4096]{1,0:T(8,128)(2,1)}) fusion(f32[512,4096]{1,0:T(8,128)} %get-tuple-element.176, f32[4096]{0:T(1024)S(1)} %slice_bitcast_fusion.2, bf16[512,1024]{1,0:T(8,128)(2,1)S(1)} %get-tuple-element.84, bf16[4096,1024]{1,0:T(8,128)(2,1)S(1)} %bitcast.414), kind=kOutput, calls=%fused_computation.11 | convolution fusion | flops 4322226176 | bytes 22052864 | tf_op jit(solution)/shard_map/dot_general | solution.py:425
  230.8 6.4 %convolution_convert_fusion.3 = bf16[1024,2048]{1,0:T(8,128)(2,1)} fusion(bf16[512,4096]{1,0:T(8,128)(2,1)} %get-tuple-element.183, f32[512,1024]{1,0:T(8,128)S(1)} %copy-done.15, f32[1024]{0:T(1024)S(1)} %add.499, f32[1024]{0:T(1024)S(1)} %mul.402, f32[512]{0:T(512)S(1)} %add_rsqrt_fusion.1, f32[512]{0:T(512)S(1)} %broadcast_multiply_fusion.5), kind=kOutput, calls=%fused_computation.39 | convolution fusion | flops 2152202240 | bytes 8400896 | tf_op jit(solution)/shard_map/dot_general | solution.py:419
  237.2 4.7 convolution_convert_fusion.2
  241.9 7.2 %multiply_reduce_fusion = (f32[1024]{0:T(1024)S(1)}, f32[512]{0:T(512)S(1)}, f32[512]{0:T(512)S(1)}, f32[1024]{0:T(1024)S(1)}, f32[512,1024]{1,0:T(8,128)S(1)}) fusion(f32[512,1024]{1,0:T(8,128)S(1)} %copy-done.15, f32[512]{0:T(512)S(1)} %add_rsqrt_fusion.1, f32[512]{0:T(512)S(1)} %broadcast_multiply_fusion.5, f32[1024]{0:T(1024)S(1)} %mul.402, ...), kind=kOutput, calls=%fused_computation.72 | convolution fusion | flops 4300207104 | bytes 18894848 | tf_op jit(solution)/shard_map/dot_general | solution.py:429
  258.1 3.8 constant_dynamic-slice_fusion.20
  273.2 8.4 %collective-permute-done.71 = f32[2,2,2,1,320]{4,2,1,0,3:T(2,128)S(1)} collective-permute-done((f32[2,2,2,1,320]{4,2,1,0,3:T(2,128)S(1)}, f32[2,2,2,1,320]{4,2,1,0,3:T(2,128)S(1)}, u32[]{:S(2)}, u32[]{:S(2)}) %collective-permute-start.71) | collective-permute-done | bytes 10272 | tf_op jit(solution)/shard_map/ppermute | solution.py:201
  303.9 23.9 %attend_backward.3 = (bf16[2048,128]{1,0:T(8,128)(2,1)S(1)}, bf16[2048,128]{1,0:T(8,128)(2,1)S(1)}, bf16[2048,128]{1,0:T(8,128)(2,1)S(1)}) custom-call(bf16[2048,256]{1,0:T(8,128)(2,1)S(1)} %copy-done.5, bf16[2048,256]{1,0:T(8,128)(2,1)S(1)} %copy-done.3, bf16[2048,256]{1,0:T(8,128)(2,1)S(1)} %get-tuple-element.104.v_ref, ...), custom_call_target="tpu_custom_call" | custom-call | flops 21474836480 | bytes 5242880 | tf_op jit(solution)/shard_map/attend_backward/pallas_call | solution.py:176
  327.8 23.6 %attend_backward.2 = (bf16[2048,128]{1,0:T(8,128)(2,1)S(1)}, bf16[2048,128]{1,0:T(8,128)(2,1)S(1)}, bf16[2048,128]{1,0:T(8,128)(2,1)S(1)}) custom-call(bf16[2048,256]{1,0:T(8,128)(2,1)S(1)} %copy-done.5, bf16[2048,256]{1,0:T(8,128)(2,1)S(1)} %copy-done.3, bf16[2048,256]{1,0:T(8,128)(2,1)S(1)} %get-tuple-element.104.v_ref, bf16[2048,128]{1,0:T(8,128)(2,1)S(1)} %copy-done.1, ...), custom_call_target="tpu_custom_call" | custom-call | flops 21474836480 | bytes 5242880 | tf_op jit(solution)/shard_map/attend_backward/pallas_call | solution.py:176
  360.4 5.7 convolution_convert_fusion.4
  381.1 24.2 %collective-permute-done.41 = bf16[2,2,2,32,512]{4,3,1,2,0:T(8,128)(2,1)S(1)} collective-permute-done((bf16[2,2,2,32,512]{4,3,1,2,0:T(8,128)(2,1)S(1)}, bf16[2,2,2,32,512]{4,3,1,2,0:T(8,128)(2,1)S(1)}, u32[]{:S(2)}, u32[]{:S(2)}) %collective-permute-start.41) | collective-permute-done | bytes 262176 | tf_op jit(solution)/shard_map/ppermute | solution.py:201
  406.9 6.0 %collective-permute-done.46 = bf16[2,2,2,32,512]{4,3,1,2,0:T(8,128)(2,1)S(1)} collective-permute-done((bf16[2,2,2,32,512]{4,3,1,2,0:T(8,128)(2,1)S(1)}, bf16[2,2,2,32,512]{4,3,1,2,0:T(8,128)(2,1)S(1)}, u32[]{:S(2)}, u32[]{:S(2)}) %collective-permute-start.46) | collective-permute-done | bytes 262176 | tf_op jit(solution)/shard_map/ppermute | solution.py:201
  438.8 7.5 %collective-permute-done.35 = bf16[4,2,32,768]{3,2,1,0:T(8,128)(2,1)S(1)} collective-permute-done((bf16[4,2,32,768]{3,2,1,0:T(8,128)(2,1)S(1)}, bf16[4,2,32,768]{3,2,1,0:T(8,128)(2,1)S(1)}, u32[]{:S(2)}, u32[]{:S(2)}) %collective-permute-start.35) | collective-permute-done | bytes 393248 | tf_op jit(solution)/shard_map/ppermute | solution.py:201
  448.1 6.9 %collective-permute-done.36 = bf16[4,32,768]{2,1,0:T(8,128)(2,1)S(1)} collective-permute-done((bf16[4,32,768]{2,1,0:T(8,128)(2,1)S(1)}, bf16[4,32,768]{2,1,0:T(8,128)(2,1)S(1)}, u32[]{:S(2)}, u32[]{:S(2)}) %collective-permute-start.36) | collective-permute-done | bytes 196640 | tf_op jit(solution)/shard_map/ppermute | solution.py:201
  480.0 14.2 %collective-permute-done.61 = bf16[2,2,2,128,512]{4,3,1,2,0:T(8,128)(2,1)S(1)} collective-permute-done((bf16[2,2,2,128,512]{4,3,1,2,0:T(8,128)(2,1)S(1)}, bf16[2,2,2,128,512]{4,3,1,2,0:T(8,128)(2,1)S(1)}, u32[]{:S(2)}, u32[]{:S(2)}) %collective-permute-start.61) | collective-permute-done | bytes 1048608 | tf_op jit(solution)/shard_map/ppermute | solution.py:201
  499.2 17.4 %collective-permute-done.51 = bf16[2,2,2,32,2048]{4,3,1,2,0:T(8,128)(2,1)S(1)} collective-permute-done((bf16[2,2,2,32,2048]{4,3,1,2,0:T(8,128)(2,1)S(1)}, bf16[2,2,2,32,2048]{4,3,1,2,0:T(8,128)(2,1)S(1)}, u32[]{:S(2)}, u32[]{:S(2)}) %collective-permute-start.51) | collective-permute-done | bytes 1048608 | tf_op jit(solution)/shard_map/ppermute | solution.py:201
  521.8 9.3 %collective-permute-done.62 = bf16[2,2,128,512]{3,2,0,1:T(8,128)(2,1)S(1)} collective-permute-done((bf16[2,2,128,512]{3,2,0,1:T(8,128)(2,1)S(1)}, bf16[2,2,128,512]{3,2,0,1:T(8,128)(2,1)S(1)}, u32[]{:S(2)}, u32[]{:S(2)}) %collective-permute-start.62) | collective-permute-done | bytes 524320 | tf_op jit(solution)/shard_map/ppermute | solution.py:201
  533.6 7.9 %collective-permute-done.52 = bf16[2,2,32,2048]{3,2,0,1:T(8,128)(2,1)S(1)} collective-permute-done((bf16[2,2,32,2048]{3,2,0,1:T(8,128)(2,1)S(1)}, bf16[2,2,32,2048]{3,2,0,1:T(8,128)(2,1)S(1)}, u32[]{:S(2)}, u32[]{:S(2)}) %collective-permute-start.52) | collective-permute-done | bytes 524320 | tf_op jit(solution)/shard_map/ppermute | solution.py:201
  547.3 9.3 %collective-permute-done.53 = bf16[2,32,2048]{2,1,0:T(8,128)(2,1)S(1)} collective-permute-done((bf16[2,32,2048]{2,1,0:T(8,128)(2,1)S(1)}, bf16[2,32,2048]{2,1,0:T(8,128)(2,1)S(1)}, u32[]{:S(2)}, u32[]{:S(2)}) %collective-permute-start.53) | collective-permute-done | bytes 262176 | tf_op jit(solution)/shard_map/ppermute | solution.py:201
  560.8 8.3 %collective-permute-done.54 = bf16[32,2048]{1,0:T(8,128)(2,1)S(1)} collective-permute-done((bf16[32,2048]{1,0:T(8,128)(2,1)S(1)}, bf16[32,2048]{1,0:T(8,128)(2,1)S(1)}, u32[]{:S(2)}, u32[]{:S(2)}) %collective-permute-start.54) | collective-permute-done | bytes 131104 | tf_op jit(solution)/shard_map/ppermute | solution.py:201
  (522 shorter events, 223.0 us)
Async XLA Ops:
  7.2 160.2 %all-gather.3.cloned.1.call-start = ((), (), s32[]{:S(2)}) async-start(), calls=%async_computation | async-start | bytes 8650752 | tf_op jit(solution)/shard_map/all_gather | solution.py:370
  9.2 187.0 %all-gather.5.cloned.1.call-start = ((), (), s32[]{:S(2)}) async-start(), calls=%async_computation.1 | async-start | bytes 8650752 | tf_op jit(solution)/shard_map/all_gather | solution.py:371
  20.4 65.8 %collective-permute-start = (bf16[256,1024]{1,0:T(8,128)(2,1)}, bf16[256,1024]{1,0:T(8,128)(2,1)}, u32[]{:S(2)}, u32[]{:S(2)}) collective-permute-start(bf16[256,1024]{1,0:T(8,128)(2,1)} %get-tuple-element.123), channel_id=1, source_target_pairs={{0,8},{8,0},{16,24},{24,16},{1,9},{9,1},{17,25},{25,17},{2,10},{10... | collective-permute-start | bytes 1572872 | tf_op jit(solution)/shard_map/ppermute | solution.py:201
  20.4 87.4 %collective-permute-start.2 = (bf16[256,1024]{1,0:T(8,128)(2,1)}, bf16[256,1024]{1,0:T(8,128)(2,1)}, u32[]{:S(2)}, u32[]{:S(2)}) collective-permute-start(bf16[256,1024]{1,0:T(8,128)(2,1)} %get-tuple-element.123), channel_id=1, source_target_pairs={{0,16},{8,24},{16,0},{24,8},{1,17},{9,25},{17,1},{25,9},{2,18},{10... | collective-permute-start | bytes 1572872 | tf_op jit(solution)/shard_map/ppermute | solution.py:201
  43.1 46.6 %collective-permute-start.1 = (bf16[256,1024]{1,0:T(8,128)(2,1)}, bf16[256,1024]{1,0:T(8,128)(2,1)S(1)}, u32[]{:S(2)}, u32[]{:S(2)}) collective-permute-start(bf16[256,1024]{1,0:T(8,128)(2,1)} %get-tuple-element.122), channel_id=1, source_target_pairs={{0,8},{8,0},{16,24},{24,16},{1,9},{9,1},{17,25},{25,17},{2,10},{10... | collective-permute-start | bytes 1572872 | tf_op jit(solution)/shard_map/ppermute | solution.py:201
  44.6 47.6 %collective-permute-start.3 = (bf16[256,1024]{1,0:T(8,128)(2,1)}, bf16[256,1024]{1,0:T(8,128)(2,1)S(1)}, u32[]{:S(2)}, u32[]{:S(2)}) collective-permute-start(bf16[256,1024]{1,0:T(8,128)(2,1)} %get-tuple-element.122), channel_id=1, source_target_pairs={{0,16},{8,24},{16,0},{24,8},{1,17},{9,25},{17,1},{25,9},{2,18},{10... | collective-permute-start | bytes 1572872 | tf_op jit(solution)/shard_map/ppermute | solution.py:201
  86.1 21.5 %collective-permute-start.10 = (bf16[4,2,32,768]{3,2,0,1:T(8,128)(2,1)S(1)}, bf16[4,2,32,768]{3,2,0,1:T(8,128)(2,1)S(1)}, u32[]{:S(2)}, u32[]{:S(2)}) collective-permute-start(bf16[4,2,32,768]{3,2,0,1:T(8,128)(2,1)S(1)} %pad_maximum_fusion.8), channel_id=1, source_target_pairs={{0,2},{1,3},{2,0},{3,1},{4,6},{5,7},{6,4},{7,5},{8,10},{9,11},{10,... | collective-permute-start | bytes 1179656 | tf_op jit(solution)/shard_map/ppermute | solution.py:201
  86.2 22.7 %collective-permute-start.26 = (bf16[2,2,2,32,1024]{4,3,2,1,0:T(8,128)(2,1)S(1)}, bf16[2,2,2,32,1024]{4,3,2,1,0:T(8,128)(2,1)S(1)}, u32[]{:S(2)}, u32[]{:S(2)}) collective-permute-start(bf16[2,2,2,32,1024]{4,3,2,1,0:T(8,128)(2,1)S(1)} %pad_maximum_fusion.5), channel_id=1, source_target_pairs={{0,8},{8,0},{16,24},{24,16},{1,9},{9,1},{17,25},{25,17},{2,10},{10... | collective-permute-start | bytes 1572872 | tf_op jit(solution)/shard_map/ppermute | solution.py:201
  89.6 20.1 %collective-permute-start.4 = (bf16[256,1024]{1,0:T(8,128)(2,1)}, bf16[256,1024]{1,0:T(8,128)(2,1)S(1)}, u32[]{:S(2)}, u32[]{:S(2)}) collective-permute-start(bf16[256,1024]{1,0:T(8,128)(2,1)} %collective-permute-done), channel_id=1, source_target_pairs={{0,16},{8,24},{16,0},{24,8},{1,17},{9,25},{17,1},{25,9},{2,18},{10... | collective-permute-start | bytes 1572872 | tf_op jit(solution)/shard_map/ppermute | solution.py:201
  92.2 23.1 %collective-permute-start.5 = (bf16[256,1024]{1,0:T(8,128)(2,1)S(1)}, bf16[256,1024]{1,0:T(8,128)(2,1)S(1)}, u32[]{:S(2)}, u32[]{:S(2)}) collective-permute-start(bf16[256,1024]{1,0:T(8,128)(2,1)S(1)} %collective-permute-done.3), channel_id=1, source_target_pairs={{0,8},{8,0},{16,24},{24,16},{1,9},{9,1},{17,25},{25,17},{2,10},{10... | collective-permute-start | bytes 1572872 | tf_op jit(solution)/shard_map/ppermute | solution.py:201
  109.1 54.2 %collective-permute-start.27 = (bf16[2,2,2,2,32,1024]{5,4,3,2,1,0:T(8,128)(2,1)S(1)}, bf16[2,2,2,2,32,1024]{5,4,3,2,1,0:T(8,128)(2,1)S(1)}, u32[]{:S(2)}, u32[]{:S(2)}) collective-permute-start(bf16[2,2,2,2,32,1024]{5,4,3,2,1,0:T(8,128)(2,1)S(1)} %pad_maximum_fusion.2), channel_id=1, source_target_pairs={{0,1},{1,0},{2,3},{3,2},{4,5},{5,4},{6,7},{7,6},{8,9},{9,8},{10,11... | collective-permute-start | bytes 3145736 | tf_op jit(solution)/shard_map/ppermute | solution.py:201
  136.4 19.7 %collective-permute-start.17 = (bf16[512,128]{1,0:T(8,128)(2,1)S(1)}, bf16[512,128]{1,0:T(8,128)(2,1)S(1)}, u32[]{:S(2)}, u32[]{:S(2)}) collective-permute-start(bf16[512,128]{1,0:T(8,128)(2,1)S(1)} %get-tuple-element.133), channel_id=1, source_target_pairs={{0,24},{8,16},{16,8},{24,0},{1,25},{9,17},{17,9},{25,1},{2,26},{10... | collective-permute-start | bytes 393224 | tf_op jit(solution)/shard_map/ppermute | solution.py:201
  138.3 19.9 %collective-permute-start.19 = (bf16[512,128]{1,0:T(8,128)(2,1)S(1)}, bf16[512,128]{1,0:T(8,128)(2,1)S(1)}, u32[]{:S(2)}, u32[]{:S(2)}) collective-permute-start(bf16[512,128]{1,0:T(8,128)(2,1)S(1)} %get-tuple-element.131), channel_id=1, source_target_pairs={{0,8},{8,0},{16,24},{24,16},{1,9},{9,1},{17,25},{25,17},{2,10},{10... | collective-permute-start | bytes 393224 | tf_op jit(solution)/shard_map/ppermute | solution.py:201
  255.2 44.2 %collective-permute-start.29 = (bf16[512,256]{1,0:T(8,128)(2,1)}, bf16[512,256]{1,0:T(8,128)(2,1)}, u32[]{:S(2)}, u32[]{:S(2)}) collective-permute-start(bf16[512,256]{1,0:T(8,128)(2,1)} %get-tuple-element.118), channel_id=1, source_target_pairs={{0,16},{8,24},{16,0},{24,8},{1,17},{9,25},{17,1},{25,9},{2,18},{10... | collective-permute-start | bytes 786440 | tf_op jit(solution)/shard_map/ppermute | solution.py:201
  263.4 202.2 %collective-permute-start.60 = (bf16[2,2,2,2,128,512]{5,4,2,3,0,1:T(8,128)(2,1)}, bf16[2,2,2,2,128,512]{5,4,2,3,0,1:T(8,128)(2,1)}, u32[]{:S(2)}, u32[]{:S(2)}) collective-permute-start(bf16[2,2,2,2,128,512]{5,4,2,3,0,1:T(8,128)(2,1)} %bitcast.382), channel_id=1, source_target_pairs={{0,1},{1,0},{2,3},{3,2},{4,5},{5,4},{6,7},{7,6},{8,9},{9,8},{10,11... | collective-permute-start | bytes 6291464 | tf_op jit(solution)/shard_map/ppermute | solution.py:201
  267.6 31.8 %collective-permute-start.28 = (bf16[512,256]{1,0:T(8,128)(2,1)}, bf16[512,256]{1,0:T(8,128)(2,1)}, u32[]{:S(2)}, u32[]{:S(2)}) collective-permute-start(bf16[512,256]{1,0:T(8,128)(2,1)} %get-tuple-element.119), channel_id=1, source_target_pairs={{0,8},{8,0},{16,24},{24,16},{1,9},{9,1},{17,25},{25,17},{2,10},{10... | collective-permute-start | bytes 786440 | tf_op jit(solution)/shard_map/ppermute | solution.py:201
  269.1 30.3 %collective-permute-start.30 = (bf16[512,256]{1,0:T(8,128)(2,1)S(1)}, bf16[512,256]{1,0:T(8,128)(2,1)}, u32[]{:S(2)}, u32[]{:S(2)}) collective-permute-start(bf16[512,256]{1,0:T(8,128)(2,1)S(1)} %get-tuple-element.117), channel_id=1, source_target_pairs={{0,24},{8,16},{16,8},{24,0},{1,25},{9,17},{17,9},{25,1},{2,26},{10... | collective-permute-start | bytes 786440 | tf_op jit(solution)/shard_map/ppermute | solution.py:201
  297.3 79.2 %collective-permute-start.40 = (bf16[2,2,2,2,32,512]{5,4,2,3,0,1:T(8,128)(2,1)}, bf16[2,2,2,2,32,512]{5,4,2,3,0,1:T(8,128)(2,1)}, u32[]{:S(2)}, u32[]{:S(2)}) collective-permute-start(bf16[2,2,2,2,32,512]{5,4,2,3,0,1:T(8,128)(2,1)} %bitcast.386), channel_id=1, source_target_pairs={{0,1},{1,0},{2,3},{3,2},{4,5},{5,4},{6,7},{7,6},{8,9},{9,8},{10,11... | collective-permute-start | bytes 1572872 | tf_op jit(solution)/shard_map/ppermute | solution.py:201
  299.3 79.0 %collective-permute-start.45 = (bf16[2,2,2,2,32,512]{5,4,2,3,1,0:T(8,128)(2,1)}, bf16[2,2,2,2,32,512]{5,4,2,3,1,0:T(8,128)(2,1)}, u32[]{:S(2)}, u32[]{:S(2)}) collective-permute-start(bf16[2,2,2,2,32,512]{5,4,2,3,1,0:T(8,128)(2,1)} %bitcast.385), channel_id=1, source_target_pairs={{0,1},{1,0},{2,3},{3,2},{4,5},{5,4},{6,7},{7,6},{8,9},{9,8},{10,11... | collective-permute-start | bytes 1572872 | tf_op jit(solution)/shard_map/ppermute | solution.py:201
  370.3 62.2 %collective-permute-start.34 = (bf16[4,2,2,32,768]{4,3,2,1,0:T(8,128)(2,1)S(1)}, bf16[4,2,2,32,768]{4,3,2,1,0:T(8,128)(2,1)S(1)}, u32[]{:S(2)}, u32[]{:S(2)}) collective-permute-start(bf16[4,2,2,32,768]{4,3,2,1,0:T(8,128)(2,1)S(1)} %dynamic-slice_bitcast_fusion.4), channel_id=1, source_target_pairs={{0,1},{1,0},{2,3},{3,2},{4,5},{5,4},{6,7},{7,6},{8,9},{9,8},{10,11... | collective-permute-start | bytes 2359304 | tf_op jit(solution)/shard_map/ppermute | solution.py:201
  374.4 80.6 %collective-permute-start.31 = (bf16[512,1024]{1,0:T(8,128)(2,1)S(1)}, bf16[512,1024]{1,0:T(8,128)(2,1)S(1)}, u32[]{:S(2)}, u32[]{:S(2)}) collective-permute-start(bf16[512,1024]{1,0:T(8,128)(2,1)S(1)} %get-tuple-element.101), channel_id=1, source_target_pairs={{0,8},{8,0},{16,24},{24,16},{1,9},{9,1},{17,25},{25,17},{2,10},{10... | collective-permute-start | bytes 3145736 | tf_op jit(solution)/shard_map/ppermute | solution.py:201
  376.5 80.1 %collective-permute-start.32 = (bf16[512,1024]{1,0:T(8,128)(2,1)S(1)}, bf16[512,1024]{1,0:T(8,128)(2,1)S(1)}, u32[]{:S(2)}, u32[]{:S(2)}) collective-permute-start(bf16[512,1024]{1,0:T(8,128)(2,1)S(1)} %get-tuple-element.103), channel_id=1, source_target_pairs={{0,16},{8,24},{16,0},{24,8},{1,17},{9,25},{17,1},{25,9},{2,18},{10... | collective-permute-start | bytes 3145736 | tf_op jit(solution)/shard_map/ppermute | solution.py:201
  378.4 26.9 %collective-permute-start.41 = (bf16[2,2,2,32,512]{4,3,1,2,0:T(8,128)(2,1)S(1)}, bf16[2,2,2,32,512]{4,3,1,2,0:T(8,128)(2,1)S(1)}, u32[]{:S(2)}, u32[]{:S(2)}) collective-permute-start(bf16[2,2,2,32,512]{4,3,1,2,0:T(8,128)(2,1)S(1)} %dynamic-slice_bitcast_fusion.15), channel_id=1, source_target_pairs={{0,8},{8,0},{16,24},{24,16},{1,9},{9,1},{17,25},{25,17},{2,10},{10... | collective-permute-start | bytes 786440 | tf_op jit(solution)/shard_map/ppermute | solution.py:201
  437.4 20.7 %collective-permute-start.33 = (bf16[512,1024]{1,0:T(8,128)(2,1)S(1)}, bf16[512,1024]{1,0:T(8,128)(2,1)S(1)}, u32[]{:S(2)}, u32[]{:S(2)}) collective-permute-start(bf16[512,1024]{1,0:T(8,128)(2,1)S(1)} %get-tuple-element.102), channel_id=1, source_target_pairs={{0,24},{8,16},{16,8},{24,0},{1,25},{9,17},{17,9},{25,1},{2,26},{10... | collective-permute-start | bytes 3145736 | tf_op jit(solution)/shard_map/ppermute | solution.py:201
  468.0 26.1 %collective-permute-start.61 = (bf16[2,2,2,128,512]{4,3,1,2,0:T(8,128)(2,1)S(1)}, bf16[2,2,2,128,512]{4,3,1,2,0:T(8,128)(2,1)S(1)}, u32[]{:S(2)}, u32[]{:S(2)}) collective-permute-start(bf16[2,2,2,128,512]{4,3,1,2,0:T(8,128)(2,1)S(1)} %dynamic-slice_bitcast_fusion.1), channel_id=1, source_target_pairs={{0,8},{8,0},{16,24},{24,16},{1,9},{9,1},{17,25},{25,17},{2,10},{10... | collective-permute-start | bytes 3145736 | tf_op jit(solution)/shard_map/ppermute | solution.py:201
  471.3 26.1 %collective-permute-start.66 = (bf16[2,2,2,128,512]{4,3,1,2,0:T(8,128)(2,1)S(1)}, bf16[2,2,2,128,512]{4,3,1,2,0:T(8,128)(2,1)S(1)}, u32[]{:S(2)}, u32[]{:S(2)}) collective-permute-start(bf16[2,2,2,128,512]{4,3,1,2,0:T(8,128)(2,1)S(1)} %dynamic-slice_bitcast_fusion), channel_id=1, source_target_pairs={{0,16},{8,24},{16,0},{24,8},{1,17},{9,25},{17,1},{25,9},{2,18},{10... | collective-permute-start | bytes 3145736 | tf_op jit(solution)/shard_map/ppermute | solution.py:201
  475.4 41.2 %collective-permute-start.51 = (bf16[2,2,2,32,2048]{4,3,1,2,0:T(8,128)(2,1)S(1)}, bf16[2,2,2,32,2048]{4,3,1,2,0:T(8,128)(2,1)S(1)}, u32[]{:S(2)}, u32[]{:S(2)}) collective-permute-start(bf16[2,2,2,32,2048]{4,3,1,2,0:T(8,128)(2,1)S(1)} %dynamic-slice_bitcast_fusion.3), channel_id=1, source_target_pairs={{0,8},{8,0},{16,24},{24,16},{1,9},{9,1},{17,25},{25,17},{2,10},{10... | collective-permute-start | bytes 3145736 | tf_op jit(solution)/shard_map/ppermute | solution.py:201
  478.7 41.2 %collective-permute-start.56 = (bf16[2,2,2,32,2048]{4,3,1,2,0:T(8,128)(2,1)S(1)}, bf16[2,2,2,32,2048]{4,3,1,2,0:T(8,128)(2,1)S(1)}, u32[]{:S(2)}, u32[]{:S(2)}) collective-permute-start(bf16[2,2,2,32,2048]{4,3,1,2,0:T(8,128)(2,1)S(1)} %dynamic-slice_bitcast_fusion.2), channel_id=1, source_target_pairs={{0,16},{8,24},{16,0},{24,8},{1,17},{9,25},{17,1},{25,9},{2,18},{10... | collective-permute-start | bytes 3145736 | tf_op jit(solution)/shard_map/ppermute | solution.py:201
  494.5 36.6 %collective-permute-start.62 = (bf16[2,2,128,512]{3,2,0,1:T(8,128)(2,1)S(1)}, bf16[2,2,128,512]{3,2,0,1:T(8,128)(2,1)S(1)}, u32[]{:S(2)}, u32[]{:S(2)}) collective-permute-start(bf16[2,2,128,512]{3,2,0,1:T(8,128)(2,1)S(1)} %dynamic-slice_bitcast_fusion.6), channel_id=1, source_target_pairs={{0,16},{8,24},{16,0},{24,8},{1,17},{9,25},{17,1},{25,9},{2,18},{10... | collective-permute-start | bytes 1572872 | tf_op jit(solution)/shard_map/ppermute | solution.py:201
  497.7 33.9 %collective-permute-start.67 = (bf16[2,2,128,512]{3,2,0,1:T(8,128)(2,1)S(1)}, bf16[2,2,128,512]{3,2,0,1:T(8,128)(2,1)S(1)}, u32[]{:S(2)}, u32[]{:S(2)}) collective-permute-start(bf16[2,2,128,512]{3,2,0,1:T(8,128)(2,1)S(1)} %dynamic-slice_bitcast_fusion.5), channel_id=1, source_target_pairs={{0,8},{8,0},{16,24},{24,16},{1,9},{9,1},{17,25},{25,17},{2,10},{10... | collective-permute-start | bytes 1572872 | tf_op jit(solution)/shard_map/ppermute | solution.py:201
  517.1 24.4 %collective-permute-start.52 = (bf16[2,2,32,2048]{3,2,0,1:T(8,128)(2,1)S(1)}, bf16[2,2,32,2048]{3,2,0,1:T(8,128)(2,1)S(1)}, u32[]{:S(2)}, u32[]{:S(2)}) collective-permute-start(bf16[2,2,32,2048]{3,2,0,1:T(8,128)(2,1)S(1)} %dynamic-slice_bitcast_fusion.8), channel_id=1, source_target_pairs={{0,16},{8,24},{16,0},{24,8},{1,17},{9,25},{17,1},{25,9},{2,18},{10... | collective-permute-start | bytes 1572872 | tf_op jit(solution)/shard_map/ppermute | solution.py:201
  520.3 21.4 %collective-permute-start.57 = (bf16[2,2,32,2048]{3,2,0,1:T(8,128)(2,1)S(1)}, bf16[2,2,32,2048]{3,2,0,1:T(8,128)(2,1)S(1)}, u32[]{:S(2)}, u32[]{:S(2)}) collective-permute-start(bf16[2,2,32,2048]{3,2,0,1:T(8,128)(2,1)S(1)} %dynamic-slice_bitcast_fusion.7), channel_id=1, source_target_pairs={{0,8},{8,0},{16,24},{24,16},{1,9},{9,1},{17,25},{25,17},{2,10},{10... | collective-permute-start | bytes 1572872 | tf_op jit(solution)/shard_map/ppermute | solution.py:201
  (112 other events, 1087.2 us)
Sparse Core Ops, SparseCore 0:
  11.6 100.7 all-gather.2
  116.0 80.1 all-gather.4

commit v2 on v1

--- a/solution.py
+++ b/solution.py
@@ -29,11 +29,12 @@
     return inverse * (scaled - jnp.mean(scaled, axis=-1, keepdims=True) - normed * inner)
 
 
+def normal_share(hidden):
+    return 0.5 * (1.0 + lax.erf(hidden * 0.7071067811865476))
+
+
 def gelu_slope(hidden):
-    return (
-        0.5 * (1.0 + lax.erf(hidden * 0.7071067811865476))
-        + hidden * jnp.exp(-0.5 * hidden * hidden) * 0.3989422804014327
-    )
+    return normal_share(hidden) + hidden * jnp.exp(-0.5 * hidden * hidden) * 0.3989422804014327
 
 
 def adam_update(param, grad, moment, squares, decay):
@@ -207,30 +208,21 @@
     return [(axis, 1 << b, size, (mine >> b) & 1) for b in reversed(range(count))]
 
 
-def gather_bits(value, bits, order):
-    held = []
-    for place in order:
-        axis, mask, size, bit = bits[place]
-        other = swap(value, axis, mask, size)
-        at = sum(1 for h in held if h < place)
-        low = jnp.where(bit == 1, other, value)
-        high = jnp.where(bit == 1, value, other)
-        value = jnp.stack([low, high], axis=at)
-        held.append(place)
-    return value
-
-
-def scatter_bits(value, bits, order, last=F32, wire=BF16):
-    left = list(range(len(bits)))
-    for place in order:
-        axis, mask, size, bit = bits[place]
-        at = left.index(place)
-        away = lax.dynamic_index_in_dim(value, 1 - bit, at, keepdims=False).astype(wire)
-        keep = lax.dynamic_index_in_dim(value, bit, at, keepdims=False)
-        left.remove(place)
-        value = keep.astype(F32) + swap(away, axis, mask, size).astype(F32)
-        value = value.astype(wire if left else last)
-    return value
+def split(value, bit, at):
+    keep = lax.dynamic_index_in_dim(value, bit, at, keepdims=False)
+    away = lax.dynamic_index_in_dim(value, 1 - bit, at, keepdims=False)
+    return keep, away
+
+
+def add(*values, dtype=BF16):
+    total = values[0].astype(F32)
+    for value in values[1:]:
+        total = total + value.astype(F32)
+    return total.astype(dtype)
+
+
+def hold(value, *others):
+    return lax.optimization_barrier((value,) + others)[0]
 
 
 def in_number_order(pieces, mine):
@@ -252,6 +244,29 @@
     for mask in masks:
         held.update({r ^ mask: swap(piece, axis, mask, size) for r, piece in list(held.items())})
     return held
+
+
+def gather_direct(value, axis, size, step=1):
+    mine = lax.axis_index(axis) // step
+    pieces = [value] + [swap(value, axis, r, size) for r in range(step, size, step)]
+    return jnp.stack(in_number_order(pieces, mine))
+
+
+def gather_core(value, size, at):
+    other = swap(value, "shard", 1, size)
+    bit = lax.axis_index("shard") & 1
+    low = jnp.where(bit == 1, other, value)
+    high = jnp.where(bit == 1, value, other)
+    return jnp.stack([low, high], axis=at)
+
+
+def scatter_direct(value, axis, size, step=1):
+    mine = lax.axis_index(axis) // step
+    parts = [lax.dynamic_index_in_dim(value, mine, 0, keepdims=False)]
+    for r in range(1, size // step):
+        away = lax.dynamic_index_in_dim(value, mine ^ r, 0, keepdims=False)
+        parts.append(swap(away, axis, r * step, size))
+    return parts
 
 
 def body(
@@ -309,68 +324,71 @@
         squares_hidden,
     )
     devices = seqs * shards
+    far = shards // 2
     mine = lax.axis_index("seq")
-    seq_bits = bits_of("seq", seqs)
-    shard_bits = bits_of("shard", shards)
-    bits = seq_bits + shard_bits
-    ks, kh = len(seq_bits), len(shard_bits)
-    core = ks + kh - 1
-    far = [place for place in reversed(range(ks, core))]
-    one_way = [core] + list(reversed(range(ks))) + far
-    other_way = [core] + list(range(ks)) + far
+    core = lax.axis_index("shard") & 1
+    masks = [1 << b for b in range(seqs.bit_length() - 1)]
     tokens = layer_input[0]
     count, width = tokens.shape
+    half = count // 2
     local = width // seqs
     pairs = local // 128
     hidden_width = bias_hidden.shape[0] * devices
     part = norm_gains.shape[1]
 
+    by_heads = weight_qkv.astype(BF16).reshape(-1, 3, seqs, local)
+    by_heads = by_heads.transpose(2, 0, 1, 3).reshape(seqs, -1, 3 * local)
+    own_qkv = jnp.stack(in_number_order(scatter_direct(by_heads, "seq", seqs), mine))
+
+    upper = gather_blocks(tokens[:half], "seq", seqs, masks)
+    lower = gather_blocks(tokens[half:], "seq", seqs, masks[::-1])
+
+    each = own_qkv.shape[0] * own_qkv.shape[1]
+    own_bias = all_biases[1:3].astype(BF16).reshape(1, 2 * part)
+    own_qkv = jnp.concatenate(
+        [
+            own_qkv.reshape(each, 3 * local),
+            jnp.pad(own_bias, ((0, 7), (0, 3 * local - 2 * part))),
+        ],
+        axis=0,
+    )
+    own_qkv = gather_direct(own_qkv, "shard", shards, 2)
+    own_qkv = gather_core(own_qkv, shards, 1)
+    own_bias = own_qkv[:, :, each, : 2 * part].astype(F32).reshape(shards, 2, part)
+    own_bias = own_bias.transpose(1, 0, 2).reshape(2, local)
+    own_qkv = own_qkv[:, :, :each].reshape(far, 2, seqs, -1, 3 * local)
+    own_qkv = own_qkv.transpose(2, 0, 1, 3, 4).reshape(width, 3 * local)
+
+    deep = weight_expand.shape[0]
     small = jnp.concatenate(
         [
             norm_gains.astype(BF16).reshape(-1),
             all_biases.astype(BF16).reshape(-1),
             bias_hidden.astype(BF16),
         ]
-    )
-    small = gather_bits(small[None], bits, list(range(len(bits))))
-    small = small.reshape(devices, 8 * part + bias_hidden.shape[0]).astype(F32)
+    ).reshape(deep, -1)
+    thin = small.shape[1]
+    mixed = jnp.concatenate(
+        [
+            weight_expand.astype(BF16),
+            weight_merge.astype(BF16),
+            jnp.pad(small, ((0, 0), (0, 128 - thin))),
+        ],
+        axis=1,
+    )
+    mixed = lax.all_gather(mixed, ("seq", "shard"), axis=0, tiled=True)
+    full_expand = mixed[:, :hidden_width]
+    full_merge = mixed[:, hidden_width : hidden_width + width]
+    small = mixed[:, hidden_width + width :][:, :thin].reshape(devices, -1).astype(F32)
     rows = small[:, : 8 * part].reshape(devices, 8, part).transpose(1, 0, 2).reshape(8, width)
     gains, biases = rows[:2], rows[2:]
     hidden_bias = small[:, 8 * part :].reshape(hidden_width)
 
-    by_heads = weight_qkv.astype(BF16).reshape(-1, 3, seqs, local)
-    columns = [
-        swap(lax.dynamic_index_in_dim(by_heads, mine ^ r, 2, keepdims=False), "seq", r, seqs)
-        if r
-        else lax.dynamic_index_in_dim(by_heads, mine, 2, keepdims=False)
-        for r in range(seqs)
-    ]
-    columns = jnp.stack(in_number_order(columns, mine))
-    columns = columns.reshape(seqs, -1, 3 * local)
-    for place in range(kh):
-        axis, mask, size, bit = shard_bits[place]
-        other = swap(columns, axis, mask, size)
-        columns = jnp.stack(
-            [jnp.where(bit == 1, other, columns), jnp.where(bit == 1, columns, other)],
-            axis=1 + place,
-        )
-    own_qkv = columns.reshape(width, 3 * local)
-
-    half = count // 2
-    masks = [1 << b for b in range(ks)]
-    upper = gather_blocks(tokens[:half], "seq", seqs, masks)
-    lower = gather_blocks(tokens[half:], "seq", seqs, masks[::-1])
     every = jnp.concatenate(
         [piece for r in range(seqs) for piece in (upper[r], lower[r])], axis=0
     )
-
-    full_merge = gather_bits(
-        weight_merge.astype(BF16), bits, list(range(ks, core)) + list(range(ks)) + [core]
-    ).reshape(width, width)
-    full_expand = lax.all_gather(weight_expand.astype(BF16), ("seq", "shard"), axis=0, tiled=True)
     full_shrink = lax.all_gather(weight_shrink.astype(BF16), ("seq", "shard"), axis=0, tiled=True)
 
-    own_bias = lax.dynamic_slice_in_dim(biases[1:3], mine * local, local, 1)
     bias_row = jnp.concatenate([own_bias[0], jnp.zeros((local,), F32), own_bias[1]])
     qkv = (jnp.dot(every, own_qkv, preferred_element_type=F32) + bias_row).astype(BF16)
     query, keys, values = qkv[:, :local], qkv[:, local : 2 * local], qkv[:, 2 * local :]
@@ -402,7 +420,7 @@
     )
     first_low = first.astype(BF16)
     hidden = jnp.dot(first_low, full_expand, preferred_element_type=F32) + hidden_bias
-    active = jax.nn.gelu(hidden, approximate=False).astype(BF16)
+    active = (hidden * normal_share(hidden)).astype(BF16)
     branch = jnp.dot(active, full_shrink, preferred_element_type=F32) + biases[5]
     result, normed_two, inverse_two = norm_forward(first + branch, gains[1], biases[4])
     grad_out = cotangent[0]
@@ -412,20 +430,41 @@
     grad_branch = grad_mid.astype(BF16)
     grad_shrink_bias = jnp.sum(grad_branch, axis=0, dtype=F32)
 
-    def summed_weight(left, right):
-        middle = right.shape[1] // 2
-        parts = []
-        for piece, order in ((right[:, :middle], one_way), (right[:, middle:], other_way)):
-            grad = lax.dot_general(left, piece, TN, preferred_element_type=F32).astype(BF16)
-            grad = grad.reshape((2,) * len(bits) + (-1, middle))
-            parts.append(scatter_bits(grad, bits, order))
-        return jnp.concatenate(parts, axis=1)
-
-    summed_shrink = summed_weight(active, grad_branch)
+    def core_step(left, right, extra=None):
+        grad = lax.dot_general(left, right, TN, preferred_element_type=F32).astype(BF16)
+        grad = grad.reshape(seqs, far, 2, -1, grad.shape[1])
+        if extra is not None:
+            grad = jnp.concatenate([grad, extra], axis=-1)
+        keep, away = split(grad, core, 2)
+        return keep, swap(away, "shard", 1, shards), away
+
+    def halving_start(grad, way):
+        grad = grad.reshape((2,) * len(masks) + grad.shape[1:])
+        return halving_send(grad, masks[::-1], way)
+
+    def halving_send(grad, left, way):
+        mask = way[0]
+        keep, away = split(grad, (mine // mask) & 1, left.index(mask))
+        left = [m for m in left if m != mask]
+        return keep, swap(away, "seq", mask, seqs), away, left, way[1:]
+
+    def halving_next(started, *others):
+        if not isinstance(started, tuple):
+            return started
+        keep, got, _, left, way = started
+        grad = add(keep, hold(got, *others))
+        return halving_send(grad, left, way) if way else grad
+
+    grad_shrink = lax.dot_general(active, grad_branch, TN, preferred_element_type=F32).astype(BF16)
+    summed_shrink = lax.psum_scatter(
+        grad_shrink, ("seq", "shard"), scatter_dimension=0, tiled=True
+    ).astype(F32)
+    grad_branch = hold(grad_branch, grad_shrink)
     grad_active = lax.dot_general(grad_branch, full_shrink, NT, preferred_element_type=F32)
     grad_hidden = (grad_active * gelu_slope(hidden)).astype(BF16)
     grad_hidden_bias = jnp.sum(grad_hidden, axis=0, dtype=F32)
-    summed_expand = summed_weight(first_low, grad_hidden)
+    expand_keep, expand_got, away = core_step(first_low, grad_hidden)
+    grad_hidden = hold(grad_hidden, away)
     grad_first = grad_mid + lax.dot_general(
         grad_hidden, full_expand, NT, preferred_element_type=F32
     )
@@ -437,17 +476,8 @@
     grad_heads = lax.dot_general(
         grad_attended, full_merge, NT, preferred_element_type=F32
     ).astype(BF16)
-    grad_context = jnp.concatenate(
-        [
-            swap(lax.dynamic_slice_in_dim(grad_heads, (mine ^ r) * local, local, 1), "seq", r, seqs)
-            if r
-            else lax.dynamic_slice_in_dim(grad_heads, mine * local, local, 1)
-            for r in range(seqs)
-        ],
-        axis=0,
-    )
-    summed_merge = summed_weight(context, grad_attended)
-
+    grad_heads = grad_heads.reshape(count, seqs, local).transpose(1, 0, 2)
+    grad_context = jnp.concatenate(scatter_direct(grad_heads, "seq", seqs), axis=0)
     small_grads = jnp.concatenate(
         [
             jnp.stack(
@@ -467,42 +497,55 @@
         ],
         axis=1,
     )
-    small_grads = scatter_bits(
-        small_grads.reshape((2,) * len(bits) + (1, -1)), bits, list(range(len(bits))), F32, F32
-    )[0]
-
-    grads = [
-        attend_backward(
-            query, keys, values, contexts[pair], grad_context, totals[pair], pair, block
-        )
-        for pair in range(pairs)
+    small_grads = small_grads.astype(BF16).reshape(seqs, far, 2, deep, -1)
+    slim = small_grads.shape[-1]
+    small_grads = jnp.pad(small_grads, ((0, 0),) * 4 + ((0, 128 - slim),))
+    merge_keep, merge_got, away = core_step(context, grad_attended, small_grads)
+
+    expand = add(expand_keep, hold(expand_got, grad_context))
+    middle = expand.shape[-1] // 2
+    expand = [
+        halving_start(expand[..., :middle], masks),
+        halving_start(expand[..., middle:], masks[::-1]),
     ]
+    grad_context = hold(grad_context, away, *[part[2] for part in expand])
+
+    grads = []
+    for pair in range(pairs):
+        grads.append(
+            attend_backward(
+                query, keys, values, contexts[pair], grad_context, totals[pair], pair, block
+            )
+        )
+        if pair == 0:
+            merge = halving_start(add(merge_keep, hold(merge_got, grads[0][0])), masks)
+            expand = [halving_next(part, grads[0][0]) for part in expand]
+            grad_context = hold(grad_context, merge[2], *[part[2] for part in expand])
+    last = grads[-1][0]
+    while isinstance(merge, tuple):
+        merge = halving_next(merge, last)
+        expand = [halving_next(part, last) for part in expand]
     grad_rows = jnp.concatenate(
         [grads[pair][which] for which in range(3) for pair in range(pairs)], axis=1
     )
-    grad_weight = lax.dot_general(every, grad_rows, TN, preferred_element_type=F32).astype(BF16)
-    grad_weight = grad_weight.reshape((seqs,) + (2,) * kh + (-1, 3 * local))
-    for turn, place in enumerate(reversed(range(kh))):
-        axis, mask, size, bit = shard_bits[place]
-        away = lax.dynamic_index_in_dim(grad_weight, 1 - bit, 1 + place, keepdims=False)
-        keep = lax.dynamic_index_in_dim(grad_weight, bit, 1 + place, keepdims=False)
-        grad_weight = (
-            keep.astype(F32) + swap(away, axis, mask, size).astype(F32)
-        ).astype(BF16)
-    summed_qkv = in_number_order(
-        [
-            swap(lax.dynamic_index_in_dim(grad_weight, mine ^ r, 0, keepdims=False), "seq", r, seqs)
-            if r
-            else lax.dynamic_index_in_dim(grad_weight, mine, 0, keepdims=False)
-            for r in range(seqs)
-        ],
-        mine,
-    )
-    summed_qkv = (
-        jnp.stack([piece.reshape(-1, 3, local) for piece in summed_qkv], axis=2)
-        .reshape(-1, 3 * width)
-        .astype(F32)
-    )
+
+    spread = lax.dot_general(grad_rows, own_qkv, NT, preferred_element_type=F32).astype(BF16)
+    spread = spread.reshape((2,) * len(masks) + (2, half, width))
+    sides = []
+    for side, way in ((0, masks), (1, masks[::-1])):
+        held = lax.index_in_dim(spread, side, len(masks), keepdims=False)
+        left = masks[::-1]
+        for mask in way:
+            at = left.index(mask)
+            left = [m for m in left if m != mask]
+            held = add(
+                lax.index_in_dim(held, 0, at, keepdims=False),
+                swap(lax.index_in_dim(held, 1, at, keepdims=False), "seq", mask, seqs),
+                dtype=BF16 if left else F32,
+            )
+        sides.append(held)
+    grad_input = grad_residual + jnp.concatenate(sides, axis=0)
+
     head_sums = jnp.stack(
         [
             jnp.sum(grad_rows[:, :local], axis=0, dtype=F32).reshape(shards, part),
@@ -510,14 +553,27 @@
         ],
         axis=1,
     )
-    head_sums = scatter_bits(
-        head_sums.reshape((2,) * kh + (2, part)), shard_bits, list(range(kh)), F32, F32
-    )
-    spread = lax.dot_general(grad_rows, own_qkv, NT, preferred_element_type=F32)
-    grad_input = grad_residual + spread[:count]
-    for r in range(1, seqs):
-        away = spread[r * count : (r + 1) * count].astype(BF16)
-        grad_input = grad_input + swap(away, "seq", r, seqs).astype(F32)
+    head_sums = head_sums.astype(BF16).reshape(1, far, 2, deep, 2)
+    head_sums = jnp.broadcast_to(
+        jnp.pad(head_sums, ((0, 0),) * 4 + ((0, 126),)), (seqs, far, 2, deep, 128)
+    )
+    keep, got, _ = core_step(every, grad_rows, head_sums)
+    grad_weight = add(keep, got).transpose(1, 0, 2, 3)
+    grad_weight = add(*scatter_direct(grad_weight, "shard", shards, 2))
+    arrived = scatter_direct(grad_weight, "seq", seqs)
+    head_sums = arrived[0][:, 3 * local : 3 * local + 2].astype(F32).reshape(2, part)
+    summed_qkv = in_number_order([piece[:, : 3 * local] for piece in arrived], mine)
+    summed_qkv = (
+        jnp.stack([piece.reshape(-1, 3, local) for piece in summed_qkv], axis=2)
+        .reshape(-1, 3 * width)
+        .astype(F32)
+    )
+
+    others = jnp.concatenate(expand + [merge], axis=-1)
+    others = add(*scatter_direct(others, "shard", shards, 2), dtype=F32)
+    summed_expand = others[:, :hidden_width]
+    summed_merge = others[:, hidden_width : hidden_width + width]
+    small_grads = others[:, hidden_width + width :][:, :slim].reshape(-1)
 
     small_rows = small_grads[: 6 * part].reshape(6, part)
     summed = (

time: 586 us -> 484 us (0.83)
  waiting for transfers between devices: 217 us -> 123 us
  starting transfers between devices: 78.9 us -> 57.1 us
  other arithmetic: 45.4 us -> 65 us
  matrix products: 93.8 us -> 80 us
  local copies, waits for them, and re-layouts: 52.2 us -> 58.7 us
    ppermute x78 -> x44, waiting for transfers between devices: 216 us -> 78.7 us  [swap(): return lax.ppermute(value, axis, [(i, i ^ mask) for i in range(size)])]
    all_gather x1, waiting for transfers between devices: 0.83 us -> 44.5 us  [body(): lax.all_gather(weight_shrink.astype(BF16), ('seq', 'shard'), axis=0, tile...]
    dynamic_slice x17 -> x0, local copies, waits for them, and re-layouts: 22.8 us -> none  [the longest x6 11.1 us: scatter_bits(): keep = lax.dynamic_index_in_dim(value, bit, at, keepdims=False)]
    ppermute x78 -> x44, starting transfers between devices: 78.8 us -> 57 us  [swap(): return lax.ppermute(value, axis, [(i, i ^ mask) for i in range(size)])]
    dot_general x1, matrix products: 27.9 us -> 8.16 us  [body(): jnp.dot(first_low, full_expand, preferred_element_type=F32) + hidden_bias]
    unnamed x143 -> x141, local copies, waits for them, and re-layouts: 19.2 us -> 29.2 us
    squeeze x34 -> x19, local copies, waits for them, and re-layouts: 1.09 us -> 10.9 us  [the longest x8 6.47 us: split(): away = lax.dynamic_index_in_dim(value, 1 - bit, at, keepdims=False)]
    another operation x25 -> x8, other arithmetic: 1.99 us -> 8.65 us  [the longest x2 4.79 us: gather_core(): return jnp.stack([low, high], axis=at)]
  transfers between devices with their start and end apart: 80 -> 47, of which waited for: 40 -> 17; matrix products, arithmetic and copies ran while one was open for 21% -> 30% of each run, Pallas kernels for 13% -> 16%
where the time goes in v2:
time: 484 us; the launch traced here: 476 us
  waiting for transfers between devices  123 us (25%)
  matrix products  80 us (17%)
  Pallas kernels  77.1 us (16%)
  other arithmetic  65 us (13%)
  local copies, waits for them, and re-layouts  58.7 us (12%)
  starting transfers between devices  57.1 us (12%)
  between operations  15.4 us (3%)
    ppermute x44, waiting for transfers between devices, swap(): return lax.ppermute(value, axis, [(i, i ^ mask) for i in range(size)])  78.7 us
    ppermute x44, starting transfers between devices, swap(): return lax.ppermute(value, axis, [(i, i ^ mask) for i in range(size)])  57 us
    pallas_call x2, Pallas kernels, attend_backward(): pl.pallas_call(backward_kernel, grid=(length // block,), in_specs=[whole,...  47.6 us
    all_gather x1, waiting for transfers between devices, body(): lax.all_gather(weight_shrink.astype(BF16), ('seq', 'shard'), axis=0, tile...  44.5 us
    pallas_call x2, Pallas kernels, attend_forward(): pl.pallas_call(forward_kernel, grid=(length // block,), in_specs=[pl.Bloc...  29.4 us
    unnamed x141, local copies, waits for them, and re-layouts  29.2 us
    convert_element_type x12, other arithmetic, add(): return total.astype(dtype)  16.3 us
    dot_general x3, matrix products, core_step(): lax.dot_general(left, right, TN, preferred_element_type=F32).astype(BF16)  15.6 us
  transfers between devices with their start and end apart: 47, of which 17 were waited for; matrix products, arithmetic and copies ran while one was open for 30% of the time, Pallas kernels for 16%

profile of v2, /device:TPU:0, one launch (start us, length us, event | category | flops | bytes accessed | tf_op | source)
XLA Modules:
  0.0 476.4 jit_solution(5798390451864486633)
XLA Ops:
  14.0 4.0 collective-permute-start.6
  28.5 18.5 %collective-permute-done.10 = bf16[136,768]{1,0:T(8,128)(2,1)S(1)} collective-permute-done((bf16[136,768]{1,0:T(8,128)(2,1)S(1)}, bf16[136,768]{1,0:T(8,128)(2,1)S(1)}, u32[]{:S(2)}, u32[]{:S(2)}) %collective-permute-start.10) | collective-permute-done | bytes 208928 | tf_op jit(solution)/shard_map/ppermute | solution.py:202
  50.2 2.8 pad_maximum_fusion.2
  55.2 8.1 %collective-permute-done.3 = bf16[256,1024]{1,0:T(8,128)(2,1)} collective-permute-done((bf16[256,1024]{1,0:T(8,128)(2,1)}, bf16[256,1024]{1,0:T(8,128)(2,1)}, u32[]{:S(2)}, u32[]{:S(2)}) %collective-permute-start.3) | collective-permute-done | bytes 524320 | tf_op jit(solution)/shard_map/ppermute | solution.py:202
  76.7 3.6 select_bitcast_fusion
  82.2 6.2 %add_convert_fusion = bf16[2048,768]{1,0:T(8,128)(2,1)S(1)} fusion(bf16[2048,1024]{1,0:T(8,128)(2,1)} %constant_dynamic-update-slice_fusion, bf16[1024,768]{1,0:T(8,128)(2,1)S(1)} %bitcast.251, f32[768]{0:T(1024)S(1)} %pad_maximum_fusion.5), kind=kOutput, calls=%fused_computation.17 | convolution fusion | flops 3224371200 | bytes 8915968 | tf_op jit(solution)/shard_map/dot_general | solution.py:393
  88.6 14.6 %attend_forward.2 = (bf16[2048,128]{1,0:T(8,128)(2,1)S(1)}, f32[1,2,2048]{2,1,0:T(2,128)S(1)}) custom-call(bf16[2048,256]{1,0:T(8,128)(2,1)S(1)} %get-tuple-element.125.q_ref, bf16[2048,256]{1,0:T(8,128)(2,1)S(1)} %get-tuple-element.124.k_ref, bf16[2048,256]{1,0:T(8,128)(2,1)S(1)} %get-tuple-element.123.v_ref), custom_call_target="tpu_custom_call" | custom-call | flops 8589934592 | bytes 2097152 | tf_op jit(solution)/shard_map/attend_forward/pallas_call | solution.py:81
  106.8 14.8 %attend_forward.3 = (bf16[2048,128]{1,0:T(8,128)(2,1)S(1)}, f32[1,2,2048]{2,1,0:T(2,128)S(1)}) custom-call(bf16[2048,256]{1,0:T(8,128)(2,1)S(1)} %get-tuple-element.125.q_ref, bf16[2048,256]{1,0:T(8,128)(2,1)S(1)} %get-tuple-element.124.k_ref, bf16[2048,256]{1,0:T(8,128)(2,1)S(1)} %get-tuple-element.123.v_ref), custom_call_target="tpu_custom_call" | custom-call | flops 8589934592 | bytes 2097152 | tf_op jit(solution)/shard_map/attend_forward/pallas_call | solution.py:81
  138.0 3.4 fusion.80
  143.8 8.2 %multiply_convert_fusion = (bf16[512,4096]{1,0:T(8,128)(2,1)}, f32[512,4096]{1,0:T(8,128)}) fusion(f32[4096]{0:T(1024)S(1)} %slice_bitcast_fusion.10, bf16[1024,5248]{1,0:T(8,128)(2,1)S(1)} %copy-done.50, f32[512,1024]{1,0:T(8,128)S(1)} %get-tuple-element.167, f32[1024]{0:T(1024)S(1)} %add.352, f32[1024]{0:T(1024)S(1)} %mul.384, ...), kind=kOutput, calls=%fused_computation.9 | convolution fusion | flops 4310171648 | bytes 23097344 | tf_op jit(solution)/shard_map/dot_general | solution.py:422
  151.9 44.5 %all-gather.5.cloned.1.call-done = bf16[4096,1024]{1,0:T(8,128)(2,1)} async-done(((bf16[128,1024]{1,0:T(8,128)(2,1)}), bf16[4096,1024]{1,0:T(8,128)(2,1)}) %all-gather.5.cloned.1.call-update) | async-done | bytes 8388624 | tf_op jit(solution)/shard_map/all_gather | solution.py:390
  196.4 9.9 %fusion.81 = (f32[512]{0:T(512)S(1)}, f32[512,1024]{1,0:T(8,128)S(1)}) fusion(f32[1024]{0:T(1024)S(1)} %add.359, bf16[512,4096]{1,0:T(8,128)(2,1)} %get-tuple-element.168, bf16[4096,1024]{1,0:T(8,128)(2,1)} %all-gather.5.cloned.1.call-done, f32[1024]{0:T(1024)S(1)} %add.352, f32[1024]{0:T(1024)S(1)} %mul.384, f32[512]{0:T(512)S(1)} %add_rsqrt_fusion.1, ...), kind=kOutput, calls=%fused_computation.275 | convolution fusion | flops 4298636800 | bytes 16795648 | tf_op jit(solution)/shard_map/dot_general | solution.py:424
  208.1 4.0 fusion.19
  215.1 6.7 %convolution_convert_fusion.1 = bf16[4096,1024]{1,0:T(8,128)(2,1)} fusion(bf16[512,4096]{1,0:T(8,128)(2,1)S(1)} %copy-done.58, bf16[512,1024]{1,0:T(8,128)(2,1)S(1)} %get-tuple-element.54), kind=kOutput, calls=%fused_computation.12 | convolution fusion | flops 4299161600 | bytes 13631488 | tf_op jit(solution)/shard_map/dot_general | solution.py:458
  221.8 10.9 %fusion.82 = (bf16[4096]{0:T(1024)(128)(2,1)S(1)}, bf16[512,4096]{1,0:T(8,128)(2,1)S(1)}) fusion(f32[512,4096]{1,0:T(8,128)} %get-tuple-element.169, f32[4096]{0:T(1024)S(1)} %slice_bitcast_fusion.10, bf16[512,1024]{1,0:T(8,128)(2,1)S(1)} %get-tuple-element.54, bf16[4096,1024]{1,0:T(8,128)(2,1)} %all-gather.5.cloned.1.call-done), kind=kOutput, calls=%fused_computation.276 | convolution fusion | flops 4320129024 | bytes 22044672 | tf_op jit(solution)/shard_map/dot_general | solution.py:463
  232.7 5.5 %convolution_convert_fusion = bf16[1024,4096]{1,0:T(8,128)(2,1)S(1)} fusion(bf16[512,4096]{1,0:T(8,128)(2,1)S(1)} %get-tuple-element.55, f32[512,1024]{1,0:T(8,128)S(1)} %copy-done.16, f32[1024]{0:T(1024)S(1)} %add.352, f32[1024]{0:T(1024)S(1)} %mul.384, f32[512]{0:T(512)S(1)} %add_rsqrt_fusion.1, f32[512]{0:T(512)S(1)} %broadcast_multiply_fusion.5), kind=kOutput, calls=%fused_computation.11 | convolution fusion | flops 4301783040 | bytes 14692352 | tf_op jit(solution)/shard_map/dot_general | solution.py:434
  243.1 11.2 %multiply_reduce_fusion = (bf16[1024]{0:T(1024)(128)(2,1)S(1)}, f32[512]{0:T(512)S(1)}, f32[512]{0:T(512)S(1)}, bf16[1024]{0:T(1024)(128)(2,1)S(1)}, f32[512,1024]{1,0:T(8,128)S(1)}) fusion(f32[512,1024]{1,0:T(8,128)} %copy-done.15, f32[512]{0:T(512)S(1)} %add_rsqrt_fusion.1, f32[512]{0:T(512)S(1)} %broadcast_multiply_fusion.5, f32[1024]{0:T(1024)S(1)} %mul.384, ...), kind=kOutput, calls=%fused_computation.42 | convolution fusion | flops 4300207104 | bytes 18890752 | tf_op jit(solution)/shard_map/dot_general | solution.py:468
  256.4 4.0 fusion.31
  269.7 3.2 convolution_convert_fusion.3
  276.1 8.3 %collective-permute-done.20 = bf16[512,256]{1,0:T(8,128)(2,1)} collective-permute-done((bf16[512,256]{1,0:T(8,128)(2,1)S(1)}, bf16[512,256]{1,0:T(8,128)(2,1)}, u32[]{:S(2)}, u32[]{:S(2)}) %collective-permute-start.20) | collective-permute-done | bytes 262176 | tf_op jit(solution)/shard_map/ppermute | solution.py:202
  286.5 5.1 %fusion.6 = bf16[4,4,32,4096]{3,2,1,0:T(8,128)(2,1)S(1)} fusion(bf16[4,4,32,4096]{3,2,1,0:T(8,128)(2,1)} %collective-permute-done.22, bf16[4,4,2,32,4096]{4,3,2,1,0:T(8,128)(2,1)} %bitcast.235, s32[]{:T(128)S(6)} %select_n.334), kind=kLoop, calls=%fused_computation.8 | loop fusion | flops 8388608 | bytes 12582916 | tf_op jit(solution)/shard_map/convert_element_type | solution.py:221
  296.3 23.7 %attend_backward.2 = (bf16[2048,128]{1,0:T(8,128)(2,1)S(1)}, bf16[2048,128]{1,0:T(8,128)(2,1)S(1)}, bf16[2048,128]{1,0:T(8,128)(2,1)S(1)}) custom-call(bf16[2048,256]{1,0:T(8,128)(2,1)S(1)} %copy-done.3, bf16[2048,256]{1,0:T(8,128)(2,1)S(1)} %copy-done.1, bf16[2048,256]{1,0:T(8,128)(2,1)S(1)} %get-tuple-element.123.v_ref, ...), custom_call_target="tpu_custom_call" | custom-call | flops 21474836480 | bytes 5242880 | tf_op jit(solution)/shard_map/attend_backward/pallas_call | solution.py:177
  321.7 4.7 collective-permute-done.25
  337.1 23.9 %attend_backward.3 = (bf16[2048,128]{1,0:T(8,128)(2,1)S(1)}, bf16[2048,128]{1,0:T(8,128)(2,1)S(1)}, bf16[2048,128]{1,0:T(8,128)(2,1)S(1)}) custom-call(bf16[2048,256]{1,0:T(8,128)(2,1)S(1)} %copy-done.3, bf16[2048,256]{1,0:T(8,128)(2,1)S(1)} %copy-done.1, bf16[2048,256]{1,0:T(8,128)(2,1)S(1)} %get-tuple-element.123.v_ref, ...), custom_call_target="tpu_custom_call" | custom-call | flops 21474836480 | bytes 5242880 | tf_op jit(solution)/shard_map/attend_backward/pallas_call | solution.py:177
  370.9 6.8 %convolution_convert_fusion.4 = bf16[1024,768]{1,0:T(8,128)(2,1)S(1)} fusion(bf16[2048,1024]{1,0:T(8,128)(2,1)} %constant_dynamic-update-slice_fusion, bf16[2048,768]{1,0:T(8,128)(2,1)} %constant_dynamic-update-slice_fusion.14), kind=kOutput, calls=%fused_computation.66 | convolution fusion | flops 3222011904 | bytes 8912896 | tf_op jit(solution)/shard_map/dot_general | solution.py:434
  380.0 4.0 convolution_convert_fusion.2
  389.9 3.7 collective-permute-start.43
  395.9 8.3 %collective-permute-done.41 = bf16[32,5248]{1,0:T(8,128)(2,1)S(1)} collective-permute-done((bf16[32,5248]{1,0:T(8,128)(2,1)S(1)}, bf16[32,5248]{1,0:T(8,128)(2,1)S(1)}, u32[]{:S(2)}, u32[]{:S(2)}) %collective-permute-start.41) | collective-permute-done | bytes 335904 | tf_op jit(solution)/shard_map/ppermute | solution.py:202
  405.8 9.6 %collective-permute-done.42 = bf16[32,5248]{1,0:T(8,128)(2,1)S(1)} collective-permute-done((bf16[32,5248]{1,0:T(8,128)(2,1)S(1)}, bf16[32,5248]{1,0:T(8,128)(2,1)S(1)}, u32[]{:S(2)}, u32[]{:S(2)}) %collective-permute-start.42) | collective-permute-done | bytes 335904 | tf_op jit(solution)/shard_map/ppermute | solution.py:202
  419.0 2.8 multiply_subtract_fusion.1
  426.8 7.4 %collective-permute-start.31 = (bf16[4,32,896]{2,1,0:T(8,128)(2,1)S(1)}, bf16[4,32,896]{2,1,0:T(8,128)(2,1)S(1)}, u32[]{:S(2)}, u32[]{:S(2)}) collective-permute-start(bf16[4,32,896]{2,1,0:T(8,128)(2,1)S(1)} %get-tuple-element.138), channel_id=1, source_target_pairs={{0,2},{1,3},{2,0},{3,1},{4,6},{5,7},{6,4},{7,5},{8,10},{9,11},{10,... | collective-permute-start | bytes 688136 | tf_op jit(solution)/shard_map/ppermute | solution.py:202
  443.4 10.1 %collective-permute-done.32 = bf16[4,32,896]{2,1,0:T(8,128)(2,1)S(1)} collective-permute-done((bf16[4,32,896]{2,1,0:T(8,128)(2,1)S(1)}, bf16[4,32,896]{2,1,0:T(8,128)(2,1)S(1)}, u32[]{:S(2)}, u32[]{:S(2)}) %collective-permute-start.32) | collective-permute-done | bytes 229408 | tf_op jit(solution)/shard_map/ppermute | solution.py:202
  (385 shorter events, 158.6 us)
Async XLA Ops:
  7.2 127.0 %all-gather.3.cloned.1.call-start = ((), (), s32[]{:S(2)}) async-start(), calls=%async_computation.1 | async-start | bytes 11083776 | tf_op jit(solution)/shard_map/all_gather | solution.py:379
  12.5 183.9 %all-gather.5.cloned.1.call-start = ((), (), s32[]{:S(2)}) async-start(), calls=%async_computation.2 | async-start | bytes 8650752 | tf_op jit(solution)/shard_map/all_gather | solution.py:390
  13.3 453.9 %reduce-scatter.2.cloned.1.call-start = ((), (), s32[]{:S(2)}) async-start(), calls=%async_computation.3 | async-start | bytes 8650752 | tf_op jit(solution)/shard_map/reduce_scatter | solution.py:459
  19.6 33.4 %collective-permute-start = (bf16[256,1024]{1,0:T(8,128)(2,1)}, bf16[256,1024]{1,0:T(8,128)(2,1)}, u32[]{:S(2)}, u32[]{:S(2)}) collective-permute-start(bf16[256,1024]{1,0:T(8,128)(2,1)} %get-tuple-element.137), channel_id=1, source_target_pairs={{0,8},{8,0},{16,24},{24,16},{1,9},{9,1},{17,25},{25,17},{2,10},{10... | collective-permute-start | bytes 1572872 | tf_op jit(solution)/shard_map/ppermute | solution.py:202
  21.5 48.2 %collective-permute-start.2 = (bf16[256,1024]{1,0:T(8,128)(2,1)}, bf16[256,1024]{1,0:T(8,128)(2,1)}, u32[]{:S(2)}, u32[]{:S(2)}) collective-permute-start(bf16[256,1024]{1,0:T(8,128)(2,1)} %get-tuple-element.137), channel_id=1, source_target_pairs={{0,16},{8,24},{16,0},{24,8},{1,17},{9,25},{17,1},{25,9},{2,18},{10... | collective-permute-start | bytes 1572872 | tf_op jit(solution)/shard_map/ppermute | solution.py:202
  23.2 23.8 %collective-permute-start.10 = (bf16[136,768]{1,0:T(8,128)(2,1)S(1)}, bf16[136,768]{1,0:T(8,128)(2,1)S(1)}, u32[]{:S(2)}, u32[]{:S(2)}) collective-permute-start(bf16[136,768]{1,0:T(8,128)(2,1)S(1)} %fusion.56), channel_id=1, source_target_pairs={{0,4},{1,5},{2,6},{3,7},{4,0},{5,1},{6,2},{7,3},{8,12},{9,13},{10,... | collective-permute-start | bytes 626696 | tf_op jit(solution)/shard_map/ppermute | solution.py:202
  25.9 21.7 %collective-permute-start.11 = (bf16[136,768]{1,0:T(8,128)(2,1)S(1)}, bf16[136,768]{1,0:T(8,128)(2,1)S(1)}, u32[]{:S(2)}, u32[]{:S(2)}) collective-permute-start(bf16[136,768]{1,0:T(8,128)(2,1)S(1)} %fusion.56), channel_id=1, source_target_pairs={{0,2},{1,3},{2,0},{3,1},{4,6},{5,7},{6,4},{7,5},{8,10},{9,11},{10,... | collective-permute-start | bytes 626696 | tf_op jit(solution)/shard_map/ppermute | solution.py:202
  27.4 21.1 %collective-permute-start.9 = (bf16[136,768]{1,0:T(8,128)(2,1)S(1)}, bf16[136,768]{1,0:T(8,128)(2,1)S(1)}, u32[]{:S(2)}, u32[]{:S(2)}) collective-permute-start(bf16[136,768]{1,0:T(8,128)(2,1)S(1)} %fusion.56), channel_id=1, source_target_pairs={{0,6},{1,7},{2,4},{3,5},{4,2},{5,3},{6,0},{7,1},{8,14},{9,15},{10,... | collective-permute-start | bytes 626696 | tf_op jit(solution)/shard_map/ppermute | solution.py:202
  47.0 20.8 %collective-permute-start.1 = (bf16[256,1024]{1,0:T(8,128)(2,1)}, bf16[256,1024]{1,0:T(8,128)(2,1)}, u32[]{:S(2)}, u32[]{:S(2)}) collective-permute-start(bf16[256,1024]{1,0:T(8,128)(2,1)} %get-tuple-element.136), channel_id=1, source_target_pairs={{0,8},{8,0},{16,24},{24,16},{1,9},{9,1},{17,25},{25,17},{2,10},{10... | collective-permute-start | bytes 1572872 | tf_op jit(solution)/shard_map/ppermute | solution.py:202
  53.0 23.6 %collective-permute-start.12 = (bf16[4,136,768]{2,0,1:T(4,128)(2,1)}, bf16[4,136,768]{2,0,1:T(4,128)(2,1)}, u32[]{:S(2)}, u32[]{:S(2)}) collective-permute-start(bf16[4,136,768]{2,0,1:T(4,128)(2,1)} %pad_maximum_fusion.2), channel_id=1, source_target_pairs={{0,1},{1,0},{2,3},{3,2},{4,5},{5,4},{6,7},{7,6},{8,9},{9,8},{10,11... | collective-permute-start | bytes 2506760 | tf_op jit(solution)/shard_map/ppermute | solution.py:202
  53.1 20.5 %collective-permute-start.4 = (bf16[256,1024]{1,0:T(8,128)(2,1)}, bf16[256,1024]{1,0:T(8,128)(2,1)}, u32[]{:S(2)}, u32[]{:S(2)}) collective-permute-start(bf16[256,1024]{1,0:T(8,128)(2,1)} %collective-permute-done), channel_id=1, source_target_pairs={{0,16},{8,24},{16,0},{24,8},{1,17},{9,25},{17,1},{25,9},{2,18},{10... | collective-permute-start | bytes 1572872 | tf_op jit(solution)/shard_map/ppermute | solution.py:202
  103.3 20.3 %collective-permute-start.13 = (bf16[512,128]{1,0:T(8,128)(2,1)S(1)}, bf16[512,128]{1,0:T(8,128)(2,1)S(1)}, u32[]{:S(2)}, u32[]{:S(2)}) collective-permute-start(bf16[512,128]{1,0:T(8,128)(2,1)S(1)} %get-tuple-element.150), channel_id=1, source_target_pairs={{0,24},{8,16},{16,8},{24,0},{1,25},{9,17},{17,9},{25,1},{2,26},{10... | collective-permute-start | bytes 393224 | tf_op jit(solution)/shard_map/ppermute | solution.py:202
  104.8 20.4 %collective-permute-start.14 = (bf16[512,128]{1,0:T(8,128)(2,1)S(1)}, bf16[512,128]{1,0:T(8,128)(2,1)S(1)}, u32[]{:S(2)}, u32[]{:S(2)}) collective-permute-start(bf16[512,128]{1,0:T(8,128)(2,1)S(1)} %get-tuple-element.149), channel_id=1, source_target_pairs={{0,16},{8,24},{16,0},{24,8},{1,17},{9,25},{17,1},{25,9},{2,18},{10... | collective-permute-start | bytes 393224 | tf_op jit(solution)/shard_map/ppermute | solution.py:202
  105.1 20.1 %collective-permute-start.15 = (bf16[512,128]{1,0:T(8,128)(2,1)S(1)}, bf16[512,128]{1,0:T(8,128)(2,1)S(1)}, u32[]{:S(2)}, u32[]{:S(2)}) collective-permute-start(bf16[512,128]{1,0:T(8,128)(2,1)S(1)} %get-tuple-element.148), channel_id=1, source_target_pairs={{0,8},{8,0},{16,24},{24,16},{1,9},{9,1},{17,25},{25,17},{2,10},{10... | collective-permute-start | bytes 393224 | tf_op jit(solution)/shard_map/ppermute | solution.py:202
  242.9 43.7 %collective-permute-start.22 = (bf16[4,4,32,4096]{3,2,1,0:T(8,128)(2,1)}, bf16[4,4,32,4096]{3,2,1,0:T(8,128)(2,1)}, u32[]{:S(2)}, u32[]{:S(2)}) collective-permute-start(bf16[4,4,32,4096]{3,2,1,0:T(8,128)(2,1)} %dynamic-slice_bitcast_fusion), channel_id=1, source_target_pairs={{0,1},{1,0},{2,3},{3,2},{4,5},{5,4},{6,7},{7,6},{8,9},{9,8},{10,11... | collective-permute-start | bytes 12582920 | tf_op jit(solution)/shard_map/ppermute | solution.py:202
  266.2 18.2 %collective-permute-start.20 = (bf16[512,256]{1,0:T(8,128)(2,1)S(1)}, bf16[512,256]{1,0:T(8,128)(2,1)}, u32[]{:S(2)}, u32[]{:S(2)}) collective-permute-start(bf16[512,256]{1,0:T(8,128)(2,1)S(1)} %bitcast.257), channel_id=1, source_target_pairs={{0,16},{8,24},{16,0},{24,8},{1,17},{9,25},{17,1},{25,9},{2,18},{10... | collective-permute-start | bytes 786440 | tf_op jit(solution)/shard_map/ppermute | solution.py:202
  273.4 46.6 %collective-permute-start.23 = (bf16[4,4,32,1152]{3,2,1,0:T(8,128)(2,1)S(1)}, bf16[4,4,32,1152]{3,2,1,0:T(8,128)(2,1)S(1)}, u32[]{:S(2)}, u32[]{:S(2)}) collective-permute-start(bf16[4,4,32,1152]{3,2,1,0:T(8,128)(2,1)S(1)} %dynamic-slice_bitcast_fusion.1), channel_id=1, source_target_pairs={{0,1},{1,0},{2,3},{3,2},{4,5},{5,4},{6,7},{7,6},{8,9},{9,8},{10,11... | collective-permute-start | bytes 3538952 | tf_op jit(solution)/shard_map/ppermute | solution.py:202
  293.1 33.3 %collective-permute-start.25 = (bf16[2,4,32,2048]{3,2,1,0:T(8,128)(2,1)}, bf16[2,4,32,2048]{3,2,1,0:T(8,128)(2,1)}, u32[]{:S(2)}, u32[]{:S(2)}) collective-permute-start(bf16[2,4,32,2048]{3,2,1,0:T(8,128)(2,1)} %dynamic-slice_bitcast_fusion.2), channel_id=1, source_target_pairs={{0,16},{8,24},{16,0},{24,8},{1,17},{9,25},{17,1},{25,9},{2,18},{10... | collective-permute-start | bytes 3145736 | tf_op jit(solution)/shard_map/ppermute | solution.py:202
  293.9 37.4 %collective-permute-start.24 = (bf16[2,4,32,2048]{3,2,1,0:T(8,128)(2,1)S(1)}, bf16[2,4,32,2048]{3,2,1,0:T(8,128)(2,1)}, u32[]{:S(2)}, u32[]{:S(2)}) collective-permute-start(bf16[2,4,32,2048]{3,2,1,0:T(8,128)(2,1)S(1)} %dynamic-slice_bitcast_fusion.3), channel_id=1, source_target_pairs={{0,8},{8,0},{16,24},{24,16},{1,9},{9,1},{17,25},{25,17},{2,10},{10... | collective-permute-start | bytes 3145736 | tf_op jit(solution)/shard_map/ppermute | solution.py:202
  320.8 41.1 %collective-permute-start.39 = (bf16[2,4,32,1152]{3,2,1,0:T(8,128)(2,1)S(1)}, bf16[2,4,32,1152]{3,2,1,0:T(8,128)(2,1)S(1)}, u32[]{:S(2)}, u32[]{:S(2)}) collective-permute-start(bf16[2,4,32,1152]{3,2,1,0:T(8,128)(2,1)S(1)} %dynamic-slice_bitcast_fusion.4), channel_id=1, source_target_pairs={{0,8},{8,0},{16,24},{24,16},{1,9},{9,1},{17,25},{25,17},{2,10},{10... | collective-permute-start | bytes 1769480 | tf_op jit(solution)/shard_map/ppermute | solution.py:202
  333.9 51.7 %collective-permute-start.37 = (bf16[4,32,2048]{2,1,0:T(8,128)(2,1)}, bf16[4,32,2048]{2,1,0:T(8,128)(2,1)}, u32[]{:S(2)}, u32[]{:S(2)}) collective-permute-start(bf16[4,32,2048]{2,1,0:T(8,128)(2,1)} %dynamic-slice_bitcast_fusion.6), channel_id=1, source_target_pairs={{0,16},{8,24},{16,0},{24,8},{1,17},{9,25},{17,1},{25,9},{2,18},{10... | collective-permute-start | bytes 1572872 | tf_op jit(solution)/shard_map/ppermute | solution.py:202
  334.4 51.2 %collective-permute-start.38 = (bf16[4,32,2048]{2,1,0:T(8,128)(2,1)}, bf16[4,32,2048]{2,1,0:T(8,128)(2,1)}, u32[]{:S(2)}, u32[]{:S(2)}) collective-permute-start(bf16[4,32,2048]{2,1,0:T(8,128)(2,1)} %dynamic-slice_bitcast_fusion.5), channel_id=1, source_target_pairs={{0,8},{8,0},{16,24},{24,16},{1,9},{9,1},{17,25},{25,17},{2,10},{10... | collective-permute-start | bytes 1572872 | tf_op jit(solution)/shard_map/ppermute | solution.py:202
  363.6 20.6 %collective-permute-start.40 = (bf16[4,32,1152]{2,1,0:T(8,128)(2,1)}, bf16[4,32,1152]{2,1,0:T(8,128)(2,1)S(1)}, u32[]{:S(2)}, u32[]{:S(2)}) collective-permute-start(bf16[4,32,1152]{2,1,0:T(8,128)(2,1)} %dynamic-slice_bitcast_fusion.10), channel_id=1, source_target_pairs={{0,16},{8,24},{16,0},{24,8},{1,17},{9,25},{17,1},{25,9},{2,18},{10... | collective-permute-start | bytes 884744 | tf_op jit(solution)/shard_map/ppermute | solution.py:202
  379.9 45.3 %collective-permute-start.30 = (bf16[4,4,32,896]{3,2,1,0:T(8,128)(2,1)}, bf16[4,4,32,896]{3,2,1,0:T(8,128)(2,1)}, u32[]{:S(2)}, u32[]{:S(2)}) collective-permute-start(bf16[4,4,32,896]{3,2,1,0:T(8,128)(2,1)} %fusion.41), channel_id=1, source_target_pairs={{0,1},{1,0},{2,3},{3,2},{4,5},{5,4},{6,7},{7,6},{8,9},{9,8},{10,11... | collective-permute-start | bytes 2752520 | tf_op jit(solution)/shard_map/ppermute | solution.py:202
  389.3 26.1 %collective-permute-start.42 = (bf16[32,5248]{1,0:T(8,128)(2,1)S(1)}, bf16[32,5248]{1,0:T(8,128)(2,1)S(1)}, u32[]{:S(2)}, u32[]{:S(2)}) collective-permute-start(bf16[32,5248]{1,0:T(8,128)(2,1)S(1)} %get-tuple-element.131), channel_id=1, source_target_pairs={{0,4},{1,5},{2,6},{3,7},{4,0},{5,1},{6,2},{7,3},{8,12},{9,13},{10,... | collective-permute-start | bytes 1007624 | tf_op jit(solution)/shard_map/ppermute | solution.py:202
  389.9 25.4 %collective-permute-start.43 = (bf16[32,5248]{1,0:T(8,128)(2,1)S(1)}, bf16[32,5248]{1,0:T(8,128)(2,1)S(1)}, u32[]{:S(2)}, u32[]{:S(2)}) collective-permute-start(bf16[32,5248]{1,0:T(8,128)(2,1)S(1)} %get-tuple-element.130), channel_id=1, source_target_pairs={{0,6},{1,7},{2,4},{3,5},{4,2},{5,3},{6,0},{7,1},{8,14},{9,15},{10,... | collective-permute-start | bytes 1007624 | tf_op jit(solution)/shard_map/ppermute | solution.py:202
  394.7 41.9 %collective-permute-start.26 = (bf16[2,256,1024]{2,1,0:T(8,128)(2,1)}, bf16[2,256,1024]{2,1,0:T(8,128)(2,1)}, u32[]{:S(2)}, u32[]{:S(2)}) collective-permute-start(bf16[2,256,1024]{2,1,0:T(8,128)(2,1)} %slice_bitcast_fusion.2), channel_id=1, source_target_pairs={{0,8},{8,0},{16,24},{24,16},{1,9},{9,1},{17,25},{25,17},{2,10},{10... | collective-permute-start | bytes 3145736 | tf_op jit(solution)/shard_map/ppermute | solution.py:202
  404.2 35.0 %collective-permute-start.28 = (bf16[2,256,1024]{2,1,0:T(8,128)(2,1)}, bf16[2,256,1024]{2,1,0:T(8,128)(2,1)}, u32[]{:S(2)}, u32[]{:S(2)}) collective-permute-start(bf16[2,256,1024]{2,1,0:T(8,128)(2,1)} %slice_bitcast_fusion), channel_id=1, source_target_pairs={{0,16},{8,24},{16,0},{24,8},{1,17},{9,25},{17,1},{25,9},{2,18},{10... | collective-permute-start | bytes 3145736 | tf_op jit(solution)/shard_map/ppermute | solution.py:202
  434.2 19.3 %collective-permute-start.32 = (bf16[4,32,896]{2,1,0:T(8,128)(2,1)S(1)}, bf16[4,32,896]{2,1,0:T(8,128)(2,1)S(1)}, u32[]{:S(2)}, u32[]{:S(2)}) collective-permute-start(bf16[4,32,896]{2,1,0:T(8,128)(2,1)S(1)} %get-tuple-element.140), channel_id=1, source_target_pairs={{0,4},{1,5},{2,6},{3,7},{4,0},{5,1},{6,2},{7,3},{8,12},{9,13},{10,... | collective-permute-start | bytes 688136 | tf_op jit(solution)/shard_map/ppermute | solution.py:202
  434.2 19.3 %collective-permute-start.33 = (bf16[4,32,896]{2,1,0:T(8,128)(2,1)S(1)}, bf16[4,32,896]{2,1,0:T(8,128)(2,1)S(1)}, u32[]{:S(2)}, u32[]{:S(2)}) collective-permute-start(bf16[4,32,896]{2,1,0:T(8,128)(2,1)S(1)} %get-tuple-element.139), channel_id=1, source_target_pairs={{0,6},{1,7},{2,4},{3,5},{4,2},{5,3},{6,0},{7,1},{8,14},{9,15},{10,... | collective-permute-start | bytes 688136 | tf_op jit(solution)/shard_map/ppermute | solution.py:202
  439.1 23.7 %collective-permute-start.27 = (bf16[256,1024]{1,0:T(8,128)(2,1)}, bf16[256,1024]{1,0:T(8,128)(2,1)}, u32[]{:S(2)}, u32[]{:S(2)}) collective-permute-start(bf16[256,1024]{1,0:T(8,128)(2,1)} %slice_bitcast_fusion.6), channel_id=1, source_target_pairs={{0,16},{8,24},{16,0},{24,8},{1,17},{9,25},{17,1},{25,9},{2,18},{10... | collective-permute-start | bytes 1572872 | tf_op jit(solution)/shard_map/ppermute | solution.py:202
  442.0 22.1 %collective-permute-start.29 = (bf16[256,1024]{1,0:T(8,128)(2,1)}, bf16[256,1024]{1,0:T(8,128)(2,1)}, u32[]{:S(2)}, u32[]{:S(2)}) collective-permute-start(bf16[256,1024]{1,0:T(8,128)(2,1)} %slice_bitcast_fusion.4), channel_id=1, source_target_pairs={{0,8},{8,0},{16,24},{24,16},{1,9},{9,1},{17,25},{25,17},{2,10},{10... | collective-permute-start | bytes 1572872 | tf_op jit(solution)/shard_map/ppermute | solution.py:202
  (75 other events, 497.9 us)
Sparse Core Ops, SparseCore 0:
  12.6 103.6 all-gather.2
  119.9 76.5 all-gather.4
  243.2 151.9 reduce-scatter.1

commit v3 on v2

--- a/solution.py
+++ b/solution.py
@@ -379,7 +379,8 @@
     mixed = lax.all_gather(mixed, ("seq", "shard"), axis=0, tiled=True)
     full_expand = mixed[:, :hidden_width]
     full_merge = mixed[:, hidden_width : hidden_width + width]
-    small = mixed[:, hidden_width + width :][:, :thin].reshape(devices, -1).astype(F32)
+    full_shrink = lax.all_gather(weight_shrink.astype(BF16), ("seq", "shard"), axis=0, tiled=True)
+    small = mixed[:, hidden_width + width : hidden_width + width + thin].reshape(devices, -1).astype(F32)
     rows = small[:, : 8 * part].reshape(devices, 8, part).transpose(1, 0, 2).reshape(8, width)
     gains, biases = rows[:2], rows[2:]
     hidden_bias = small[:, 8 * part :].reshape(hidden_width)
@@ -387,7 +388,6 @@
     every = jnp.concatenate(
         [piece for r in range(seqs) for piece in (upper[r], lower[r])], axis=0
     )
-    full_shrink = lax.all_gather(weight_shrink.astype(BF16), ("seq", "shard"), axis=0, tiled=True)
 
     bias_row = jnp.concatenate([own_bias[0], jnp.zeros((local,), F32), own_bias[1]])
     qkv = (jnp.dot(every, own_qkv, preferred_element_type=F32) + bias_row).astype(BF16)
@@ -463,8 +463,6 @@
     grad_active = lax.dot_general(grad_branch, full_shrink, NT, preferred_element_type=F32)
     grad_hidden = (grad_active * gelu_slope(hidden)).astype(BF16)
     grad_hidden_bias = jnp.sum(grad_hidden, axis=0, dtype=F32)
-    expand_keep, expand_got, away = core_step(first_low, grad_hidden)
-    grad_hidden = hold(grad_hidden, away)
     grad_first = grad_mid + lax.dot_general(
         grad_hidden, full_expand, NT, preferred_element_type=F32
     )
@@ -500,15 +498,9 @@
     small_grads = small_grads.astype(BF16).reshape(seqs, far, 2, deep, -1)
     slim = small_grads.shape[-1]
     small_grads = jnp.pad(small_grads, ((0, 0),) * 4 + ((0, 128 - slim),))
-    merge_keep, merge_got, away = core_step(context, grad_attended, small_grads)
-
-    expand = add(expand_keep, hold(expand_got, grad_context))
-    middle = expand.shape[-1] // 2
-    expand = [
-        halving_start(expand[..., :middle], masks),
-        halving_start(expand[..., middle:], masks[::-1]),
-    ]
-    grad_context = hold(grad_context, away, *[part[2] for part in expand])
+    merge_keep, merge_got, merge_away = core_step(context, grad_attended, small_grads)
+    expand_keep, expand_got, expand_away = core_step(hold(first_low, grad_heads), grad_hidden)
+    grad_context = hold(grad_context, merge_away, expand_away)
 
     grads = []
     for pair in range(pairs):
@@ -519,32 +511,21 @@
         )
         if pair == 0:
             merge = halving_start(add(merge_keep, hold(merge_got, grads[0][0])), masks)
-            expand = [halving_next(part, grads[0][0]) for part in expand]
+            expand = add(expand_keep, hold(expand_got, grads[0][0]))
+            middle = expand.shape[-1] // 2
+            expand = [
+                halving_start(expand[..., :middle], masks),
+                halving_start(expand[..., middle:], masks[::-1]),
+            ]
             grad_context = hold(grad_context, merge[2], *[part[2] for part in expand])
-    last = grads[-1][0]
-    while isinstance(merge, tuple):
-        merge = halving_next(merge, last)
-        expand = [halving_next(part, last) for part in expand]
     grad_rows = jnp.concatenate(
         [grads[pair][which] for which in range(3) for pair in range(pairs)], axis=1
     )
 
     spread = lax.dot_general(grad_rows, own_qkv, NT, preferred_element_type=F32).astype(BF16)
-    spread = spread.reshape((2,) * len(masks) + (2, half, width))
-    sides = []
-    for side, way in ((0, masks), (1, masks[::-1])):
-        held = lax.index_in_dim(spread, side, len(masks), keepdims=False)
-        left = masks[::-1]
-        for mask in way:
-            at = left.index(mask)
-            left = [m for m in left if m != mask]
-            held = add(
-                lax.index_in_dim(held, 0, at, keepdims=False),
-                swap(lax.index_in_dim(held, 1, at, keepdims=False), "seq", mask, seqs),
-                dtype=BF16 if left else F32,
-            )
-        sides.append(held)
-    grad_input = grad_residual + jnp.concatenate(sides, axis=0)
+    spread = lax.optimization_barrier(spread)
+    spread = spread.reshape(seqs, count, width)
+    spread = [spread[0]] + [swap(spread[r], "seq", r, seqs) for r in reversed(range(1, seqs))]
 
     head_sums = jnp.stack(
         [
@@ -557,10 +538,17 @@
     head_sums = jnp.broadcast_to(
         jnp.pad(head_sums, ((0, 0),) * 4 + ((0, 126),)), (seqs, far, 2, deep, 128)
     )
-    keep, got, _ = core_step(every, grad_rows, head_sums)
+    keep, got, away = core_step(every, grad_rows, head_sums)
+
+    while isinstance(merge, tuple):
+        merge = halving_next(merge, grad_rows)
+        expand = [halving_next(part, grad_rows) for part in expand]
+    others = scatter_direct(jnp.concatenate(expand + [merge], axis=-1), "shard", shards, 2)
     grad_weight = add(keep, got).transpose(1, 0, 2, 3)
-    grad_weight = add(*scatter_direct(grad_weight, "shard", shards, 2))
-    arrived = scatter_direct(grad_weight, "seq", seqs)
+    grad_weight = scatter_direct(grad_weight, "shard", shards, 2)
+    spread = spread[:1] + [hold(piece, grad_weight[0], others[0]) for piece in spread[1:]]
+    grad_input = add(grad_residual, *spread, dtype=F32)
+    arrived = scatter_direct(add(*grad_weight), "seq", seqs)
     head_sums = arrived[0][:, 3 * local : 3 * local + 2].astype(F32).reshape(2, part)
     summed_qkv = in_number_order([piece[:, : 3 * local] for piece in arrived], mine)
     summed_qkv = (
@@ -568,9 +556,7 @@
         .reshape(-1, 3 * width)
         .astype(F32)
     )
-
-    others = jnp.concatenate(expand + [merge], axis=-1)
-    others = add(*scatter_direct(others, "shard", shards, 2), dtype=F32)
+    others = add(*others, dtype=F32)
     summed_expand = others[:, :hidden_width]
     summed_merge = others[:, hidden_width : hidden_width + width]
     small_grads = others[:, hidden_width + width :][:, :slim].reshape(-1)

time: 484 us -> 476 us (0.983)
  waiting for transfers between devices: 123 us -> 140 us
  local copies, waits for them, and re-layouts: 58.7 us -> 45.9 us
  starting transfers between devices: 57.1 us -> 49.2 us
    ppermute x44 -> x43, waiting for transfers between devices: 78.7 us -> 97.7 us  [swap(): return lax.ppermute(value, axis, [(i, i ^ mask) for i in range(size)])]
    ppermute x44 -> x43, starting transfers between devices: 57 us -> 49 us  [swap(): return lax.ppermute(value, axis, [(i, i ^ mask) for i in range(size)])]
    unnamed x141 -> x125, local copies, waits for them, and re-layouts: 29.2 us -> 22 us
    convert_element_type x12 -> x10, other arithmetic: 16.3 us -> 11.7 us  [add(): return total.astype(dtype)]
  transfers between devices with their start and end apart: 47 -> 46, of which waited for: 17 -> 18; matrix products, arithmetic and copies ran while one was open for 30% -> 31% of each run, Pallas kernels for 16% -> 16%
where the time goes in v3:
time: 476 us; the launch traced here: 471 us
  waiting for transfers between devices  140 us (29%)
  matrix products  81.8 us (17%)
  Pallas kernels  77.1 us (16%)
  other arithmetic  61.3 us (13%)
  starting transfers between devices  49.2 us (10%)
  local copies, waits for them, and re-layouts  45.9 us (10%)
  between operations  15.3 us (3%)
    ppermute x43, waiting for transfers between devices, swap(): return lax.ppermute(value, axis, [(i, i ^ mask) for i in range(size)])  97.7 us
    ppermute x43, starting transfers between devices, swap(): return lax.ppermute(value, axis, [(i, i ^ mask) for i in range(size)])  49 us
    pallas_call x2, Pallas kernels, attend_backward(): pl.pallas_call(backward_kernel, grid=(length // block,), in_specs=[whole,...  47.3 us
    all_gather x1, waiting for transfers between devices, body(): lax.all_gather(weight_shrink.astype(BF16), ('seq', 'shard'), axis=0, tile...  42.7 us
    pallas_call x2, Pallas kernels, attend_forward(): pl.pallas_call(forward_kernel, grid=(length // block,), in_specs=[pl.Bloc...  29.8 us
    unnamed x125, local copies, waits for them, and re-layouts  22 us
    dot_general x3, matrix products, core_step(): lax.dot_general(left, right, TN, preferred_element_type=F32).astype(BF16)  14.5 us
    convert_element_type x10, other arithmetic, add(): return total.astype(dtype)  11.7 us
  transfers between devices with their start and end apart: 46, of which 18 were waited for; matrix products, arithmetic and copies ran while one was open for 31% of the time, Pallas kernels for 16%

profile of v3, /device:TPU:0, one launch (start us, length us, event | category | flops | bytes accessed | tf_op | source)
XLA Modules:
  0.0 471.0 jit_solution(17935916454665567808)
XLA Ops:
  14.0 4.0 collective-permute-start.6
  28.5 18.5 %collective-permute-done.10 = bf16[136,768]{1,0:T(8,128)(2,1)S(1)} collective-permute-done((bf16[136,768]{1,0:T(8,128)(2,1)S(1)}, bf16[136,768]{1,0:T(8,128)(2,1)S(1)}, u32[]{:S(2)}, u32[]{:S(2)}) %collective-permute-start.10) | collective-permute-done | bytes 208928 | tf_op jit(solution)/shard_map/ppermute | solution.py:202
  55.2 8.1 %collective-permute-done.3 = bf16[256,1024]{1,0:T(8,128)(2,1)} collective-permute-done((bf16[256,1024]{1,0:T(8,128)(2,1)}, bf16[256,1024]{1,0:T(8,128)(2,1)}, u32[]{:S(2)}, u32[]{:S(2)}) %collective-permute-start.3) | collective-permute-done | bytes 524320 | tf_op jit(solution)/shard_map/ppermute | solution.py:202
  76.7 3.7 select_bitcast_fusion
  82.3 6.2 %add_convert_fusion = bf16[2048,768]{1,0:T(8,128)(2,1)S(1)} fusion(bf16[2048,1024]{1,0:T(8,128)(2,1)} %constant_dynamic-update-slice_fusion, bf16[1024,768]{1,0:T(8,128)(2,1)S(1)} %bitcast.211, f32[768]{0:T(1024)S(1)} %pad_maximum_fusion.5), kind=kOutput, calls=%fused_computation.17 | convolution fusion | flops 3224371200 | bytes 8915968 | tf_op jit(solution)/shard_map/dot_general | solution.py:393
  88.7 14.6 %attend_forward.2 = (bf16[2048,128]{1,0:T(8,128)(2,1)S(1)}, f32[1,2,2048]{2,1,0:T(2,128)S(1)}) custom-call(bf16[2048,256]{1,0:T(8,128)(2,1)S(1)} %get-tuple-element.136.q_ref, bf16[2048,256]{1,0:T(8,128)(2,1)S(1)} %get-tuple-element.135.k_ref, bf16[2048,256]{1,0:T(8,128)(2,1)S(1)} %get-tuple-element.134.v_ref), custom_call_target="tpu_custom_call" | custom-call | flops 8589934592 | bytes 2097152 | tf_op jit(solution)/shard_map/attend_forward/pallas_call | solution.py:81
  106.9 15.1 %attend_forward.3 = (bf16[2048,128]{1,0:T(8,128)(2,1)S(1)}, f32[1,2,2048]{2,1,0:T(2,128)S(1)}) custom-call(bf16[2048,256]{1,0:T(8,128)(2,1)S(1)} %get-tuple-element.136.q_ref, bf16[2048,256]{1,0:T(8,128)(2,1)S(1)} %get-tuple-element.135.k_ref, bf16[2048,256]{1,0:T(8,128)(2,1)S(1)} %get-tuple-element.134.v_ref), custom_call_target="tpu_custom_call" | custom-call | flops 8589934592 | bytes 2097152 | tf_op jit(solution)/shard_map/attend_forward/pallas_call | solution.py:81
  143.5 10.4 %multiply_convert_fusion = (bf16[512,4096]{1,0:T(8,128)(2,1)}, f32[512,4096]{1,0:T(8,128)}) fusion(f32[4096]{0:T(1024)S(1)} %slice_bitcast_fusion.2, bf16[512,1024]{1,0:T(8,128)(2,1)S(1)} %fusion.17, bf16[1024,5248]{1,0:T(8,128)(2,1)} %all-gather.3.cloned.1.call-done), kind=kOutput, calls=%fused_computation.9 | convolution fusion | flops 4307550208 | bytes 22036480 | tf_op jit(solution)/shard_map/dot_general | solution.py:422
  153.9 42.7 %all-gather.5.cloned.1.call-done = bf16[4096,1024]{1,0:T(8,128)(2,1)} async-done(((bf16[128,1024]{1,0:T(8,128)(2,1)}), bf16[4096,1024]{1,0:T(8,128)(2,1)}) %all-gather.5.cloned.1.call-update) | async-done | bytes 8388624 | tf_op jit(solution)/shard_map/all_gather | solution.py:382
  196.6 9.9 %fusion.72 = (f32[512]{0:T(512)S(1)}, f32[512,1024]{1,0:T(8,128)S(1)}) fusion(f32[1024]{0:T(1024)S(1)} %add.356, bf16[512,4096]{1,0:T(8,128)(2,1)} %get-tuple-element.179, bf16[4096,1024]{1,0:T(8,128)(2,1)} %all-gather.5.cloned.1.call-done, f32[1024]{0:T(1024)S(1)} %add.349, f32[1024]{0:T(1024)S(1)} %mul.384, f32[512]{0:T(512)S(1)} %add_rsqrt_fusion.1, ...), kind=kOutput, calls=%fused_computation.257 | convolution fusion | flops 4298636800 | bytes 16795648 | tf_op jit(solution)/shard_map/dot_general | solution.py:424
  208.3 4.0 fusion.16
  215.5 6.7 %convolution_convert_fusion.1 = bf16[4096,1024]{1,0:T(8,128)(2,1)} fusion(bf16[512,4096]{1,0:T(8,128)(2,1)S(1)} %copy-done.50, bf16[512,1024]{1,0:T(8,128)(2,1)S(1)} %get-tuple-element.56), kind=kOutput, calls=%fused_computation.12 | convolution fusion | flops 4299161600 | bytes 13631488 | tf_op jit(solution)/shard_map/dot_general | solution.py:458
  222.2 11.0 %fusion.73 = (bf16[4096]{0:T(1024)(128)(2,1)S(1)}, bf16[512,4096]{1,0:T(8,128)(2,1)S(1)}) fusion(f32[512,4096]{1,0:T(8,128)} %get-tuple-element.180, f32[4096]{0:T(1024)S(1)} %slice_bitcast_fusion.2, bf16[512,1024]{1,0:T(8,128)(2,1)} %copy-done.38, bf16[4096,1024]{1,0:T(8,128)(2,1)} %all-gather.5.cloned.1.call-done), kind=kOutput, calls=%fused_computation.258 | convolution fusion | flops 4320129024 | bytes 22044672 | tf_op jit(solution)/shard_map/dot_general | solution.py:463
  233.2 5.1 %convolution_convert_fusion = bf16[1024,4096]{1,0:T(8,128)(2,1)S(1)} fusion(bf16[512,1024]{1,0:T(8,128)(2,1)S(1)} %fusion.17, bf16[512,4096]{1,0:T(8,128)(2,1)S(1)} %get-tuple-element.185), kind=kOutput, calls=%fused_computation.11 | convolution fusion | flops 4299161600 | bytes 13631488 | tf_op jit(solution)/shard_map/dot_general | solution.py:434
  244.2 11.2 %multiply_reduce_fusion = (bf16[1024]{0:T(1024)(128)(2,1)S(1)}, f32[512]{0:T(512)S(1)}, f32[512]{0:T(512)S(1)}, bf16[1024]{0:T(1024)(128)(2,1)S(1)}, f32[512,1024]{1,0:T(8,128)}) fusion(f32[512,1024]{1,0:T(8,128)S(1)} %copy-done.9, f32[512]{0:T(512)S(1)} %add_rsqrt_fusion.1, f32[512]{0:T(512)S(1)} %broadcast_multiply_fusion.5, f32[1024]{0:T(1024)S(1)} %mul.384, ...), kind=kOutput, calls=%fused_computation.36 | convolution fusion | flops 4300207104 | bytes 18890752 | tf_op jit(solution)/shard_map/dot_general | solution.py:466
  255.6 4.2 convert_reduce_fusion
  260.8 4.6 fusion.28
  276.8 5.0 %collective-permute-done.19 = bf16[512,256]{1,0:T(8,128)(2,1)S(1)} collective-permute-done((bf16[512,256]{1,0:T(8,128)(2,1)S(1)}, bf16[512,256]{1,0:T(8,128)(2,1)S(1)}, u32[]{:S(2)}, u32[]{:S(2)}) %collective-permute-start.19) | collective-permute-done | bytes 262176 | tf_op jit(solution)/shard_map/ppermute | solution.py:202
  281.8 8.1 %collective-permute-done.20 = bf16[512,256]{1,0:T(8,128)(2,1)S(1)} collective-permute-done((bf16[512,256]{1,0:T(8,128)(2,1)S(1)}, bf16[512,256]{1,0:T(8,128)(2,1)S(1)}, u32[]{:S(2)}, u32[]{:S(2)}) %collective-permute-start.20) | collective-permute-done | bytes 262176 | tf_op jit(solution)/shard_map/ppermute | solution.py:202
  290.9 23.6 %attend_backward.2 = (bf16[2048,128]{1,0:T(8,128)(2,1)S(1)}, bf16[2048,128]{1,0:T(8,128)(2,1)S(1)}, bf16[2048,128]{1,0:T(8,128)(2,1)S(1)}) custom-call(bf16[2048,256]{1,0:T(8,128)(2,1)S(1)} %copy-done.3, bf16[2048,256]{1,0:T(8,128)(2,1)S(1)} %copy-done.1, bf16[2048,256]{1,0:T(8,128)(2,1)S(1)} %get-tuple-element.134.v_ref, ...), custom_call_target="tpu_custom_call" | custom-call | flops 21474836480 | bytes 5242880 | tf_op jit(solution)/shard_map/attend_backward/pallas_call | solution.py:177
  316.6 5.1 %fusion.6 = bf16[4,4,32,4096]{3,2,1,0:T(8,128)(2,1)S(1)} fusion(bf16[4,4,32,4096]{3,2,1,0:T(8,128)(2,1)} %collective-permute-done.23, bf16[4,4,2,32,4096]{4,3,2,1,0:T(8,128)(2,1)} %bitcast.198, s32[]{:T(128)S(6)} %select_n.334), kind=kLoop, calls=%fused_computation.8 | loop fusion | flops 8388608 | bytes 12582916 | tf_op jit(solution)/shard_map/convert_element_type | solution.py:221
  326.6 23.7 %attend_backward.3 = (bf16[2048,128]{1,0:T(8,128)(2,1)S(1)}, bf16[2048,128]{1,0:T(8,128)(2,1)S(1)}, bf16[2048,128]{1,0:T(8,128)(2,1)S(1)}) custom-call(bf16[2048,256]{1,0:T(8,128)(2,1)S(1)} %copy-done.3, bf16[2048,256]{1,0:T(8,128)(2,1)S(1)} %copy-done.1, bf16[2048,256]{1,0:T(8,128)(2,1)S(1)} %get-tuple-element.134.v_ref, ...), custom_call_target="tpu_custom_call" | custom-call | flops 21474836480 | bytes 5242880 | tf_op jit(solution)/shard_map/attend_backward/pallas_call | solution.py:177
  353.5 6.9 %convolution_convert_fusion.4 = bf16[1024,768]{1,0:T(8,128)(2,1)S(1)} fusion(bf16[2048,1024]{1,0:T(8,128)(2,1)} %constant_dynamic-update-slice_fusion, bf16[2048,768]{1,0:T(8,128)(2,1)} %copy-done.48), kind=kOutput, calls=%fused_computation.60 | convolution fusion | flops 3222011904 | bytes 8912896 | tf_op jit(solution)/shard_map/dot_general | solution.py:434
  362.2 4.1 convolution_convert_fusion.2
  369.4 6.9 %collective-permute-done.31 = bf16[4,32,1152]{2,1,0:T(8,128)(2,1)S(1)} collective-permute-done((bf16[4,32,1152]{2,1,0:T(8,128)(2,1)S(1)}, bf16[4,32,1152]{2,1,0:T(8,128)(2,1)S(1)}, u32[]{:S(2)}, u32[]{:S(2)}) %collective-permute-start.31) | collective-permute-done | bytes 294944 | tf_op jit(solution)/shard_map/ppermute | solution.py:202
  386.9 8.6 %collective-permute-done.35 = bf16[4,32,896]{2,1,0:T(8,128)(2,1)S(1)} collective-permute-done((bf16[4,32,896]{2,1,0:T(8,128)(2,1)S(1)}, bf16[4,32,896]{2,1,0:T(8,128)(2,1)S(1)}, u32[]{:S(2)}, u32[]{:S(2)}) %collective-permute-start.35) | collective-permute-done | bytes 229408 | tf_op jit(solution)/shard_map/ppermute | solution.py:202
  403.4 17.4 %collective-permute-done.38 = bf16[32,896]{1,0:T(8,128)(2,1)S(1)} collective-permute-done((bf16[32,896]{1,0:T(8,128)(2,1)S(1)}, bf16[32,896]{1,0:T(8,128)(2,1)S(1)}, u32[]{:S(2)}, u32[]{:S(2)}) %collective-permute-start.38) | collective-permute-done | bytes 57376 | tf_op jit(solution)/shard_map/ppermute | solution.py:202
  431.1 4.1 collective-permute-done.40
  435.2 5.7 %collective-permute-done.41 = bf16[32,5248]{1,0:T(8,128)(2,1)S(1)} collective-permute-done((bf16[32,5248]{1,0:T(8,128)(2,1)S(1)}, bf16[32,5248]{1,0:T(8,128)(2,1)S(1)}, u32[]{:S(2)}, u32[]{:S(2)}) %collective-permute-start.41) | collective-permute-done | bytes 335904 | tf_op jit(solution)/shard_map/ppermute | solution.py:202
  441.3 5.3 %collective-permute-done.32 = bf16[512,1024]{1,0:T(8,128)(2,1)} collective-permute-done((bf16[512,1024]{1,0:T(8,128)(2,1)}, bf16[512,1024]{1,0:T(8,128)(2,1)}, u32[]{:S(2)}, u32[]{:S(2)}) %collective-permute-start.32) | collective-permute-done | bytes 1048608 | tf_op jit(solution)/shard_map/ppermute | solution.py:202
  446.6 3.7 collective-permute-done.33
  455.1 4.6 add_bitcast_fusion
  (360 shorter events, 143.1 us)
Async XLA Ops:
  7.2 127.9 %all-gather.3.cloned.1.call-start = ((), (), s32[]{:S(2)}) async-start(), calls=%async_computation.1 | async-start | bytes 11083776 | tf_op jit(solution)/shard_map/all_gather | solution.py:379
  12.5 184.1 %all-gather.5.cloned.1.call-start = ((), (), s32[]{:S(2)}) async-start(), calls=%async_computation.2 | async-start | bytes 8650752 | tf_op jit(solution)/shard_map/all_gather | solution.py:382
  13.3 447.8 %reduce-scatter.2.cloned.1.call-start = ((), (), s32[]{:S(2)}) async-start(), calls=%async_computation.3 | async-start | bytes 8650752 | tf_op jit(solution)/shard_map/reduce_scatter | solution.py:459
  19.6 33.4 %collective-permute-start = (bf16[256,1024]{1,0:T(8,128)(2,1)}, bf16[256,1024]{1,0:T(8,128)(2,1)}, u32[]{:S(2)}, u32[]{:S(2)}) collective-permute-start(bf16[256,1024]{1,0:T(8,128)(2,1)} %get-tuple-element.148), channel_id=1, source_target_pairs={{0,8},{8,0},{16,24},{24,16},{1,9},{9,1},{17,25},{25,17},{2,10},{10... | collective-permute-start | bytes 1572872 | tf_op jit(solution)/shard_map/ppermute | solution.py:202
  21.5 48.2 %collective-permute-start.2 = (bf16[256,1024]{1,0:T(8,128)(2,1)}, bf16[256,1024]{1,0:T(8,128)(2,1)}, u32[]{:S(2)}, u32[]{:S(2)}) collective-permute-start(bf16[256,1024]{1,0:T(8,128)(2,1)} %get-tuple-element.148), channel_id=1, source_target_pairs={{0,16},{8,24},{16,0},{24,8},{1,17},{9,25},{17,1},{25,9},{2,18},{10... | collective-permute-start | bytes 1572872 | tf_op jit(solution)/shard_map/ppermute | solution.py:202
  23.2 23.8 %collective-permute-start.10 = (bf16[136,768]{1,0:T(8,128)(2,1)S(1)}, bf16[136,768]{1,0:T(8,128)(2,1)S(1)}, u32[]{:S(2)}, u32[]{:S(2)}) collective-permute-start(bf16[136,768]{1,0:T(8,128)(2,1)S(1)} %fusion.48), channel_id=1, source_target_pairs={{0,4},{1,5},{2,6},{3,7},{4,0},{5,1},{6,2},{7,3},{8,12},{9,13},{10,... | collective-permute-start | bytes 626696 | tf_op jit(solution)/shard_map/ppermute | solution.py:202
  25.9 21.7 %collective-permute-start.11 = (bf16[136,768]{1,0:T(8,128)(2,1)S(1)}, bf16[136,768]{1,0:T(8,128)(2,1)S(1)}, u32[]{:S(2)}, u32[]{:S(2)}) collective-permute-start(bf16[136,768]{1,0:T(8,128)(2,1)S(1)} %fusion.48), channel_id=1, source_target_pairs={{0,2},{1,3},{2,0},{3,1},{4,6},{5,7},{6,4},{7,5},{8,10},{9,11},{10,... | collective-permute-start | bytes 626696 | tf_op jit(solution)/shard_map/ppermute | solution.py:202
  27.4 21.1 %collective-permute-start.9 = (bf16[136,768]{1,0:T(8,128)(2,1)S(1)}, bf16[136,768]{1,0:T(8,128)(2,1)S(1)}, u32[]{:S(2)}, u32[]{:S(2)}) collective-permute-start(bf16[136,768]{1,0:T(8,128)(2,1)S(1)} %fusion.48), channel_id=1, source_target_pairs={{0,6},{1,7},{2,4},{3,5},{4,2},{5,3},{6,0},{7,1},{8,14},{9,15},{10,... | collective-permute-start | bytes 626696 | tf_op jit(solution)/shard_map/ppermute | solution.py:202
  47.0 20.8 %collective-permute-start.1 = (bf16[256,1024]{1,0:T(8,128)(2,1)}, bf16[256,1024]{1,0:T(8,128)(2,1)}, u32[]{:S(2)}, u32[]{:S(2)}) collective-permute-start(bf16[256,1024]{1,0:T(8,128)(2,1)} %get-tuple-element.147), channel_id=1, source_target_pairs={{0,8},{8,0},{16,24},{24,16},{1,9},{9,1},{17,25},{25,17},{2,10},{10... | collective-permute-start | bytes 1572872 | tf_op jit(solution)/shard_map/ppermute | solution.py:202
  47.5 15.7 %collective-permute-start.3 = (bf16[256,1024]{1,0:T(8,128)(2,1)}, bf16[256,1024]{1,0:T(8,128)(2,1)}, u32[]{:S(2)}, u32[]{:S(2)}) collective-permute-start(bf16[256,1024]{1,0:T(8,128)(2,1)} %get-tuple-element.147), channel_id=1, source_target_pairs={{0,16},{8,24},{16,0},{24,8},{1,17},{9,25},{17,1},{25,9},{2,18},{10... | collective-permute-start | bytes 1572872 | tf_op jit(solution)/shard_map/ppermute | solution.py:202
  53.0 23.6 %collective-permute-start.12 = (bf16[4,136,768]{2,0,1:T(4,128)(2,1)}, bf16[4,136,768]{2,0,1:T(4,128)(2,1)}, u32[]{:S(2)}, u32[]{:S(2)}) collective-permute-start(bf16[4,136,768]{2,0,1:T(4,128)(2,1)} %pad_maximum_fusion.2), channel_id=1, source_target_pairs={{0,1},{1,0},{2,3},{3,2},{4,5},{5,4},{6,7},{7,6},{8,9},{9,8},{10,11... | collective-permute-start | bytes 2506760 | tf_op jit(solution)/shard_map/ppermute | solution.py:202
  53.1 20.5 %collective-permute-start.4 = (bf16[256,1024]{1,0:T(8,128)(2,1)}, bf16[256,1024]{1,0:T(8,128)(2,1)}, u32[]{:S(2)}, u32[]{:S(2)}) collective-permute-start(bf16[256,1024]{1,0:T(8,128)(2,1)} %collective-permute-done), channel_id=1, source_target_pairs={{0,16},{8,24},{16,0},{24,8},{1,17},{9,25},{17,1},{25,9},{2,18},{10... | collective-permute-start | bytes 1572872 | tf_op jit(solution)/shard_map/ppermute | solution.py:202
  103.4 20.6 %collective-permute-start.13 = (bf16[512,128]{1,0:T(8,128)(2,1)S(1)}, bf16[512,128]{1,0:T(8,128)(2,1)S(1)}, u32[]{:S(2)}, u32[]{:S(2)}) collective-permute-start(bf16[512,128]{1,0:T(8,128)(2,1)S(1)} %get-tuple-element.161), channel_id=1, source_target_pairs={{0,24},{8,16},{16,8},{24,0},{1,25},{9,17},{17,9},{25,1},{2,26},{10... | collective-permute-start | bytes 393224 | tf_op jit(solution)/shard_map/ppermute | solution.py:202
  104.9 20.8 %collective-permute-start.14 = (bf16[512,128]{1,0:T(8,128)(2,1)S(1)}, bf16[512,128]{1,0:T(8,128)(2,1)S(1)}, u32[]{:S(2)}, u32[]{:S(2)}) collective-permute-start(bf16[512,128]{1,0:T(8,128)(2,1)S(1)} %get-tuple-element.160), channel_id=1, source_target_pairs={{0,16},{8,24},{16,0},{24,8},{1,17},{9,25},{17,1},{25,9},{2,18},{10... | collective-permute-start | bytes 393224 | tf_op jit(solution)/shard_map/ppermute | solution.py:202
  105.2 20.4 %collective-permute-start.15 = (bf16[512,128]{1,0:T(8,128)(2,1)S(1)}, bf16[512,128]{1,0:T(8,128)(2,1)S(1)}, u32[]{:S(2)}, u32[]{:S(2)}) collective-permute-start(bf16[512,128]{1,0:T(8,128)(2,1)S(1)} %get-tuple-element.159), channel_id=1, source_target_pairs={{0,8},{8,0},{16,24},{24,16},{1,9},{9,1},{17,25},{25,17},{2,10},{10... | collective-permute-start | bytes 393224 | tf_op jit(solution)/shard_map/ppermute | solution.py:202
  243.9 72.7 %collective-permute-start.23 = (bf16[4,4,32,4096]{3,2,1,0:T(8,128)(2,1)}, bf16[4,4,32,4096]{3,2,1,0:T(8,128)(2,1)}, u32[]{:S(2)}, u32[]{:S(2)}) collective-permute-start(bf16[4,4,32,4096]{3,2,1,0:T(8,128)(2,1)} %dynamic-slice_bitcast_fusion), channel_id=1, source_target_pairs={{0,1},{1,0},{2,3},{3,2},{4,5},{5,4},{6,7},{7,6},{8,9},{9,8},{10,11... | collective-permute-start | bytes 12582920 | tf_op jit(solution)/shard_map/ppermute | solution.py:202
  271.4 18.5 %collective-permute-start.20 = (bf16[512,256]{1,0:T(8,128)(2,1)S(1)}, bf16[512,256]{1,0:T(8,128)(2,1)S(1)}, u32[]{:S(2)}, u32[]{:S(2)}) collective-permute-start(bf16[512,256]{1,0:T(8,128)(2,1)S(1)} %bitcast.217), channel_id=1, source_target_pairs={{0,16},{8,24},{16,0},{24,8},{1,17},{9,25},{17,1},{25,9},{2,18},{10... | collective-permute-start | bytes 786440 | tf_op jit(solution)/shard_map/ppermute | solution.py:202
  272.2 17.7 %collective-permute-start.21 = (bf16[512,256]{1,0:T(8,128)(2,1)S(1)}, bf16[512,256]{1,0:T(8,128)(2,1)S(1)}, u32[]{:S(2)}, u32[]{:S(2)}) collective-permute-start(bf16[512,256]{1,0:T(8,128)(2,1)S(1)} %bitcast.218), channel_id=1, source_target_pairs={{0,24},{8,16},{16,8},{24,0},{1,25},{9,17},{17,9},{25,1},{2,26},{10... | collective-permute-start | bytes 786440 | tf_op jit(solution)/shard_map/ppermute | solution.py:202
  276.7 37.9 %collective-permute-start.22 = (bf16[4,4,32,1152]{3,2,1,0:T(8,128)(2,1)S(1)}, bf16[4,4,32,1152]{3,2,1,0:T(8,128)(2,1)S(1)}, u32[]{:S(2)}, u32[]{:S(2)}) collective-permute-start(bf16[4,4,32,1152]{3,2,1,0:T(8,128)(2,1)S(1)} %dynamic-slice_bitcast_fusion.1), channel_id=1, source_target_pairs={{0,1},{1,0},{2,3},{3,2},{4,5},{5,4},{6,7},{7,6},{8,9},{9,8},{10,11... | collective-permute-start | bytes 3538952 | tf_op jit(solution)/shard_map/ppermute | solution.py:202
  315.0 35.9 %collective-permute-start.30 = (bf16[2,4,32,1152]{3,2,1,0:T(8,128)(2,1)S(1)}, bf16[2,4,32,1152]{3,2,1,0:T(8,128)(2,1)S(1)}, u32[]{:S(2)}, u32[]{:S(2)}) collective-permute-start(bf16[2,4,32,1152]{3,2,1,0:T(8,128)(2,1)S(1)} %dynamic-slice_bitcast_fusion.4), channel_id=1, source_target_pairs={{0,8},{8,0},{16,24},{24,16},{1,9},{9,1},{17,25},{25,17},{2,10},{10... | collective-permute-start | bytes 1769480 | tf_op jit(solution)/shard_map/ppermute | solution.py:202
  323.3 57.8 %collective-permute-start.26 = (bf16[2,4,32,2048]{3,2,1,0:T(8,128)(2,1)}, bf16[2,4,32,2048]{3,2,1,0:T(8,128)(2,1)}, u32[]{:S(2)}, u32[]{:S(2)}) collective-permute-start(bf16[2,4,32,2048]{3,2,1,0:T(8,128)(2,1)} %dynamic-slice_bitcast_fusion.3), channel_id=1, source_target_pairs={{0,8},{8,0},{16,24},{24,16},{1,9},{9,1},{17,25},{25,17},{2,10},{10... | collective-permute-start | bytes 3145736 | tf_op jit(solution)/shard_map/ppermute | solution.py:202
  325.3 59.1 %collective-permute-start.28 = (bf16[2,4,32,2048]{3,2,1,0:T(8,128)(2,1)}, bf16[2,4,32,2048]{3,2,1,0:T(8,128)(2,1)}, u32[]{:S(2)}, u32[]{:S(2)}) collective-permute-start(bf16[2,4,32,2048]{3,2,1,0:T(8,128)(2,1)} %dynamic-slice_bitcast_fusion.2), channel_id=1, source_target_pairs={{0,16},{8,24},{16,0},{24,8},{1,17},{9,25},{17,1},{25,9},{2,18},{10... | collective-permute-start | bytes 3145736 | tf_op jit(solution)/shard_map/ppermute | solution.py:202
  360.6 15.7 %collective-permute-start.25 = (bf16[4,4,32,896]{3,2,1,0:T(8,128)(2,1)S(1)}, bf16[4,4,32,896]{3,2,1,0:T(8,128)(2,1)S(1)}, u32[]{:S(2)}, u32[]{:S(2)}) collective-permute-start(bf16[4,4,32,896]{3,2,1,0:T(8,128)(2,1)S(1)} %fusion.38), channel_id=1, source_target_pairs={{0,1},{1,0},{2,3},{3,2},{4,5},{5,4},{6,7},{7,6},{8,9},{9,8},{10,11... | collective-permute-start | bytes 2752520 | tf_op jit(solution)/shard_map/ppermute | solution.py:202
  376.7 18.7 %collective-permute-start.35 = (bf16[4,32,896]{2,1,0:T(8,128)(2,1)S(1)}, bf16[4,32,896]{2,1,0:T(8,128)(2,1)S(1)}, u32[]{:S(2)}, u32[]{:S(2)}) collective-permute-start(bf16[4,32,896]{2,1,0:T(8,128)(2,1)S(1)} %get-tuple-element.151), channel_id=1, source_target_pairs={{0,4},{1,5},{2,6},{3,7},{4,0},{5,1},{6,2},{7,3},{8,12},{9,13},{10,... | collective-permute-start | bytes 688136 | tf_op jit(solution)/shard_map/ppermute | solution.py:202
  377.6 17.9 %collective-permute-start.36 = (bf16[4,32,896]{2,1,0:T(8,128)(2,1)S(1)}, bf16[4,32,896]{2,1,0:T(8,128)(2,1)S(1)}, u32[]{:S(2)}, u32[]{:S(2)}) collective-permute-start(bf16[4,32,896]{2,1,0:T(8,128)(2,1)S(1)} %get-tuple-element.150), channel_id=1, source_target_pairs={{0,6},{1,7},{2,4},{3,5},{4,2},{5,3},{6,0},{7,1},{8,14},{9,15},{10,... | collective-permute-start | bytes 688136 | tf_op jit(solution)/shard_map/ppermute | solution.py:202
  383.6 39.1 %collective-permute-start.27 = (bf16[4,32,2048]{2,1,0:T(8,128)(2,1)}, bf16[4,32,2048]{2,1,0:T(8,128)(2,1)}, u32[]{:S(2)}, u32[]{:S(2)}) collective-permute-start(bf16[4,32,2048]{2,1,0:T(8,128)(2,1)} %dynamic-slice_bitcast_fusion.6), channel_id=1, source_target_pairs={{0,16},{8,24},{16,0},{24,8},{1,17},{9,25},{17,1},{25,9},{2,18},{10... | collective-permute-start | bytes 1572872 | tf_op jit(solution)/shard_map/ppermute | solution.py:202
  386.9 35.8 %collective-permute-start.29 = (bf16[4,32,2048]{2,1,0:T(8,128)(2,1)}, bf16[4,32,2048]{2,1,0:T(8,128)(2,1)}, u32[]{:S(2)}, u32[]{:S(2)}) collective-permute-start(bf16[4,32,2048]{2,1,0:T(8,128)(2,1)} %dynamic-slice_bitcast_fusion.5), channel_id=1, source_target_pairs={{0,8},{8,0},{16,24},{24,16},{1,9},{9,1},{17,25},{25,17},{2,10},{10... | collective-permute-start | bytes 1572872 | tf_op jit(solution)/shard_map/ppermute | solution.py:202
  397.6 23.2 %collective-permute-start.38 = (bf16[32,896]{1,0:T(8,128)(2,1)S(1)}, bf16[32,896]{1,0:T(8,128)(2,1)S(1)}, u32[]{:S(2)}, u32[]{:S(2)}) collective-permute-start(bf16[32,896]{1,0:T(8,128)(2,1)S(1)} %get-tuple-element.172), channel_id=1, source_target_pairs={{0,16},{8,24},{16,0},{24,8},{1,17},{9,25},{17,1},{25,9},{2,18},{10... | collective-permute-start | bytes 172040 | tf_op jit(solution)/shard_map/ppermute | solution.py:202
  398.5 23.4 %collective-permute-start.39 = (bf16[32,896]{1,0:T(8,128)(2,1)S(1)}, bf16[32,896]{1,0:T(8,128)(2,1)S(1)}, u32[]{:S(2)}, u32[]{:S(2)}) collective-permute-start(bf16[32,896]{1,0:T(8,128)(2,1)S(1)} %get-tuple-element.171), channel_id=1, source_target_pairs={{0,8},{8,0},{16,24},{24,16},{1,9},{9,1},{17,25},{25,17},{2,10},{10... | collective-permute-start | bytes 172040 | tf_op jit(solution)/shard_map/ppermute | solution.py:202
  401.2 40.1 %collective-permute-start.24 = (bf16[512,1024]{1,0:T(8,128)(2,1)}, bf16[512,1024]{1,0:T(8,128)(2,1)}, u32[]{:S(2)}, u32[]{:S(2)}) collective-permute-start(bf16[512,1024]{1,0:T(8,128)(2,1)} %get-tuple-element.129), channel_id=1, source_target_pairs={{0,24},{8,16},{16,8},{24,0},{1,25},{9,17},{17,9},{25,1},{2,26},{10... | collective-permute-start | bytes 3145736 | tf_op jit(solution)/shard_map/ppermute | solution.py:202
  420.8 25.7 %collective-permute-start.32 = (bf16[512,1024]{1,0:T(8,128)(2,1)}, bf16[512,1024]{1,0:T(8,128)(2,1)}, u32[]{:S(2)}, u32[]{:S(2)}) collective-permute-start(bf16[512,1024]{1,0:T(8,128)(2,1)} %get-tuple-element.131), channel_id=1, source_target_pairs={{0,16},{8,24},{16,0},{24,8},{1,17},{9,25},{17,1},{25,9},{2,18},{10... | collective-permute-start | bytes 3145736 | tf_op jit(solution)/shard_map/ppermute | solution.py:202
  425.5 15.4 %collective-permute-start.41 = (bf16[32,5248]{1,0:T(8,128)(2,1)S(1)}, bf16[32,5248]{1,0:T(8,128)(2,1)S(1)}, u32[]{:S(2)}, u32[]{:S(2)}) collective-permute-start(bf16[32,5248]{1,0:T(8,128)(2,1)S(1)} %get-tuple-element.142), channel_id=1, source_target_pairs={{0,4},{1,5},{2,6},{3,7},{4,0},{5,1},{6,2},{7,3},{8,12},{9,13},{10,... | collective-permute-start | bytes 1007624 | tf_op jit(solution)/shard_map/ppermute | solution.py:202
  (66 other events, 482.3 us)
Sparse Core Ops, SparseCore 0:
  12.6 103.3 all-gather.2
  119.6 76.9 all-gather.4
  222.3 152.1 reduce-scatter.1

commit v4 on v3

--- a/solution.py
+++ b/solution.py
@@ -523,9 +523,22 @@
     )
 
     spread = lax.dot_general(grad_rows, own_qkv, NT, preferred_element_type=F32).astype(BF16)
-    spread = lax.optimization_barrier(spread)
-    spread = spread.reshape(seqs, count, width)
-    spread = [spread[0]] + [swap(spread[r], "seq", r, seqs) for r in reversed(range(1, seqs))]
+    spread, grad_rows = lax.optimization_barrier((spread, grad_rows))
+    spread = spread.reshape((2,) * len(masks) + (2, half, width))
+
+    def spread_send(held, left, way):
+        at = left.index(way[0])
+        keep = lax.index_in_dim(held, 0, at, keepdims=False)
+        away = lax.index_in_dim(held, 1, at, keepdims=False)
+        left = [m for m in left if m != way[0]]
+        return keep, swap(away, "seq", way[0], seqs), left, way[1:]
+
+    sides = [
+        spread_send(
+            lax.index_in_dim(spread, side, len(masks), keepdims=False), masks[::-1], way
+        )
+        for side, way in ((0, masks), (1, masks[::-1]))
+    ]
 
     head_sums = jnp.stack(
         [
@@ -543,12 +556,27 @@
     while isinstance(merge, tuple):
         merge = halving_next(merge, grad_rows)
         expand = [halving_next(part, grad_rows) for part in expand]
+        fence = [part[2] for part in expand if isinstance(part, tuple)]
+        if sides[0][3]:
+            sides = [
+                spread_send(add(held, hold(arrived, *fence)), left, way)
+                for held, arrived, left, way in sides
+            ]
+    while sides[0][3]:
+        sides = [
+            spread_send(add(held, arrived), left, way) for held, arrived, left, way in sides
+        ]
+    expand = [hold(part, sides[0][0], sides[1][0]) for part in expand]
     others = scatter_direct(jnp.concatenate(expand + [merge], axis=-1), "shard", shards, 2)
     grad_weight = add(keep, got).transpose(1, 0, 2, 3)
     grad_weight = scatter_direct(grad_weight, "shard", shards, 2)
-    spread = spread[:1] + [hold(piece, grad_weight[0], others[0]) for piece in spread[1:]]
-    grad_input = add(grad_residual, *spread, dtype=F32)
+    sides = [
+        add(held, hold(arrived, grad_weight[0], others[0]), dtype=F32)
+        for held, arrived, _, _ in sides
+    ]
+    grad_input = grad_residual + jnp.concatenate(sides, axis=0)
     arrived = scatter_direct(add(*grad_weight), "seq", seqs)
+    arrived = arrived[:1] + [hold(piece, others[0]) for piece in arrived[1:]]
     head_sums = arrived[0][:, 3 * local : 3 * local + 2].astype(F32).reshape(2, part)
     summed_qkv = in_number_order([piece[:, : 3 * local] for piece in arrived], mine)
     summed_qkv = (

time: 476 us -> 478 us (level)
  waiting for transfers between devices: 140 us -> 130 us
  local copies, waits for them, and re-layouts: 45.9 us -> 51.6 us
    ppermute x43 -> x44, waiting for transfers between devices: 97.7 us -> 88.9 us  [swap(): return lax.ppermute(value, axis, [(i, i ^ mask) for i in range(size)])]
    ppermute x43 -> x44, starting transfers between devices: 49 us -> 50.7 us  [swap(): return lax.ppermute(value, axis, [(i, i ^ mask) for i in range(size)])]
    convert_element_type x10 -> x12, other arithmetic: 11.7 us -> 10.3 us  [add(): return total.astype(dtype)]
    unnamed x125 -> x127, local copies, waits for them, and re-layouts: 22 us -> 22.8 us
  transfers between devices with their start and end apart: 46 -> 47, of which waited for: 18 -> 19; matrix products, arithmetic and copies ran while one was open for 31% -> 33% of each run, Pallas kernels for 16% -> 16%
where the time goes in v4:
time: 478 us; the launch traced here: 472 us
  waiting for transfers between devices  130 us (27%)
  matrix products  83.9 us (18%)
  Pallas kernels  76.5 us (16%)
  other arithmetic  63 us (13%)
  local copies, waits for them, and re-layouts  51.6 us (11%)
  starting transfers between devices  50.8 us (11%)
  between operations  15.6 us (3%)
    ppermute x44, waiting for transfers between devices, swap(): return lax.ppermute(value, axis, [(i, i ^ mask) for i in range(size)])  88.9 us
    ppermute x44, starting transfers between devices, swap(): return lax.ppermute(value, axis, [(i, i ^ mask) for i in range(size)])  50.7 us
    pallas_call x2, Pallas kernels, attend_backward(): pl.pallas_call(backward_kernel, grid=(length // block,), in_specs=[whole,...  47.1 us
    all_gather x1, waiting for transfers between devices, body(): lax.all_gather(weight_shrink.astype(BF16), ('seq', 'shard'), axis=0, tile...  41.2 us
    pallas_call x2, Pallas kernels, attend_forward(): pl.pallas_call(forward_kernel, grid=(length // block,), in_specs=[pl.Bloc...  29.4 us
    unnamed x127, local copies, waits for them, and re-layouts  22.8 us
    dot_general x3, matrix products, core_step(): lax.dot_general(left, right, TN, preferred_element_type=F32).astype(BF16)  14.7 us
    dot_general x1, matrix products, body(): lax.dot_general(grad_hidden, full_expand, NT, preferred_element_type=F32)  11.2 us
  transfers between devices with their start and end apart: 47, of which 19 were waited for; matrix products, arithmetic and copies ran while one was open for 33% of the time, Pallas kernels for 16%

profile of v4, /device:TPU:0, one launch (start us, length us, event | category | flops | bytes accessed | tf_op | source)
XLA Modules:
  0.0 471.5 jit_solution(13138796358541001922)
XLA Ops:
  14.0 4.0 collective-permute-start.6
  28.5 18.5 %collective-permute-done.10 = bf16[136,768]{1,0:T(8,128)(2,1)S(1)} collective-permute-done((bf16[136,768]{1,0:T(8,128)(2,1)S(1)}, bf16[136,768]{1,0:T(8,128)(2,1)S(1)}, u32[]{:S(2)}, u32[]{:S(2)}) %collective-permute-start.10) | collective-permute-done | bytes 208928 | tf_op jit(solution)/shard_map/ppermute | solution.py:202
  55.2 8.1 %collective-permute-done.3 = bf16[256,1024]{1,0:T(8,128)(2,1)} collective-permute-done((bf16[256,1024]{1,0:T(8,128)(2,1)}, bf16[256,1024]{1,0:T(8,128)(2,1)}, u32[]{:S(2)}, u32[]{:S(2)}) %collective-permute-start.3) | collective-permute-done | bytes 524320 | tf_op jit(solution)/shard_map/ppermute | solution.py:202
  76.7 3.9 select_bitcast_fusion
  82.4 6.2 %add_convert_fusion = bf16[2048,768]{1,0:T(8,128)(2,1)S(1)} fusion(bf16[2048,1024]{1,0:T(8,128)(2,1)} %constant_dynamic-update-slice_fusion, bf16[1024,768]{1,0:T(8,128)(2,1)S(1)} %bitcast.247, f32[768]{0:T(1024)S(1)} %pad_maximum_fusion.5), kind=kOutput, calls=%fused_computation.17 | convolution fusion | flops 3224371200 | bytes 8915968 | tf_op jit(solution)/shard_map/dot_general | solution.py:393
  88.9 14.6 %attend_forward.2 = (bf16[2048,128]{1,0:T(8,128)(2,1)S(1)}, f32[1,2,2048]{2,1,0:T(2,128)S(1)}) custom-call(bf16[2048,256]{1,0:T(8,128)(2,1)S(1)} %get-tuple-element.151.q_ref, bf16[2048,256]{1,0:T(8,128)(2,1)S(1)} %get-tuple-element.150.k_ref, bf16[2048,256]{1,0:T(8,128)(2,1)S(1)} %get-tuple-element.149.v_ref), custom_call_target="tpu_custom_call" | custom-call | flops 8589934592 | bytes 2097152 | tf_op jit(solution)/shard_map/attend_forward/pallas_call | solution.py:81
  107.1 14.8 %attend_forward.3 = (bf16[2048,128]{1,0:T(8,128)(2,1)S(1)}, f32[1,2,2048]{2,1,0:T(2,128)S(1)}) custom-call(bf16[2048,256]{1,0:T(8,128)(2,1)S(1)} %get-tuple-element.151.q_ref, bf16[2048,256]{1,0:T(8,128)(2,1)S(1)} %get-tuple-element.150.k_ref, bf16[2048,256]{1,0:T(8,128)(2,1)S(1)} %get-tuple-element.149.v_ref), custom_call_target="tpu_custom_call" | custom-call | flops 8589934592 | bytes 2097152 | tf_op jit(solution)/shard_map/attend_forward/pallas_call | solution.py:81
  138.7 3.5 fusion.73
  144.6 10.7 %multiply_convert_fusion = (bf16[512,4096]{1,0:T(8,128)(2,1)}, f32[512,4096]{1,0:T(8,128)}) fusion(f32[4096]{0:T(1024)S(1)} %slice_bitcast_fusion.10, bf16[512,1024]{1,0:T(8,128)(2,1)S(1)} %fusion.20, bf16[1024,5248]{1,0:T(8,128)(2,1)} %all-gather.3.cloned.1.call-done), kind=kOutput, calls=%fused_computation.9 | convolution fusion | flops 4307550208 | bytes 22036480 | tf_op jit(solution)/shard_map/dot_general | solution.py:422
  155.2 41.2 %all-gather.5.cloned.1.call-done = bf16[4096,1024]{1,0:T(8,128)(2,1)} async-done(((bf16[128,1024]{1,0:T(8,128)(2,1)}), bf16[4096,1024]{1,0:T(8,128)(2,1)}) %all-gather.5.cloned.1.call-update) | async-done | bytes 8388624 | tf_op jit(solution)/shard_map/all_gather | solution.py:382
  196.4 10.1 %fusion.74 = (f32[512]{0:T(512)S(1)}, f32[512,1024]{1,0:T(8,128)S(1)}) fusion(f32[1024]{0:T(1024)S(1)} %add.359, bf16[512,4096]{1,0:T(8,128)(2,1)} %get-tuple-element.198, bf16[4096,1024]{1,0:T(8,128)(2,1)} %all-gather.5.cloned.1.call-done, f32[1024]{0:T(1024)S(1)} %add.352, f32[1024]{0:T(1024)S(1)} %mul.384, f32[512]{0:T(512)S(1)} %add_rsqrt_fusion.1, ...), kind=kOutput, calls=%fused_computation.272 | convolution fusion | flops 4298636800 | bytes 16795648 | tf_op jit(solution)/shard_map/dot_general | solution.py:424
  208.4 4.0 fusion.19
  215.5 6.7 %convolution_convert_fusion.1 = bf16[4096,1024]{1,0:T(8,128)(2,1)} fusion(bf16[512,4096]{1,0:T(8,128)(2,1)S(1)} %copy-done.51, bf16[512,1024]{1,0:T(8,128)(2,1)S(1)} %get-tuple-element.64), kind=kOutput, calls=%fused_computation.12 | convolution fusion | flops 4299161600 | bytes 13631488 | tf_op jit(solution)/shard_map/dot_general | solution.py:458
  222.3 11.0 %fusion.75 = (bf16[4096]{0:T(1024)(128)(2,1)S(1)}, bf16[512,4096]{1,0:T(8,128)(2,1)S(1)}) fusion(f32[512,4096]{1,0:T(8,128)} %get-tuple-element.199, f32[4096]{0:T(1024)S(1)} %slice_bitcast_fusion.10, bf16[512,1024]{1,0:T(8,128)(2,1)} %copy-done.39, bf16[4096,1024]{1,0:T(8,128)(2,1)} %all-gather.5.cloned.1.call-done), kind=kOutput, calls=%fused_computation.273 | convolution fusion | flops 4320129024 | bytes 22044672 | tf_op jit(solution)/shard_map/dot_general | solution.py:463
  233.3 5.3 %convolution_convert_fusion = bf16[1024,4096]{1,0:T(8,128)(2,1)S(1)} fusion(bf16[512,1024]{1,0:T(8,128)(2,1)S(1)} %copy-done.38, bf16[512,4096]{1,0:T(8,128)(2,1)S(1)} %get-tuple-element.204), kind=kOutput, calls=%fused_computation.11 | convolution fusion | flops 4299161600 | bytes 13631488 | tf_op jit(solution)/shard_map/dot_general | solution.py:434
  240.9 3.3 copy-done.10
  244.5 11.2 %multiply_reduce_fusion = (bf16[1024]{0:T(1024)(128)(2,1)S(1)}, f32[512]{0:T(512)S(1)}, f32[512]{0:T(512)S(1)}, bf16[1024]{0:T(1024)(128)(2,1)S(1)}, f32[512,1024]{1,0:T(8,128)}) fusion(f32[512,1024]{1,0:T(8,128)S(1)} %copy-done.7, f32[512]{0:T(512)S(1)} %add_rsqrt_fusion.1, f32[512]{0:T(512)S(1)} %broadcast_multiply_fusion.5, f32[1024]{0:T(1024)S(1)} %mul.384, ...), kind=kOutput, calls=%fused_computation.42 | convolution fusion | flops 4300207104 | bytes 18890752 | tf_op jit(solution)/shard_map/dot_general | solution.py:466
  255.9 4.2 convert_reduce_fusion
  261.1 4.5 fusion.31
  268.4 4.7 constant_dynamic-slice_fusion.3
  280.1 4.5 collective-permute-done.19
  284.5 9.1 %collective-permute-done.20 = bf16[512,256]{1,0:T(8,128)(2,1)S(1)} collective-permute-done((bf16[512,256]{1,0:T(8,128)(2,1)S(1)}, bf16[512,256]{1,0:T(8,128)(2,1)S(1)}, u32[]{:S(2)}, u32[]{:S(2)}) %collective-permute-start.20) | collective-permute-done | bytes 262176 | tf_op jit(solution)/shard_map/ppermute | solution.py:202
  294.8 23.7 %attend_backward.2 = (bf16[2048,128]{1,0:T(8,128)(2,1)S(1)}, bf16[2048,128]{1,0:T(8,128)(2,1)S(1)}, bf16[2048,128]{1,0:T(8,128)(2,1)S(1)}) custom-call(bf16[2048,256]{1,0:T(8,128)(2,1)S(1)} %copy-done.1, bf16[2048,256]{1,0:T(8,128)(2,1)S(1)} %get-tuple-element.150.k_ref, bf16[2048,256]{1,0:T(8,128)(2,1)S(1)} %get-tuple-element.149.v_ref, ...), custom_call_target="tpu_custom_call" | custom-call | flops 21474836480 | bytes 5242880 | tf_op jit(solution)/shard_map/attend_backward/pallas_call | solution.py:177
  319.9 5.1 %fusion.6 = bf16[4,4,32,4096]{3,2,1,0:T(8,128)(2,1)S(1)} fusion(bf16[4,4,32,4096]{3,2,1,0:T(8,128)(2,1)} %collective-permute-done.23, bf16[4,4,2,32,4096]{4,3,2,1,0:T(8,128)(2,1)} %bitcast.231, s32[]{:T(128)S(6)} %select_n.334), kind=kLoop, calls=%fused_computation.8 | loop fusion | flops 8388608 | bytes 12582916 | tf_op jit(solution)/shard_map/convert_element_type | solution.py:221
  329.5 23.5 %attend_backward.3 = (bf16[2048,128]{1,0:T(8,128)(2,1)S(1)}, bf16[2048,128]{1,0:T(8,128)(2,1)S(1)}, bf16[2048,128]{1,0:T(8,128)(2,1)S(1)}) custom-call(bf16[2048,256]{1,0:T(8,128)(2,1)S(1)} %copy-done.1, bf16[2048,256]{1,0:T(8,128)(2,1)S(1)} %get-tuple-element.150.k_ref, bf16[2048,256]{1,0:T(8,128)(2,1)S(1)} %get-tuple-element.149.v_ref, ...), custom_call_target="tpu_custom_call" | custom-call | flops 21474836480 | bytes 5242880 | tf_op jit(solution)/shard_map/attend_backward/pallas_call | solution.py:177
  354.5 5.3 %convolution_convert_fusion.2 = bf16[2048,1024]{1,0:T(8,128)(2,1)} fusion(bf16[2048,768]{1,0:T(8,128)(2,1)S(1)} %constant_dynamic-update-slice_fusion.14, bf16[1024,768]{1,0:T(8,128)(2,1)S(1)} %bitcast.248), kind=kOutput, calls=%fused_computation.21 | convolution fusion | flops 3223322624 | bytes 8912896 | tf_op jit(solution)/shard_map/dot_general | solution.py:525
  362.0 6.9 %convolution_convert_fusion.4 = bf16[1024,768]{1,0:T(8,128)(2,1)S(1)} fusion(bf16[2048,1024]{1,0:T(8,128)(2,1)} %constant_dynamic-update-slice_fusion, bf16[2048,768]{1,0:T(8,128)(2,1)} %copy-done.27), kind=kOutput, calls=%fused_computation.66 | convolution fusion | flops 3222011904 | bytes 8912896 | tf_op jit(solution)/shard_map/dot_general | solution.py:434
  376.8 3.3 collective-permute-start.37
  381.8 13.3 %collective-permute-done.24 = bf16[2,256,1024]{2,1,0:T(8,128)(2,1)S(1)} collective-permute-done((bf16[2,256,1024]{2,1,0:T(8,128)(2,1)S(1)}, bf16[2,256,1024]{2,1,0:T(8,128)(2,1)S(1)}, u32[]{:S(2)}, u32[]{:S(2)}) %collective-permute-start.24) | collective-permute-done | bytes 1048608 | tf_op jit(solution)/shard_map/ppermute | solution.py:202
  401.8 8.1 %collective-permute-done.29 = bf16[4,32,2048]{2,1,0:T(8,128)(2,1)S(1)} collective-permute-done((bf16[4,32,2048]{2,1,0:T(8,128)(2,1)S(1)}, bf16[4,32,2048]{2,1,0:T(8,128)(2,1)S(1)}, u32[]{:S(2)}, u32[]{:S(2)}) %collective-permute-start.29) | collective-permute-done | bytes 524320 | tf_op jit(solution)/shard_map/ppermute | solution.py:202
  418.0 7.2 %collective-permute-done.41 = bf16[32,5248]{1,0:T(8,128)(2,1)} collective-permute-done((bf16[32,5248]{1,0:T(8,128)(2,1)}, bf16[32,5248]{1,0:T(8,128)(2,1)}, u32[]{:S(2)}, u32[]{:S(2)}) %collective-permute-start.41) | collective-permute-done | bytes 335904 | tf_op jit(solution)/shard_map/ppermute | solution.py:202
  426.5 11.5 %collective-permute-done.42 = bf16[32,5248]{1,0:T(8,128)(2,1)} collective-permute-done((bf16[32,5248]{1,0:T(8,128)(2,1)}, bf16[32,5248]{1,0:T(8,128)(2,1)}, u32[]{:S(2)}, u32[]{:S(2)}) %collective-permute-start.42) | collective-permute-done | bytes 335904 | tf_op jit(solution)/shard_map/ppermute | solution.py:202
  (371 shorter events, 144.2 us)
Async XLA Ops:
  7.2 127.8 %all-gather.3.cloned.1.call-start = ((), (), s32[]{:S(2)}) async-start(), calls=%async_computation.1 | async-start | bytes 11083776 | tf_op jit(solution)/shard_map/all_gather | solution.py:379
  12.5 183.9 %all-gather.5.cloned.1.call-start = ((), (), s32[]{:S(2)}) async-start(), calls=%async_computation.2 | async-start | bytes 8650752 | tf_op jit(solution)/shard_map/all_gather | solution.py:382
  13.3 448.1 %reduce-scatter.2.cloned.1.call-start = ((), (), s32[]{:S(2)}) async-start(), calls=%async_computation.3 | async-start | bytes 8650752 | tf_op jit(solution)/shard_map/reduce_scatter | solution.py:459
  19.6 33.4 %collective-permute-start = (bf16[256,1024]{1,0:T(8,128)(2,1)}, bf16[256,1024]{1,0:T(8,128)(2,1)}, u32[]{:S(2)}, u32[]{:S(2)}) collective-permute-start(bf16[256,1024]{1,0:T(8,128)(2,1)} %get-tuple-element.167), channel_id=1, source_target_pairs={{0,8},{8,0},{16,24},{24,16},{1,9},{9,1},{17,25},{25,17},{2,10},{10... | collective-permute-start | bytes 1572872 | tf_op jit(solution)/shard_map/ppermute | solution.py:202
  21.5 48.2 %collective-permute-start.2 = (bf16[256,1024]{1,0:T(8,128)(2,1)}, bf16[256,1024]{1,0:T(8,128)(2,1)}, u32[]{:S(2)}, u32[]{:S(2)}) collective-permute-start(bf16[256,1024]{1,0:T(8,128)(2,1)} %get-tuple-element.167), channel_id=1, source_target_pairs={{0,16},{8,24},{16,0},{24,8},{1,17},{9,25},{17,1},{25,9},{2,18},{10... | collective-permute-start | bytes 1572872 | tf_op jit(solution)/shard_map/ppermute | solution.py:202
  23.2 23.8 %collective-permute-start.10 = (bf16[136,768]{1,0:T(8,128)(2,1)S(1)}, bf16[136,768]{1,0:T(8,128)(2,1)S(1)}, u32[]{:S(2)}, u32[]{:S(2)}) collective-permute-start(bf16[136,768]{1,0:T(8,128)(2,1)S(1)} %fusion.51), channel_id=1, source_target_pairs={{0,4},{1,5},{2,6},{3,7},{4,0},{5,1},{6,2},{7,3},{8,12},{9,13},{10,... | collective-permute-start | bytes 626696 | tf_op jit(solution)/shard_map/ppermute | solution.py:202
  25.9 21.7 %collective-permute-start.11 = (bf16[136,768]{1,0:T(8,128)(2,1)S(1)}, bf16[136,768]{1,0:T(8,128)(2,1)S(1)}, u32[]{:S(2)}, u32[]{:S(2)}) collective-permute-start(bf16[136,768]{1,0:T(8,128)(2,1)S(1)} %fusion.51), channel_id=1, source_target_pairs={{0,2},{1,3},{2,0},{3,1},{4,6},{5,7},{6,4},{7,5},{8,10},{9,11},{10,... | collective-permute-start | bytes 626696 | tf_op jit(solution)/shard_map/ppermute | solution.py:202
  27.4 21.1 %collective-permute-start.9 = (bf16[136,768]{1,0:T(8,128)(2,1)S(1)}, bf16[136,768]{1,0:T(8,128)(2,1)S(1)}, u32[]{:S(2)}, u32[]{:S(2)}) collective-permute-start(bf16[136,768]{1,0:T(8,128)(2,1)S(1)} %fusion.51), channel_id=1, source_target_pairs={{0,6},{1,7},{2,4},{3,5},{4,2},{5,3},{6,0},{7,1},{8,14},{9,15},{10,... | collective-permute-start | bytes 626696 | tf_op jit(solution)/shard_map/ppermute | solution.py:202
  47.0 20.8 %collective-permute-start.1 = (bf16[256,1024]{1,0:T(8,128)(2,1)}, bf16[256,1024]{1,0:T(8,128)(2,1)}, u32[]{:S(2)}, u32[]{:S(2)}) collective-permute-start(bf16[256,1024]{1,0:T(8,128)(2,1)} %get-tuple-element.166), channel_id=1, source_target_pairs={{0,8},{8,0},{16,24},{24,16},{1,9},{9,1},{17,25},{25,17},{2,10},{10... | collective-permute-start | bytes 1572872 | tf_op jit(solution)/shard_map/ppermute | solution.py:202
  47.5 15.7 %collective-permute-start.3 = (bf16[256,1024]{1,0:T(8,128)(2,1)}, bf16[256,1024]{1,0:T(8,128)(2,1)}, u32[]{:S(2)}, u32[]{:S(2)}) collective-permute-start(bf16[256,1024]{1,0:T(8,128)(2,1)} %get-tuple-element.166), channel_id=1, source_target_pairs={{0,16},{8,24},{16,0},{24,8},{1,17},{9,25},{17,1},{25,9},{2,18},{10... | collective-permute-start | bytes 1572872 | tf_op jit(solution)/shard_map/ppermute | solution.py:202
  53.0 23.6 %collective-permute-start.12 = (bf16[4,136,768]{2,0,1:T(4,128)(2,1)}, bf16[4,136,768]{2,0,1:T(4,128)(2,1)}, u32[]{:S(2)}, u32[]{:S(2)}) collective-permute-start(bf16[4,136,768]{2,0,1:T(4,128)(2,1)} %pad_maximum_fusion.2), channel_id=1, source_target_pairs={{0,1},{1,0},{2,3},{3,2},{4,5},{5,4},{6,7},{7,6},{8,9},{9,8},{10,11... | collective-permute-start | bytes 2506760 | tf_op jit(solution)/shard_map/ppermute | solution.py:202
  53.1 20.6 %collective-permute-start.4 = (bf16[256,1024]{1,0:T(8,128)(2,1)}, bf16[256,1024]{1,0:T(8,128)(2,1)}, u32[]{:S(2)}, u32[]{:S(2)}) collective-permute-start(bf16[256,1024]{1,0:T(8,128)(2,1)} %collective-permute-done), channel_id=1, source_target_pairs={{0,16},{8,24},{16,0},{24,8},{1,17},{9,25},{17,1},{25,9},{2,18},{10... | collective-permute-start | bytes 1572872 | tf_op jit(solution)/shard_map/ppermute | solution.py:202
  103.5 20.2 %collective-permute-start.13 = (bf16[512,128]{1,0:T(8,128)(2,1)S(1)}, bf16[512,128]{1,0:T(8,128)(2,1)S(1)}, u32[]{:S(2)}, u32[]{:S(2)}) collective-permute-start(bf16[512,128]{1,0:T(8,128)(2,1)S(1)} %get-tuple-element.180), channel_id=1, source_target_pairs={{0,24},{8,16},{16,8},{24,0},{1,25},{9,17},{17,9},{25,1},{2,26},{10... | collective-permute-start | bytes 393224 | tf_op jit(solution)/shard_map/ppermute | solution.py:202
  105.1 20.4 %collective-permute-start.14 = (bf16[512,128]{1,0:T(8,128)(2,1)S(1)}, bf16[512,128]{1,0:T(8,128)(2,1)S(1)}, u32[]{:S(2)}, u32[]{:S(2)}) collective-permute-start(bf16[512,128]{1,0:T(8,128)(2,1)S(1)} %get-tuple-element.179), channel_id=1, source_target_pairs={{0,16},{8,24},{16,0},{24,8},{1,17},{9,25},{17,1},{25,9},{2,18},{10... | collective-permute-start | bytes 393224 | tf_op jit(solution)/shard_map/ppermute | solution.py:202
  105.4 20.1 %collective-permute-start.15 = (bf16[512,128]{1,0:T(8,128)(2,1)S(1)}, bf16[512,128]{1,0:T(8,128)(2,1)S(1)}, u32[]{:S(2)}, u32[]{:S(2)}) collective-permute-start(bf16[512,128]{1,0:T(8,128)(2,1)S(1)} %get-tuple-element.178), channel_id=1, source_target_pairs={{0,8},{8,0},{16,24},{24,16},{1,9},{9,1},{17,25},{25,17},{2,10},{10... | collective-permute-start | bytes 393224 | tf_op jit(solution)/shard_map/ppermute | solution.py:202
  244.2 75.7 %collective-permute-start.23 = (bf16[4,4,32,4096]{3,2,1,0:T(8,128)(2,1)}, bf16[4,4,32,4096]{3,2,1,0:T(8,128)(2,1)}, u32[]{:S(2)}, u32[]{:S(2)}) collective-permute-start(bf16[4,4,32,4096]{3,2,1,0:T(8,128)(2,1)} %dynamic-slice_bitcast_fusion), channel_id=1, source_target_pairs={{0,1},{1,0},{2,3},{3,2},{4,5},{5,4},{6,7},{7,6},{8,9},{9,8},{10,11... | collective-permute-start | bytes 12582920 | tf_op jit(solution)/shard_map/ppermute | solution.py:202
  274.7 18.9 %collective-permute-start.20 = (bf16[512,256]{1,0:T(8,128)(2,1)S(1)}, bf16[512,256]{1,0:T(8,128)(2,1)S(1)}, u32[]{:S(2)}, u32[]{:S(2)}) collective-permute-start(bf16[512,256]{1,0:T(8,128)(2,1)S(1)} %bitcast.253), channel_id=1, source_target_pairs={{0,16},{8,24},{16,0},{24,8},{1,17},{9,25},{17,1},{25,9},{2,18},{10... | collective-permute-start | bytes 786440 | tf_op jit(solution)/shard_map/ppermute | solution.py:202
  275.5 18.2 %collective-permute-start.21 = (bf16[512,256]{1,0:T(8,128)(2,1)S(1)}, bf16[512,256]{1,0:T(8,128)(2,1)S(1)}, u32[]{:S(2)}, u32[]{:S(2)}) collective-permute-start(bf16[512,256]{1,0:T(8,128)(2,1)S(1)} %bitcast.254), channel_id=1, source_target_pairs={{0,24},{8,16},{16,8},{24,0},{1,25},{9,17},{17,9},{25,1},{2,26},{10... | collective-permute-start | bytes 786440 | tf_op jit(solution)/shard_map/ppermute | solution.py:202
  280.0 38.6 %collective-permute-start.22 = (bf16[4,4,32,1152]{3,2,1,0:T(8,128)(2,1)S(1)}, bf16[4,4,32,1152]{3,2,1,0:T(8,128)(2,1)S(1)}, u32[]{:S(2)}, u32[]{:S(2)}) collective-permute-start(bf16[4,4,32,1152]{3,2,1,0:T(8,128)(2,1)S(1)} %dynamic-slice_bitcast_fusion.1), channel_id=1, source_target_pairs={{0,1},{1,0},{2,3},{3,2},{4,5},{5,4},{6,7},{7,6},{8,9},{9,8},{10,11... | collective-permute-start | bytes 3538952 | tf_op jit(solution)/shard_map/ppermute | solution.py:202
  318.9 41.0 %collective-permute-start.32 = (bf16[2,4,32,1152]{3,2,1,0:T(8,128)(2,1)S(1)}, bf16[2,4,32,1152]{3,2,1,0:T(8,128)(2,1)S(1)}, u32[]{:S(2)}, u32[]{:S(2)}) collective-permute-start(bf16[2,4,32,1152]{3,2,1,0:T(8,128)(2,1)S(1)} %dynamic-slice_bitcast_fusion.4), channel_id=1, source_target_pairs={{0,8},{8,0},{16,24},{24,16},{1,9},{9,1},{17,25},{25,17},{2,10},{10... | collective-permute-start | bytes 1769480 | tf_op jit(solution)/shard_map/ppermute | solution.py:202
  326.5 47.4 %collective-permute-start.25 = (bf16[2,4,32,2048]{3,2,1,0:T(8,128)(2,1)}, bf16[2,4,32,2048]{3,2,1,0:T(8,128)(2,1)}, u32[]{:S(2)}, u32[]{:S(2)}) collective-permute-start(bf16[2,4,32,2048]{3,2,1,0:T(8,128)(2,1)} %dynamic-slice_bitcast_fusion.3), channel_id=1, source_target_pairs={{0,8},{8,0},{16,24},{24,16},{1,9},{9,1},{17,25},{25,17},{2,10},{10... | collective-permute-start | bytes 3145736 | tf_op jit(solution)/shard_map/ppermute | solution.py:202
  328.7 48.1 %collective-permute-start.26 = (bf16[2,4,32,2048]{3,2,1,0:T(8,128)(2,1)}, bf16[2,4,32,2048]{3,2,1,0:T(8,128)(2,1)}, u32[]{:S(2)}, u32[]{:S(2)}) collective-permute-start(bf16[2,4,32,2048]{3,2,1,0:T(8,128)(2,1)} %dynamic-slice_bitcast_fusion.2), channel_id=1, source_target_pairs={{0,16},{8,24},{16,0},{24,8},{1,17},{9,25},{17,1},{25,9},{2,18},{10... | collective-permute-start | bytes 3145736 | tf_op jit(solution)/shard_map/ppermute | solution.py:202
  369.4 25.7 %collective-permute-start.24 = (bf16[2,256,1024]{2,1,0:T(8,128)(2,1)S(1)}, bf16[2,256,1024]{2,1,0:T(8,128)(2,1)S(1)}, u32[]{:S(2)}, u32[]{:S(2)}) collective-permute-start(bf16[2,256,1024]{2,1,0:T(8,128)(2,1)S(1)} %slice_bitcast_fusion.2), channel_id=1, source_target_pairs={{0,8},{8,0},{16,24},{24,16},{1,9},{9,1},{17,25},{25,17},{2,10},{10... | collective-permute-start | bytes 3145736 | tf_op jit(solution)/shard_map/ppermute | solution.py:202
  372.1 24.2 %collective-permute-start.30 = (bf16[2,256,1024]{2,1,0:T(8,128)(2,1)S(1)}, bf16[2,256,1024]{2,1,0:T(8,128)(2,1)S(1)}, u32[]{:S(2)}, u32[]{:S(2)}) collective-permute-start(bf16[2,256,1024]{2,1,0:T(8,128)(2,1)S(1)} %slice_bitcast_fusion), channel_id=1, source_target_pairs={{0,16},{8,24},{16,0},{24,8},{1,17},{9,25},{17,1},{25,9},{2,18},{10... | collective-permute-start | bytes 3145736 | tf_op jit(solution)/shard_map/ppermute | solution.py:202
  373.9 25.9 %collective-permute-start.35 = (bf16[4,32,896]{2,1,0:T(8,128)(2,1)S(1)}, bf16[4,32,896]{2,1,0:T(8,128)(2,1)S(1)}, u32[]{:S(2)}, u32[]{:S(2)}) collective-permute-start(bf16[4,32,896]{2,1,0:T(8,128)(2,1)S(1)} %get-tuple-element.168), channel_id=1, source_target_pairs={{0,2},{1,3},{2,0},{3,1},{4,6},{5,7},{6,4},{7,5},{8,10},{9,11},{10,... | collective-permute-start | bytes 688136 | tf_op jit(solution)/shard_map/ppermute | solution.py:202
  374.0 26.5 %collective-permute-start.36 = (bf16[4,32,896]{2,1,0:T(8,128)(2,1)S(1)}, bf16[4,32,896]{2,1,0:T(8,128)(2,1)S(1)}, u32[]{:S(2)}, u32[]{:S(2)}) collective-permute-start(bf16[4,32,896]{2,1,0:T(8,128)(2,1)S(1)} %get-tuple-element.170), channel_id=1, source_target_pairs={{0,4},{1,5},{2,6},{3,7},{4,0},{5,1},{6,2},{7,3},{8,12},{9,13},{10,... | collective-permute-start | bytes 688136 | tf_op jit(solution)/shard_map/ppermute | solution.py:202
  376.8 24.9 %collective-permute-start.37 = (bf16[4,32,896]{2,1,0:T(8,128)(2,1)S(1)}, bf16[4,32,896]{2,1,0:T(8,128)(2,1)S(1)}, u32[]{:S(2)}, u32[]{:S(2)}) collective-permute-start(bf16[4,32,896]{2,1,0:T(8,128)(2,1)S(1)} %get-tuple-element.169), channel_id=1, source_target_pairs={{0,6},{1,7},{2,4},{3,5},{4,2},{5,3},{6,0},{7,1},{8,14},{9,15},{10,... | collective-permute-start | bytes 688136 | tf_op jit(solution)/shard_map/ppermute | solution.py:202
  399.8 49.0 %collective-permute-start.27 = (bf16[256,1024]{1,0:T(8,128)(2,1)}, bf16[256,1024]{1,0:T(8,128)(2,1)}, u32[]{:S(2)}, u32[]{:S(2)}) collective-permute-start(bf16[256,1024]{1,0:T(8,128)(2,1)} %slice_bitcast_fusion.6), channel_id=1, source_target_pairs={{0,16},{8,24},{16,0},{24,8},{1,17},{9,25},{17,1},{25,9},{2,18},{10... | collective-permute-start | bytes 1572872 | tf_op jit(solution)/shard_map/ppermute | solution.py:202
  400.4 48.3 %collective-permute-start.34 = (bf16[256,1024]{1,0:T(8,128)(2,1)}, bf16[256,1024]{1,0:T(8,128)(2,1)}, u32[]{:S(2)}, u32[]{:S(2)}) collective-permute-start(bf16[256,1024]{1,0:T(8,128)(2,1)} %slice_bitcast_fusion.5), channel_id=1, source_target_pairs={{0,8},{8,0},{16,24},{24,16},{1,9},{9,1},{17,25},{25,17},{2,10},{10... | collective-permute-start | bytes 1572872 | tf_op jit(solution)/shard_map/ppermute | solution.py:202
  412.3 25.7 %collective-permute-start.42 = (bf16[32,5248]{1,0:T(8,128)(2,1)}, bf16[32,5248]{1,0:T(8,128)(2,1)}, u32[]{:S(2)}, u32[]{:S(2)}) collective-permute-start(bf16[32,5248]{1,0:T(8,128)(2,1)} %get-tuple-element.157), channel_id=1, source_target_pairs={{0,4},{1,5},{2,6},{3,7},{4,0},{5,1},{6,2},{7,3},{8,12},{9,13},{10,... | collective-permute-start | bytes 1007624 | tf_op jit(solution)/shard_map/ppermute | solution.py:202
  414.3 25.1 %collective-permute-start.43 = (bf16[32,5248]{1,0:T(8,128)(2,1)}, bf16[32,5248]{1,0:T(8,128)(2,1)}, u32[]{:S(2)}, u32[]{:S(2)}) collective-permute-start(bf16[32,5248]{1,0:T(8,128)(2,1)} %get-tuple-element.156), channel_id=1, source_target_pairs={{0,6},{1,7},{2,4},{3,5},{4,2},{5,3},{6,0},{7,1},{8,14},{9,15},{10,... | collective-permute-start | bytes 1007624 | tf_op jit(solution)/shard_map/ppermute | solution.py:202
  425.2 18.0 %collective-permute-start.40 = (bf16[32,896]{1,0:T(8,128)(2,1)}, bf16[32,896]{1,0:T(8,128)(2,1)S(1)}, u32[]{:S(2)}, u32[]{:S(2)}) collective-permute-start(bf16[32,896]{1,0:T(8,128)(2,1)} %get-tuple-element.190), channel_id=1, source_target_pairs={{0,8},{8,0},{16,24},{24,16},{1,9},{9,1},{17,25},{25,17},{2,10},{10... | collective-permute-start | bytes 172040 | tf_op jit(solution)/shard_map/ppermute | solution.py:202
  (68 other events, 397.1 us)
Sparse Core Ops, SparseCore 0:
  12.6 103.2 all-gather.2
  119.4 76.9 all-gather.4
  222.4 151.4 reduce-scatter.1
